TPU v7x, 32 devices: a whole 2x2x4 slice. The times are simulated.
32 devices in a mesh: fsdp: 16 (over z, y, core), tensor: 2 (over x).
Axes of the slice: x: 2, y: 2, z: 4, core: 2. Of those that a mesh axis runs over, the one named last changes fastest.
Arguments:
- tokens: bfloat16 [1152, 32768], P('tensor', 'fsdp'), may hold values from -6 to 6
- condition: bfloat16 [128, 1152], P('fsdp'), may hold values from -6 to 6
- grid_shapes: int32 [128, 2], P('fsdp'), may hold values from 4 to 64, as said below
- cotangent: bfloat16 [1152, 32768], P('tensor', 'fsdp'), may hold values from -6 to 6
- modulation_weight: bfloat16 [1152, 6, 1152], P('fsdp', None, 'tensor'), may hold values from -0.1875 to 0.1875
- modulation_bias: bfloat16 [6, 1152], P(None, 'tensor'), may hold values from -3 to 3
- attend_weight: bfloat16 [1152, 3, 1152], P('fsdp', None, 'tensor'), may hold values from -0.1875 to 0.1875
- attend_bias: bfloat16 [2, 1152], P(None, 'tensor'), may hold values from -3 to 3
- merge_weight: bfloat16 [1152, 1152], P('tensor', 'fsdp'), may hold values from -0.75 to 0.75
- merge_bias: bfloat16 [1152], P('tensor'), may hold values from -3 to 3
- expand_weight: bfloat16 [1152, 4608], P('fsdp', 'tensor'), may hold values from -0.1875 to 0.1875
- expand_bias: bfloat16 [4608], P('tensor'), may hold values from -3 to 3
- reduce_weight: bfloat16 [4608, 1152], P('tensor', 'fsdp'), may hold values from -0.09375 to 0.09375
- reduce_bias: bfloat16 [1152], P('tensor'), may hold values from -3 to 3
Outputs:
- output: float32 [1152, 32768], P('tensor', 'fsdp')
- tokens_grad: float32 [1152, 32768], P('tensor', 'fsdp')
- condition_grad: float32 [128, 1152], P('fsdp', 'tensor')
- modulation_weight_grad: float32 [1152, 6, 1152], P('fsdp', None, 'tensor')
- modulation_bias_grad: float32 [6, 1152], P(None, 'tensor')
- attend_weight_grad: float32 [1152, 3, 1152], P('fsdp', None, 'tensor')
- attend_bias_grad: float32 [2, 1152], P(None, 'tensor')
- merge_weight_grad: float32 [1152, 1152], P('tensor', 'fsdp')
- merge_bias_grad: float32 [1152], P('tensor')
- expand_weight_grad: float32 [1152, 4608], P('fsdp', 'tensor')
- expand_bias_grad: float32 [4608], P('tensor')
- reduce_weight_grad: float32 [4608, 1152], P('tensor', 'fsdp')
- reduce_bias_grad: float32 [1152], P('tensor')
Inputs may be any that keep to these rules, and one draw needn't show every extreme that they name: `grid_shapes`: each row gives an image's patch rows, then patch columns; their product is at most 256, and the first rows times columns slots of the image hold its patches in row-major order.
All inputs are finite; a program needn't handle non-finite values.
Results may differ from a plain program's by a relative error of at most 0.018.
The roundings to bfloat16 on the way count: a program that leaves them out, or rounds other values in their place, can miss the bound.
Values may be sent and summed in bfloat16 or wider, within the bound.
No kernel may reach another device: no remote copies, remote signals or barrier semaphores. Data moves between devices by JAX's collectives and lax.ppermute only.
A program may use at most 320 MiB of HBM per device.

v0:
```python
import math

import jax
import jax.numpy as jnp
from jax import lax
from jax.sharding import PartitionSpec as P

D = 1152
HD = 72
SLOTS = 256
MICRO = 4


EPSILON = 1e-06
NEGATIVE = -1e30


def position_table(grid_shapes, offset, columns):
    slot_line = jnp.arange(SLOTS, dtype=jnp.int32)
    across = grid_shapes[:, 1]
    row_index = slot_line[None, :] // across[:, None]
    col_index = slot_line[None, :] % across[:, None]
    channel = offset + jnp.arange(columns, dtype=jnp.int32)
    quarter = channel // (D // 4)
    within = channel % (D // 4)
    frequency = jnp.exp(within.astype(jnp.float32) * (-math.log(10000.0) / (D // 4)))
    row_angle = row_index.astype(jnp.float32)[:, :, None] * frequency
    col_angle = col_index.astype(jnp.float32)[:, :, None] * frequency
    return jnp.where(
        quarter == 0,
        jnp.sin(row_angle),
        jnp.where(
            quarter == 1,
            jnp.cos(row_angle),
            jnp.where(quarter == 2, jnp.sin(col_angle), jnp.cos(col_angle)),
        ),
    )


def slot_present(grid_shapes):
    slot_line = jnp.arange(SLOTS, dtype=jnp.int32)
    return slot_line[None, :] < (grid_shapes[:, 0] * grid_shapes[:, 1])[:, None]


def gelu_tanh(values):
    return jax.nn.gelu(values, approximate=True)


def normalize(residual):
    sums = lax.psum((jnp.sum(residual, axis=-1), jnp.sum(residual * residual, axis=-1)), "tensor")
    center = sums[0] / D
    spread = sums[1] / D - center * center
    factor = lax.rsqrt(spread + EPSILON)
    return ((residual - center[..., None]) * factor[..., None], factor)


def norm_back(upstream, normed, factor):
    sums = lax.psum((jnp.sum(upstream, axis=-1), jnp.sum(upstream * normed, axis=-1)), "tensor")
    return factor[..., None] * (
        upstream - sums[0][..., None] / D - normed * (sums[1][..., None] / D)
    )


def gather_features(features):
    return lax.all_gather(features, "tensor", axis=1, tiled=True)


def branch_output(unit_values, weight_local):
    return lax.psum_scatter(
        jnp.dot(unit_values, weight_local, preferred_element_type=jnp.float32),
        "tensor",
        scatter_dimension=1,
        tiled=True,
    )


def spread_grads(grad_rows):
    return lax.all_gather(grad_rows, "tensor", axis=1, tiled=True)


def collect_grads(partial_rows):
    return lax.psum_scatter(partial_rows, "tensor", scatter_dimension=1, tiled=True)


def attend_scores(queries, keys_side, present, score_scale):
    raw = (
        jnp.einsum("iqhe,ikhe->ihqk", queries, keys_side, preferred_element_type=jnp.float32)
        * score_scale
    )
    return jnp.where(present[:, None, None, :], raw, NEGATIVE)


def contract_rows(left, right):
    return jnp.einsum("rd,rf->df", left, right, preferred_element_type=jnp.float32)


def times_transpose(left, right):
    return jnp.einsum("rf,df->rd", left, right, preferred_element_type=jnp.float32)


def per_device(
    tokens,
    condition,
    grid_shapes,
    cotangent,
    modulation_weight,
    modulation_bias,
    attend_weight,
    attend_bias,
    merge_weight,
    merge_bias,
    expand_weight,
    expand_bias,
    reduce_weight,
    reduce_bias,
):
    width_local = tokens.shape[0]
    heads_width = attend_weight.shape[2]
    heads_local = heads_width // HD
    hidden_local = expand_weight.shape[1]
    per_micro = condition.shape[0] // MICRO
    rows_micro = per_micro * SLOTS
    offset = lax.axis_index("tensor") * width_local
    score_scale = 1.0 / math.sqrt(HD)
    sharded = (modulation_weight, attend_weight, merge_weight, expand_weight, reduce_weight)
    grad_sums = [
        jnp.zeros((D, 6 * width_local), jnp.float32),
        jnp.zeros((D, 3 * heads_width), jnp.float32),
        jnp.zeros((heads_width, D), jnp.float32),
        jnp.zeros((D, hidden_local), jnp.float32),
        jnp.zeros((hidden_local, D), jnp.float32),
    ]
    bias_sums = [
        jnp.zeros((6, width_local), jnp.float32),
        jnp.zeros((2, heads_width), jnp.float32),
        jnp.zeros((width_local,), jnp.float32),
        jnp.zeros((hidden_local,), jnp.float32),
        jnp.zeros((width_local,), jnp.float32),
    ]
    outputs_list = []
    input_grads = []
    cond_terms = []
    head_shape = (per_micro, SLOTS, heads_local, HD)
    plane = (per_micro, SLOTS, width_local)
    for micro_index in range(MICRO):
        row_range = slice(micro_index * rows_micro, (micro_index + 1) * rows_micro)
        image_range = slice(micro_index * per_micro, (micro_index + 1) * per_micro)
        forward_set = (
            lax.all_gather(sharded[0], "fsdp", axis=0, tiled=True),
            lax.all_gather(sharded[1], "fsdp", axis=0, tiled=True),
            lax.all_gather(sharded[2], "fsdp", axis=1, tiled=True),
            lax.all_gather(sharded[3], "fsdp", axis=0, tiled=True),
            lax.all_gather(sharded[4], "fsdp", axis=1, tiled=True),
        )
        grids_here = grid_shapes[image_range]
        present = slot_present(grids_here)
        residual = tokens[:, row_range].astype(jnp.float32).T.reshape(plane) + position_table(
            grids_here, offset, width_local
        )
        cond_here = condition[image_range].astype(jnp.float32)
        lifted = jax.nn.silu(cond_here).astype(jnp.bfloat16)
        modulation = (
            jnp.dot(
                lifted,
                forward_set[0].reshape(D, 6 * width_local),
                preferred_element_type=jnp.float32,
            ).reshape(per_micro, 6, width_local)
            + modulation_bias
        )
        shift_one = modulation[:, 0, None, :]
        scale_one = modulation[:, 1, None, :]
        gate_one = modulation[:, 2, None, :]
        shift_two = modulation[:, 3, None, :]
        scale_two = modulation[:, 4, None, :]
        gate_two = modulation[:, 5, None, :]
        normed_one, factor_one = normalize(residual)
        features_one = (
            (normed_one * (1.0 + scale_one) + shift_one)
            .astype(jnp.bfloat16)
            .reshape(rows_micro, width_local)
        )
        full_one = gather_features(features_one)
        projected = jnp.dot(
            full_one, forward_set[1].reshape(D, 3 * heads_width), preferred_element_type=jnp.float32
        ).reshape(rows_micro, 3, heads_width)
        queries = (projected[:, 0] + attend_bias[0]).astype(jnp.bfloat16).reshape(head_shape)
        keys_side = projected[:, 1].astype(jnp.bfloat16).reshape(head_shape)
        values_side = (projected[:, 2] + attend_bias[1]).astype(jnp.bfloat16).reshape(head_shape)
        scores = attend_scores(queries, keys_side, present, score_scale)
        highest = jnp.max(scores, axis=-1, keepdims=True)
        log_total = highest + jnp.log(jnp.sum(jnp.exp(scores - highest), axis=-1, keepdims=True))
        attention = jnp.exp(scores - log_total)
        mixture = (
            jnp.einsum(
                "ihqk,ikhe->iqhe",
                attention.astype(jnp.bfloat16),
                values_side,
                preferred_element_type=jnp.float32,
            )
            .astype(jnp.bfloat16)
            .reshape(rows_micro, heads_width)
        )
        attended = (branch_output(mixture, forward_set[2]) + merge_bias).reshape(plane)
        middle = residual + gate_one * attended
        normed_two, factor_two = normalize(middle)
        features_two = (
            (normed_two * (1.0 + scale_two) + shift_two)
            .astype(jnp.bfloat16)
            .reshape(rows_micro, width_local)
        )
        full_two = gather_features(features_two)
        expanded = (
            jnp.dot(full_two, forward_set[3], preferred_element_type=jnp.float32) + expand_bias
        )
        activated = gelu_tanh(expanded).astype(jnp.bfloat16)
        reduced = (branch_output(activated, forward_set[4]) + reduce_bias).reshape(plane)
        outputs_list.append((middle + gate_two * reduced).reshape(rows_micro, width_local))
        backward_set = (
            lax.all_gather(sharded[0], "fsdp", axis=0, tiled=True),
            lax.all_gather(sharded[1], "fsdp", axis=0, tiled=True),
            lax.all_gather(sharded[2], "fsdp", axis=1, tiled=True),
            lax.all_gather(sharded[3], "fsdp", axis=0, tiled=True),
            lax.all_gather(sharded[4], "fsdp", axis=1, tiled=True),
        )
        upstream = cotangent[:, row_range].astype(jnp.float32).T.reshape(plane)
        gate_two_grad = jnp.sum(upstream * reduced, axis=1)
        reduced_grad = (upstream * gate_two).astype(jnp.bfloat16).reshape(rows_micro, width_local)
        bias_sums[4] = bias_sums[4] + jnp.sum(reduced_grad.astype(jnp.float32), axis=0)
        reduced_full = spread_grads(reduced_grad)
        grad_sums[4] = grad_sums[4] + contract_rows(activated, reduced_full)
        activated_grad = times_transpose(reduced_full, backward_set[4])
        expanded_grad = jax.vjp(gelu_tanh, expanded)[1](activated_grad)[0].astype(jnp.bfloat16)
        bias_sums[3] = bias_sums[3] + jnp.sum(expanded_grad.astype(jnp.float32), axis=0)
        grad_sums[3] = grad_sums[3] + contract_rows(full_two, expanded_grad)
        features_two_grad = collect_grads(times_transpose(expanded_grad, backward_set[3])).reshape(
            plane
        )
        shift_two_grad = jnp.sum(features_two_grad, axis=1)
        scale_two_grad = jnp.sum(features_two_grad * normed_two, axis=1)
        middle_grad = upstream + norm_back(
            features_two_grad * (1.0 + scale_two), normed_two, factor_two
        )
        gate_one_grad = jnp.sum(middle_grad * attended, axis=1)
        attended_grad = (
            (middle_grad * gate_one).astype(jnp.bfloat16).reshape(rows_micro, width_local)
        )
        bias_sums[2] = bias_sums[2] + jnp.sum(attended_grad.astype(jnp.float32), axis=0)
        attended_full = spread_grads(attended_grad)
        grad_sums[2] = grad_sums[2] + contract_rows(mixture, attended_full)
        mixture_grad = (
            times_transpose(attended_full, backward_set[2]).astype(jnp.bfloat16).reshape(head_shape)
        )
        scores = attend_scores(queries, keys_side, present, score_scale)
        attention = jnp.exp(scores - log_total)
        attention_grad = jnp.einsum(
            "iqhe,ikhe->ihqk", mixture_grad, values_side, preferred_element_type=jnp.float32
        )
        inner_total = jnp.sum(attention * attention_grad, axis=-1, keepdims=True)
        score_grad = (attention * (attention_grad - inner_total)).astype(jnp.bfloat16)
        queries_grad = (
            jnp.einsum("ihqk,ikhe->iqhe", score_grad, keys_side, preferred_element_type=jnp.float32)
            * score_scale
        ).astype(jnp.bfloat16)
        keys_grad = (
            jnp.einsum("ihqk,iqhe->ikhe", score_grad, queries, preferred_element_type=jnp.float32)
            * score_scale
        ).astype(jnp.bfloat16)
        values_grad = jnp.einsum(
            "ihqk,iqhe->ikhe",
            attention.astype(jnp.bfloat16),
            mixture_grad,
            preferred_element_type=jnp.float32,
        ).astype(jnp.bfloat16)
        stacked = jnp.stack(
            [
                queries_grad.reshape(rows_micro, heads_width),
                keys_grad.reshape(rows_micro, heads_width),
                values_grad.reshape(rows_micro, heads_width),
            ],
            axis=1,
        ).reshape(rows_micro, 3 * heads_width)
        bias_sums[1] = bias_sums[1] + jnp.stack(
            [
                jnp.sum(queries_grad.astype(jnp.float32).reshape(rows_micro, heads_width), axis=0),
                jnp.sum(values_grad.astype(jnp.float32).reshape(rows_micro, heads_width), axis=0),
            ],
            axis=0,
        )
        grad_sums[1] = grad_sums[1] + contract_rows(full_one, stacked)
        features_one_grad = collect_grads(
            times_transpose(stacked, backward_set[1].reshape(D, 3 * heads_width))
        ).reshape(plane)
        shift_one_grad = jnp.sum(features_one_grad, axis=1)
        scale_one_grad = jnp.sum(features_one_grad * normed_one, axis=1)
        residual_grad = middle_grad + norm_back(
            features_one_grad * (1.0 + scale_one), normed_one, factor_one
        )
        input_grads.append(residual_grad.reshape(rows_micro, width_local))
        modulation_grad = jnp.stack(
            [
                shift_one_grad,
                scale_one_grad,
                gate_one_grad,
                shift_two_grad,
                scale_two_grad,
                gate_two_grad,
            ],
            axis=1,
        ).astype(jnp.bfloat16)
        bias_sums[0] = bias_sums[0] + jnp.sum(modulation_grad.astype(jnp.float32), axis=0)
        flat_grad = modulation_grad.reshape(per_micro, 6 * width_local)
        grad_sums[0] = grad_sums[0] + contract_rows(lifted, flat_grad)
        lifted_grad = times_transpose(flat_grad, backward_set[0].reshape(D, 6 * width_local))
        cond_terms.append(jax.vjp(jax.nn.silu, cond_here)[1](lifted_grad)[0])
    weight_totals = (
        lax.psum_scatter(
            grad_sums[0].reshape(D, 6, width_local).astype(jnp.bfloat16),
            "fsdp",
            scatter_dimension=0,
            tiled=True,
        ).astype(jnp.float32),
        lax.psum_scatter(
            grad_sums[1].reshape(D, 3, heads_width).astype(jnp.bfloat16),
            "fsdp",
            scatter_dimension=0,
            tiled=True,
        ).astype(jnp.float32),
        lax.psum_scatter(
            grad_sums[2].astype(jnp.bfloat16), "fsdp", scatter_dimension=1, tiled=True
        ).astype(jnp.float32),
        lax.psum_scatter(
            grad_sums[3].astype(jnp.bfloat16), "fsdp", scatter_dimension=0, tiled=True
        ).astype(jnp.float32),
        lax.psum_scatter(
            grad_sums[4].astype(jnp.bfloat16), "fsdp", scatter_dimension=1, tiled=True
        ).astype(jnp.float32),
    )
    bias_totals = lax.psum(
        (bias_sums[0], bias_sums[1], bias_sums[2], bias_sums[3], bias_sums[4]), "fsdp"
    )
    cond_total = lax.psum_scatter(
        jnp.concatenate(cond_terms, axis=0).astype(jnp.bfloat16),
        "tensor",
        scatter_dimension=1,
        tiled=True,
    ).astype(jnp.float32)
    return (
        jnp.concatenate(outputs_list, axis=0).T,
        jnp.concatenate(input_grads, axis=0).T,
        cond_total,
        weight_totals[0],
        bias_totals[0],
        weight_totals[1],
        bias_totals[1],
        weight_totals[2],
        bias_totals[2],
        weight_totals[3],
        bias_totals[3],
        weight_totals[4],
        bias_totals[4],
    )


def solution(mesh):
    return jax.shard_map(
        per_device,
        mesh=mesh,
        in_specs=(
            P("tensor", "fsdp"),
            P("fsdp", None),
            P("fsdp", None),
            P("tensor", "fsdp"),
            P("fsdp", None, "tensor"),
            P(None, "tensor"),
            P("fsdp", None, "tensor"),
            P(None, "tensor"),
            P("tensor", "fsdp"),
            P("tensor"),
            P("fsdp", "tensor"),
            P("tensor"),
            P("tensor", "fsdp"),
            P("tensor"),
        ),
        out_specs=(
            P("tensor", "fsdp"),
            P("tensor", "fsdp"),
            P("fsdp", "tensor"),
            P("fsdp", None, "tensor"),
            P(None, "tensor"),
            P("fsdp", None, "tensor"),
            P(None, "tensor"),
            P("tensor", "fsdp"),
            P("tensor"),
            P("fsdp", "tensor"),
            P("tensor"),
            P("tensor", "fsdp"),
            P("tensor"),
        ),
        check_vma=False,
    )
```

profile of v0, /device:TPU:0, one launch (start us, length us, event | category | flops | bytes accessed | tf_op | source)
XLA Modules:
  0.0 1845.9 jit_solution(3879984450310421376)
XLA Ops:
  15.7 36.7 %fusion.309 = (f32[512]{0:T(512)S(1)}, f32[512]{0:T(512)S(1)}, f32[512]{0:T(512)S(1)}, f32[512]{0:T(512)S(1)}, f32[512]{0:T(512)S(1)}, /*index=5*/f32[512]{0:T(512)S(1)}, f32[512]{0:T(512)S(1)}, f32[512]{0:T(512)S(1)}) fusion(f32[512]{0:T(512)S(1)} %bitcast.961, pred[576]{0:T(1024)(128)(4,1)S(1)} %get-tuple-element.389, ...), kind=kLoop, calls=%fused_computation.675 | loop fusion | flops 11792384 | bytes 2396096 | tf_op jit(solution)/shard_map/reduce_sum | solution.py:50
  66.2 23.9 %all-gather.22.cloned.1.call-done = bf16[1152,6,576]{2,0,1:T(8,128)(2,1)} async-done(((bf16[72,6,576]{2,0,1:T(8,128)(2,1)}), bf16[1152,6,576]{2,0,1:T(8,128)(2,1)}) %all-gather.22.cloned.1.call-update) | async-done | bytes 7962640 | tf_op jit(solution)/shard_map/all_gather | solution.py:149
  123.8 19.9 %add_convert_fusion.3 = (bf16[512,576]{0,1:T(8,128)(2,1)}, bf16[512,576]{0,1:T(8,128)(2,1)}) fusion(f32[512,576]{0,1:T(8,128)S(1)} %bitcast.878, f32[512,576]{0,1:T(8,128)S(1)} %bitcast.829, f32[512]{0:T(512)S(1)} %bitcast.972, f32[512]{0:T(512)S(1)} %bitcast.975, f32[512]{0:T(512)S(1)} %bitcast.934, pred[576]{0:T(1024)(128)(4,1)S(1)} %get-tuple-element.389, ...), kind=kLoop, calls=%fused_computation.335 | loop fusion | flops 7077888 | bytes 7098304 | tf_op jit(solution)/shard_map/convert_element_type | solution.py:179
  176.1 19.0 %add_convert_fusion.5 = (bf16[512,576]{0,1:T(8,128)(2,1)}, bf16[512,576]{0,1:T(8,128)(2,1)}) fusion(f32[512,576]{0,1:T(8,128)S(1)} %bitcast.877, f32[512,576]{0,1:T(8,128)S(1)} %bitcast.833, f32[512]{0:T(512)S(1)} %bitcast.990, f32[512]{0:T(512)S(1)} %bitcast.993, f32[512]{0:T(512)S(1)} %bitcast.954, pred[576]{0:T(1024)(128)(4,1)S(1)} %get-tuple-element.389, ...), kind=kLoop, calls=%fused_computation.343 | loop fusion | flops 7077888 | bytes 7098304 | tf_op jit(solution)/shard_map/convert_element_type | solution.py:179
  317.1 37.0 %reduce-scatter.29.cloned.1.call-done = f32[512,576]{0,1:T(8,128)} async-done(((f32[512,1152]{0,1:T(8,128)}), f32[512,576]{0,1:T(8,128)}) %reduce-scatter.29.cloned.1.call-update) | async-done | bytes 1179664 | tf_op jit(solution)/shard_map/reduce_scatter | solution.py:69
  354.1 21.4 %fusion.319 = (f32[512]{0:T(512)}, f32[512]{0:T(512)}, f32[512,576]{0,1:T(8,128)}, f32[512,576]{0,1:T(8,128)}, f32[512]{0:T(512)}, /*index=5*/f32[512]{0:T(512)}, f32[512,576]{0,1:T(8,128)S(1)}, f32[512,576]{0,1:T(8,128)}) fusion(f32[512,576]{0,1:T(8,128)} %bitcast.841, f32[512]{0:T(512)} %bitcast.932, pred[576]{0:T(1024)(128)(4,1)S(1)} %get-tuple-element.389, ...), kind=kLoop, calls=%fused_computation.685 | loop fusion | flops 7665664 | bytes 10639552 | tf_op jit(solution)/shard_map/reduce_sum | solution.py:50
  391.0 37.6 %reduce-scatter.41.cloned.1.call-done = f32[512,576]{0,1:T(8,128)} async-done(((f32[512,1152]{0,1:T(8,128)}), f32[512,576]{0,1:T(8,128)}) %reduce-scatter.41.cloned.1.call-update) | async-done | bytes 1179664 | tf_op jit(solution)/shard_map/reduce_scatter | solution.py:69
  428.6 21.5 %fusion.318 = (f32[512]{0:T(512)}, f32[512]{0:T(512)}, f32[512,576]{0,1:T(8,128)}, f32[512,576]{0,1:T(8,128)}, f32[512]{0:T(512)}, /*index=5*/f32[512]{0:T(512)}, f32[512,576]{0,1:T(8,128)}, f32[512,576]{0,1:T(8,128)}) fusion(f32[512,576]{0,1:T(8,128)} %bitcast.839, f32[512]{0:T(512)} %bitcast.952, pred[576]{0:T(1024)(128)(4,1)S(1)} %get-tuple-element.389, ...), kind=kLoop, calls=%fused_computation.684 | loop fusion | flops 7665664 | bytes 10639552 | tf_op jit(solution)/shard_map/reduce_sum | solution.py:50
  489.2 21.3 %all-gather.42.cloned.1.call-done = bf16[512,1152]{0,1:T(8,128)(2,1)} async-done(((bf16[512,576]{0,1:T(8,128)(2,1)}), bf16[512,1152]{0,1:T(8,128)(2,1)}) %all-gather.42.cloned.1.call-update) | async-done | bytes 1179664 | tf_op jit(solution)/shard_map/all_gather | solution.py:65
  518.8 50.1 %all-gather.34.cloned.1.call-done = bf16[2304,1152]{0,1:T(8,128)(2,1)} async-done(((bf16[2304,72]{0,1:T(8,128)(2,1)}), bf16[2304,1152]{0,1:T(8,128)(2,1)}) %all-gather.34.cloned.1.call-update) | async-done | bytes 5308432 | tf_op jit(solution)/shard_map/all_gather | solution.py:153
  577.6 14.7 all-gather.38.cloned.1.call-done
  677.5 37.0 %reduce-scatter.35.cloned.1.call-done = f32[512,576]{0,1:T(8,128)} async-done(((f32[512,1152]{0,1:T(8,128)}), f32[512,576]{0,1:T(8,128)}) %reduce-scatter.35.cloned.1.call-update) | async-done | bytes 1179664 | tf_op jit(solution)/shard_map/reduce_scatter | solution.py:69
  714.6 36.9 %reduce-scatter.31.cloned.1.call-done = f32[512,576]{0,1:T(8,128)} async-done(((f32[512,1152]{0,1:T(8,128)}), f32[512,576]{0,1:T(8,128)}) %reduce-scatter.31.cloned.1.call-update) | async-done | bytes 1179664 | tf_op jit(solution)/shard_map/reduce_scatter | solution.py:69
  751.5 37.1 %reduce-scatter.43.cloned.1.call-done = f32[512,576]{0,1:T(8,128)} async-done(((f32[512,1152]{0,1:T(8,128)}), f32[512,576]{0,1:T(8,128)}) %reduce-scatter.43.cloned.1.call-update) | async-done | bytes 1179664 | tf_op jit(solution)/shard_map/reduce_scatter | solution.py:69
  800.3 20.6 %all-gather.48.cloned.1.call-done = bf16[512,1152]{0,1:T(8,128)(2,1)} async-done(((bf16[512,576]{0,1:T(8,128)(2,1)}), bf16[512,1152]{0,1:T(8,128)(2,1)}) %all-gather.48.cloned.1.call-update) | async-done | bytes 1179664 | tf_op jit(solution)/shard_map/all_gather | solution.py:78
  912.8 18.5 %reduce-scatter.45.cloned.1.call-done = f32[512,576]{0,1:T(8,128)} async-done(((f32[512,1152]{0,1:T(8,128)}), f32[512,576]{0,1:T(8,128)}) %reduce-scatter.45.cloned.1.call-update) | async-done | bytes 1179664 | tf_op jit(solution)/shard_map/reduce_scatter | solution.py:82
  937.4 30.8 %reduce-scatter.49.cloned.1.call-done = f32[512,576]{0,1:T(8,128)} async-done(((f32[512,1152]{0,1:T(8,128)}), f32[512,576]{0,1:T(8,128)}) %reduce-scatter.49.cloned.1.call-update) | async-done | bytes 1179664 | tf_op jit(solution)/shard_map/reduce_scatter | solution.py:82
  974.3 30.9 %reduce-scatter.53.cloned.1.call-done = f32[512,576]{0,1:T(8,128)} async-done(((f32[512,1152]{0,1:T(8,128)}), f32[512,576]{0,1:T(8,128)}) %reduce-scatter.53.cloned.1.call-update) | async-done | bytes 1179664 | tf_op jit(solution)/shard_map/reduce_scatter | solution.py:82
  1011.3 31.0 %reduce-scatter.57.cloned.1.call-done = f32[512,576]{0,1:T(8,128)} async-done(((f32[512,1152]{0,1:T(8,128)}), f32[512,576]{0,1:T(8,128)}) %reduce-scatter.57.cloned.1.call-update) | async-done | bytes 1179664 | tf_op jit(solution)/shard_map/reduce_scatter | solution.py:82
  1257.9 139.3 %fusion.82 = (f32[2,256,576]{1,0,2:T(2,128)S(1)}, f32[2,256,576]{1,0,2:T(2,128)S(1)}, f32[2,256,576]{1,0,2:T(2,128)S(1)}, f32[2,256,576]{1,0,2:T(2,128)}) fusion(f32[2,256,576]{1,0,2:T(2,128)} %reshape.836, pred[576]{0:T(1024)(128)(4,1)S(1)} %copy-done.152, pred[576]{0:T(1024)(128)(4,1)S(1)} %copy-done.158, pred[576]{0:T(1024)(128)(4,1)S(1)} %copy-done.155, ...), kind=kLoop, calls=%fused_computation.199 | loop fusion | flops 7077888 | bytes 9457600 | tf_op jit(solution)/shard_map/add | solution.py:157
  1611.2 15.1 copy.293
  1651.3 21.3 %multiply_reduce_fusion.22 = (f32[512]{0:T(512)}, f32[512]{0:T(512)}, f32[512]{0:T(512)}, f32[512]{0:T(512)}, f32[512,576]{0,1:T(8,128)}, /*index=5*/f32[512,576]{0,1:T(8,128)}) fusion(f32[512]{0:T(512)} %bitcast.971, f32[512]{0:T(512)} %bitcast.974, f32[512]{0:T(512)} %bitcast.933, pred[576]{0:T(1024)(128)(4,1)S(1)} %copy-done.152, ...), kind=kLoop, calls=%fused_computation.305 | loop fusion | flops 7665664 | bytes 8286144 | tf_op jit(solution)/shard_map/reduce_sum | solution.py:58
  1677.6 21.2 %multiply_reduce_fusion.26 = (f32[512]{0:T(512)}, f32[512]{0:T(512)}, f32[512]{0:T(512)}, f32[512]{0:T(512)}, f32[512,576]{0,1:T(8,128)}, /*index=5*/f32[512,576]{0,1:T(8,128)}) fusion(f32[512]{0:T(512)} %bitcast.983, f32[512]{0:T(512)} %bitcast.986, f32[512]{0:T(512)} %bitcast.938, pred[576]{0:T(1024)(128)(4,1)S(1)} %copy-done.152, ...), kind=kLoop, calls=%fused_computation.317 | loop fusion | flops 7665664 | bytes 8286144 | tf_op jit(solution)/shard_map/reduce_sum | solution.py:58
  1725.8 63.5 %all-reduce.1 = (f32[6,576]{1,0:T(8,128)}, f32[2,576]{1,0:T(2,128)}, f32[576]{0:T(1024)}, f32[2304]{0:T(1024)}, f32[576]{0:T(1024)}) all-reduce(f32[6,576]{1,0:T(8,128)} %add_add_fusion, f32[2,576]{1,0:T(2,128)} %fusion.222, f32[576]{0:T(1024)} %add_add_fusion.3, ...), channel_id=1, replica_groups=mesh['fsdp'=16,'tensor'=2] {'fsdp'}, use_global_device_ids=true, to_apply=%region_122.125 | all-reduce | flops 8064 | bytes 64512 | tf_op jit(solution)/shard_map/psum | solution.py:338
  (1233 shorter events, 1020.2 us)
Async XLA Ops:
  7.9 188.8 %all-gather.26.cloned.1.call-start = ((), (), s32[]{:S(2)}) async-start(), calls=%async_computation.24 | async-start | bytes 4700160 | tf_op jit(solution)/shard_map/all_gather | solution.py:150
  8.7 194.8 %all-gather.40.cloned.1.call-start = ((), (), s32[]{:S(2)}) async-start(), calls=%async_computation.35 | async-start | bytes 1769472 | tf_op jit(solution)/shard_map/all_gather | solution.py:65
  277.9 150.7 %reduce-scatter.41.cloned.1.call-start = ((), (), s32[]{:S(2)}) async-start(), calls=%async_computation.40 | async-start | bytes 3538944 | tf_op jit(solution)/shard_map/reduce_scatter | solution.py:69
  302.9 186.4 %all-gather.32.cloned.1.call-start = ((), (), s32[]{:S(2)}) async-start(), calls=%async_computation.28 | async-start | bytes 5640192 | tf_op jit(solution)/shard_map/all_gather | solution.py:152
  303.5 207.1 %all-gather.42.cloned.1.call-start = ((), (), s32[]{:S(2)}) async-start(), calls=%async_computation.37 | async-start | bytes 1769472 | tf_op jit(solution)/shard_map/all_gather | solution.py:65
  473.5 143.0 %all-gather.30.cloned.1.call-start = ((), (), s32[]{:S(2)}) async-start(), calls=%async_computation.27 | async-start | bytes 1769472 | tf_op jit(solution)/shard_map/all_gather | solution.py:65
  480.4 160.2 %all-gather.46.cloned.1.call-start = ((), (), s32[]{:S(2)}) async-start(), calls=%async_computation.41 | async-start | bytes 1769472 | tf_op jit(solution)/shard_map/all_gather | solution.py:65
  489.2 188.3 %reduce-scatter.39.cloned.1.call-start = ((), (), s32[]{:S(2)}) async-start(), calls=%async_computation.38 | async-start | bytes 3538944 | tf_op jit(solution)/shard_map/reduce_scatter | solution.py:69
  607.9 143.6 %reduce-scatter.31.cloned.1.call-start = ((), (), s32[]{:S(2)}) async-start(), calls=%async_computation.30 | async-start | bytes 3538944 | tf_op jit(solution)/shard_map/reduce_scatter | solution.py:69
  632.0 156.5 %reduce-scatter.43.cloned.1.call-start = ((), (), s32[]{:S(2)}) async-start(), calls=%async_computation.42 | async-start | bytes 3538944 | tf_op jit(solution)/shard_map/reduce_scatter | solution.py:69
  656.2 164.8 %all-gather.48.cloned.1.call-start = ((), (), s32[]{:S(2)}) async-start(), calls=%async_computation.43 | async-start | bytes 1769472 | tf_op jit(solution)/shard_map/all_gather | solution.py:78
  863.5 141.7 %reduce-scatter.53.cloned.1.call-start = ((), (), s32[]{:S(2)}) async-start(), calls=%async_computation.52 | async-start | bytes 3538944 | tf_op jit(solution)/shard_map/reduce_scatter | solution.py:82
  887.7 154.6 %reduce-scatter.57.cloned.1.call-start = ((), (), s32[]{:S(2)}) async-start(), calls=%async_computation.56 | async-start | bytes 3538944 | tf_op jit(solution)/shard_map/reduce_scatter | solution.py:82
  912.7 179.5 %all-gather.62.cloned.1.call-start = ((), (), s32[]{:S(2)}) async-start(), calls=%async_computation.57 | async-start | bytes 1769472 | tf_op jit(solution)/shard_map/all_gather | solution.py:78
  1079.8 391.1 %reduce-scatter.59.cloned.1.call-start = ((), (), s32[]{:S(2)}) async-start(), calls=%async_computation.58 | async-start | bytes 3538944 | tf_op jit(solution)/shard_map/reduce_scatter | solution.py:82
  1116.0 369.8 %reduce-scatter.55.cloned.1.call-start = ((), (), s32[]{:S(2)}) async-start(), calls=%async_computation.54 | async-start | bytes 3538944 | tf_op jit(solution)/shard_map/reduce_scatter | solution.py:82
  1145.9 354.7 %reduce-scatter.51.cloned.1.call-start = ((), (), s32[]{:S(2)}) async-start(), calls=%async_computation.50 | async-start | bytes 3538944 | tf_op jit(solution)/shard_map/reduce_scatter | solution.py:82
  1176.0 339.3 %reduce-scatter.47.cloned.1.call-start = ((), (), s32[]{:S(2)}) async-start(), calls=%async_computation.46 | async-start | bytes 3538944 | tf_op jit(solution)/shard_map/reduce_scatter | solution.py:82
  1205.9 440.1 %reduce-scatter.71.cloned.1.call-start = ((), (), s32[]{:S(2)}) async-start(), calls=%async_computation.64 | async-start | bytes 1566720
  1220.9 426.6 %reduce-scatter.63.cloned.1.call-start = ((), (), s32[]{:S(2)}) async-start(), calls=%async_computation.60 | async-start | bytes 5640192 | tf_op jit(solution)/shard_map/reduce_scatter | solution.py:331
  1235.4 414.0 %reduce-scatter.65.cloned.1.call-start = ((), (), s32[]{:S(2)}) async-start(), calls=%async_computation.61 | async-start | bytes 5640192 | tf_op jit(solution)/shard_map/reduce_scatter | solution.py:334
  1446.1 387.0 %reduce-scatter.67.cloned.1.call-start = ((), (), s32[]{:S(2)}) async-start(), calls=%async_computation.62 | async-start | bytes 442368
  1559.3 275.4 %reduce-scatter.69.cloned.1.call-start = ((), (), s32[]{:S(2)}) async-start(), calls=%async_computation.63 | async-start | bytes 4386816
  1573.6 263.1 %reduce-scatter.61.cloned.1.call-start = ((), (), s32[]{:S(2)}) async-start(), calls=%async_computation.59 | async-start | bytes 12533760 | tf_op jit(solution)/shard_map/reduce_scatter | solution.py:316
  (331 other events, 6303.2 us)
Sparse Core Ops, SparseCore 0:
  10.2 79.8 all-gather.21
  92.3 50.3 all-gather.25
  168.1 39.2 all-gather.27
  282.2 34.7 reduce-scatter.36
  319.3 34.7 reduce-scatter.28
  356.2 34.7 reduce-scatter.32
  393.8 34.7 reduce-scatter.40
  430.6 56.3 all-gather.31
  512.5 56.3 all-gather.33
  642.7 34.7 reduce-scatter.38
  679.7 34.7 reduce-scatter.34
  753.7 34.7 reduce-scatter.42
  896.5 34.7 reduce-scatter.44
  933.4 34.7 reduce-scatter.48
  970.4 34.7 reduce-scatter.52
  1007.5 34.7 reduce-scatter.56
  1167.4 34.7 reduce-scatter.58
  1204.4 34.7 reduce-scatter.54
  1278.2 34.7 reduce-scatter.46
  1316.8 57.8 reduce-scatter.70
  1378.6 77.0 reduce-scatter.62
  1459.7 77.0 reduce-scatter.64
  1575.9 70.7 reduce-scatter.68
  1650.6 128.4 reduce-scatter.60
  (19 shorter events, 440.5 us)
where the time goes:
time: 1860 us; the launch traced here: 1850 us
  waiting for transfers between devices  510 us (27%)
  other arithmetic  497 us (27%)
  matrix products  379 us (20%)
  local copies, waits for them, and re-layouts  336 us (18%)
  blocking collectives  98.9 us (5%)
  between operations  19.3 us (1%)
    reduce_scatter x8, waiting for transfers between devices, branch_output(): lax.psum_scatter(jnp.dot(unit_values, weight_local, preferred_element_typ...  211 us
    add x1, other arithmetic, per_device(): tokens[:, row_range].astype(jnp.float32).T.reshape(plane)  139 us
    dot_general x20, matrix products, times_transpose(): jnp.einsum('rf,df->rd', left, right, preferred_element_type=jnp.float32)  117 us
    reduce_scatter x8, waiting for transfers between devices, collect_grads(): lax.psum_scatter(partial_rows, 'tensor', scatter_dimension=1, tiled=True)  111 us
    dot_general x20, matrix products, contract_rows(): jnp.einsum('rd,rf->df', left, right, preferred_element_type=jnp.float32)  98 us
    unnamed x725, local copies, waits for them, and re-layouts  87 us
    reduce_sum x3, other arithmetic, normalize(): jnp.sum(residual, axis=-1)  79.6 us
    psum x1, blocking collectives, per_device(): lax.psum((bias_sums[0], bias_sums[1], bias_sums[2], bias_sums[3], bias_su...  63.5 us
  transfers between devices with their start and end apart: 43, of which 26 were waited for; matrix products, arithmetic and copies ran while one was open for 61% of the time, Pallas kernels for 0%

commit v1 on v0

v1 whole, which is shorter than its diff:
```python
import functools
import math

import jax
import jax.numpy as jnp
from jax import lax
from jax.experimental import pallas as pl
from jax.experimental.pallas import tpu as pltpu
from jax.sharding import PartitionSpec as P

D = 1152
HD = 72
SLOTS = 256
EPSILON = 1e-06
NEGATIVE = -1e30
SPOTS = 64
SCALE = 1.0 / math.sqrt(HD)
F32 = jnp.float32
BF16 = jnp.bfloat16


def times(left, right, dim_left, dim_right):
    return lax.dot_general(
        left, right, (((dim_left,), (dim_right,)), ((), ())), preferred_element_type=F32
    )


def gelu_tanh(values):
    return jax.nn.gelu(values, approximate=True)


ARB = pltpu.CompilerParams(dimension_semantics=("arbitrary",))


def smem():
    return pl.BlockSpec(memory_space=pltpu.SMEM)


def image_rows(count, width):
    return pl.BlockSpec((count, width, SLOTS), lambda i: (0, 0, i))


def column_spec(width):
    return pl.BlockSpec((1, D, width), lambda i: (i, 0, 0))


def rows_of(ref, i, blk):
    return slice(i * blk, (i + 1) * blk)


def cost(flops, moved, trans=0):
    return pl.CostEstimate(flops=flops, bytes_accessed=moved, transcendentals=trans)


def pre_kernel(idx, tokens, table, spots, mod, res, feat, stats):
    count, blk, _ = tokens.shape
    line = lax.broadcasted_iota(jnp.int32, (6 * SPOTS, SLOTS), 0)
    target = jnp.where(line < 3 * SPOTS, spots[0, 0:1, :], spots[0, 1:2, :])
    onehot = jnp.where((line & (SPOTS - 1)) == target, 1.0, 0.0).astype(BF16)
    total = jnp.zeros((1, SLOTS), F32)
    square = jnp.zeros((1, SLOTS), F32)
    for i in range(count):
        value = tokens[idx[i]].astype(F32) + times(table[i], onehot, 1, 0)
        res[i] = value
        total = total + jnp.sum(value, axis=0, keepdims=True)
        square = square + jnp.sum(value * value, axis=0, keepdims=True)
    center = total * (1.0 / D)
    factor = lax.rsqrt(square * (1.0 / D) - center * center + EPSILON)
    stats[0:1, :] = center
    stats[1:2, :] = factor
    for i in range(count):
        rows = slice(i * blk, (i + 1) * blk)
        normed = (res[i] - center) * factor
        feat[i] = (normed * (1.0 + mod[0, rows, 1:2]) + mod[0, rows, 0:1]).astype(BF16)


def mid_kernel(res, att, mod, mid, feat, stats):
    count, blk, _ = res.shape
    total = jnp.zeros((1, SLOTS), F32)
    square = jnp.zeros((1, SLOTS), F32)
    for i in range(count):
        rows = slice(i * blk, (i + 1) * blk)
        value = res[i] + mod[0, rows, 2:3] * att[i]
        mid[i] = value
        total = total + jnp.sum(value, axis=0, keepdims=True)
        square = square + jnp.sum(value * value, axis=0, keepdims=True)
    center = total * (1.0 / D)
    factor = lax.rsqrt(square * (1.0 / D) - center * center + EPSILON)
    stats[0:1, :] = center
    stats[1:2, :] = factor
    for i in range(count):
        rows = slice(i * blk, (i + 1) * blk)
        normed = (mid[i] - center) * factor
        feat[i] = (normed * (1.0 + mod[0, rows, 4:5]) + mod[0, rows, 3:4]).astype(BF16)


def out_kernel(idx, mid, red, cot, mod, own, other, red_grad, cols, hold):
    count, blk, _ = mid.shape
    for i in range(count):
        rows = slice(i * blk, (i + 1) * blk)
        gate = mod[0, rows, 5:6]
        reduced = red[i]
        upstream = cot[idx[i]].astype(F32)
        hold[idx[i]] = mid[i] + gate * reduced
        rounded = (upstream * gate).astype(BF16)
        red_grad[i] = rounded
        cols[0, rows, 0:1] = jnp.sum(upstream * reduced, axis=1, keepdims=True)
        cols[0, rows, 1:2] = jnp.sum(rounded.astype(F32), axis=1, keepdims=True)
    kept = own.shape[0]
    own[...] = hold[0:kept]
    if other is not None:
        other[...] = hold[kept:count].astype(other.dtype)


def back_mid_kernel(idx, fgrad, mid, stats, mod, cot, att, mid_grad, att_grad, cols):
    count, blk, _ = mid.shape
    center, factor = stats[0:1, :], stats[1:2, :]
    first = jnp.zeros((1, SLOTS), F32)
    second = jnp.zeros((1, SLOTS), F32)
    for i in range(count):
        rows = slice(i * blk, (i + 1) * blk)
        grad = fgrad[i]
        normed = (mid[i] - center) * factor
        both = grad * normed
        scale = 1.0 + mod[0, rows, 4:5]
        cols[0, rows, 0:1] = jnp.sum(grad, axis=1, keepdims=True)
        cols[0, rows, 1:2] = jnp.sum(both, axis=1, keepdims=True)
        first = first + jnp.sum(grad * scale, axis=0, keepdims=True)
        second = second + jnp.sum(both * scale, axis=0, keepdims=True)
    first = first * (1.0 / D)
    second = second * (1.0 / D)
    for i in range(count):
        rows = slice(i * blk, (i + 1) * blk)
        scale = 1.0 + mod[0, rows, 4:5]
        normed = (mid[i] - center) * factor
        value = cot[idx[i]].astype(F32) + factor * (fgrad[i] * scale - first - normed * second)
        mid_grad[i] = value
        rounded = (value * mod[0, rows, 2:3]).astype(BF16)
        att_grad[i] = rounded
        cols[0, rows, 2:3] = jnp.sum(value * att[i], axis=1, keepdims=True)
        cols[0, rows, 3:4] = jnp.sum(rounded.astype(F32), axis=1, keepdims=True)


def back_pre_kernel(idx, fgrad, res, stats, mod, mid_grad, own, other, cols, hold):
    count, blk, _ = res.shape
    center, factor = stats[0:1, :], stats[1:2, :]
    first = jnp.zeros((1, SLOTS), F32)
    second = jnp.zeros((1, SLOTS), F32)
    for i in range(count):
        rows = slice(i * blk, (i + 1) * blk)
        grad = fgrad[i]
        normed = (res[i] - center) * factor
        both = grad * normed
        scale = 1.0 + mod[0, rows, 1:2]
        cols[0, rows, 0:1] = jnp.sum(grad, axis=1, keepdims=True)
        cols[0, rows, 1:2] = jnp.sum(both, axis=1, keepdims=True)
        first = first + jnp.sum(grad * scale, axis=0, keepdims=True)
        second = second + jnp.sum(both * scale, axis=0, keepdims=True)
    first = first * (1.0 / D)
    second = second * (1.0 / D)
    for i in range(count):
        rows = slice(i * blk, (i + 1) * blk)
        scale = 1.0 + mod[0, rows, 1:2]
        normed = (res[i] - center) * factor
        hold[idx[i]] = mid_grad[i] + factor * (fgrad[i] * scale - first - normed * second)
    kept = own.shape[0]
    own[...] = hold[0:kept]
    if other is not None:
        other[...] = hold[kept:count].astype(other.dtype)


def masked_scores(keys, queries, present):
    raw = times(keys, queries, 0, 0) * SCALE
    slot = lax.broadcasted_iota(jnp.int32, raw.shape, 0)
    return jnp.where(slot < present, raw, NEGATIVE)


def attend_kernel(present, qkv, mix, logs):
    here = present[pl.program_id(0)]
    for h in range(mix.shape[0]):
        scores = masked_scores(qkv[1, h], qkv[0, h], here)
        highest = jnp.max(scores, axis=0, keepdims=True)
        weight = jnp.exp(scores - highest)
        total = jnp.sum(weight, axis=0, keepdims=True)
        logs[h : h + 1, :] = highest + jnp.log(total)
        attention = (weight * (1.0 / total)).astype(BF16)
        mix[h] = times(qkv[2, h], attention, 1, 0).astype(BF16)


def attend_back_kernel(present, qkv, mix_grad, logs, grads):
    here = present[pl.program_id(0)]
    for h in range(mix_grad.shape[0]):
        queries, keys, values, upstream = qkv[0, h], qkv[1, h], qkv[2, h], mix_grad[h]
        attention = jnp.exp(masked_scores(keys, queries, here) - logs[h : h + 1, :])
        att_grad = times(values, upstream, 0, 0)
        inner = jnp.sum(attention * att_grad, axis=0, keepdims=True)
        score_grad = (attention * (att_grad - inner)).astype(BF16)
        grads[0, h] = (times(keys, score_grad, 1, 0) * SCALE).astype(BF16)
        grads[1, h] = (times(queries, score_grad, 1, 1) * SCALE).astype(BF16)
        grads[2, h] = times(upstream, attention.astype(BF16), 1, 1).astype(BF16)


def build(mesh):
    FS, T = mesh.shape["fsdp"], mesh.shape["tensor"]
    staged = T == 2 and FS % 8 == 0 and (D // FS) % 8 == 0
    Z = FS // 4
    swap_x = [(0, 1), (1, 0)]
    swap_y = [(i, i ^ 2) for i in range(FS)]
    swap_c = [(i, i ^ 1) for i in range(FS)]
    ring_z = [(i, (i + 4) % FS) for i in range(FS)]

    def over_x(v):
        return lax.ppermute(v, "tensor", swap_x)

    def over_y(v):
        return lax.ppermute(v, "fsdp", swap_y)

    def over_c(v):
        return lax.ppermute(v, "fsdp", swap_c)

    def over_z(v):
        return lax.ppermute(v, "fsdp", ring_z)

    def gather_weights(piece):
        if not staged:
            whole = lax.all_gather(piece, "fsdp", axis=0, tiled=True)
            whole = lax.all_gather(whole, "tensor", axis=0, tiled=False)
            return [[whole[i]] for i in range(T)]
        held = [piece]
        for _ in range(Z - 1):
            held.append(over_z(held[-1]))
        base = jnp.concatenate(held, axis=0)
        half = base.shape[0] // 2
        side_x, side_y = over_x(base), over_y(base)
        far_a = over_x(side_y[:half])
        far_b = over_y(side_x[half:])
        own = [base, side_y]
        other = [side_x, far_a, far_b]
        own = own + [over_c(v) for v in own]
        other = other + [over_c(v) for v in other]
        return [own, other]

    def joined(parts, start, stop):
        return jnp.concatenate([v[:, start:stop] for v in parts], axis=0)

    def scatter_grads(left, rights):
        if not staged:
            local = jnp.stack([times(left, r, 1, 1).astype(BF16) for r in rights], axis=0)
            part = lax.psum_scatter(local, "tensor", scatter_dimension=0, tiled=True)[0]
            return lax.psum_scatter(part, "fsdp", scatter_dimension=0, tiled=True).astype(F32)
        rows = D // 2
        sent = [over_c(times(left[rows:], r, 1, 1).astype(BF16)) for r in rights]
        own, other = [
            (times(left[:rows], r, 1, 1) + s.astype(F32)).astype(BF16)
            for r, s in zip(rights, sent)
        ]
        quarter, half = rows // 4, rows // 2
        from_x = over_x(other[half : half + quarter]).astype(F32)
        from_y = over_y(other[half + quarter :]).astype(F32)
        send_y = jnp.concatenate(
            [
                (own[half : half + quarter].astype(F32) + from_x).astype(BF16),
                own[half + quarter :],
            ],
            axis=0,
        )
        send_x = jnp.concatenate(
            [
                other[:quarter],
                (other[quarter:half].astype(F32) + from_y).astype(BF16),
            ],
            axis=0,
        )
        base = own[:half].astype(F32) + over_x(send_x).astype(F32) + over_y(send_y).astype(F32)
        blk = half // Z
        moving = base[blk : 2 * blk].astype(BF16)
        for k in range(2, Z + 1):
            slot = k % Z
            moving = over_z(moving).astype(F32) + base[slot * blk : (slot + 1) * blk]
            if slot:
                moving = moving.astype(BF16)
        return moving

    def per_device(
        tokens,
        condition,
        grid_shapes,
        cotangent,
        modulation_weight,
        modulation_bias,
        attend_weight,
        attend_bias,
        merge_weight,
        merge_bias,
        expand_weight,
        expand_bias,
        reduce_weight,
        reduce_bias,
    ):
        width = tokens.shape[0]
        hidden = expand_weight.shape[1]
        heads = width // HD
        group = condition.shape[0]
        images = group // T
        tok = images * SLOTS
        t, f = lax.axis_index("tensor"), lax.axis_index("fsdp")
        NB = FS if staged else 16
        blk = D // NB
        KB = NB // T if staged else NB
        rows_w = D // FS

        slot = jnp.arange(NB, dtype=jnp.int32)
        if staged:
            z, y, c = f // 4, (f // 2) % 2, f % 2
            c_rel, y_rel, k_rel = slot // (2 * Z), (slot // Z) % 2, slot % Z
            order = ((z - k_rel + Z) % Z) * 4 + (y ^ y_rel) * 2 + (c ^ c_rel)
            pick = ((order // KB) ^ t) * KB + order % KB
        else:
            order = slot
            pick = slot
        back = jnp.sum(
            jnp.where(pick[None, :] == slot[:, None], slot[None, :], 0), axis=1
        )

        attend_parts = gather_weights(attend_weight.reshape(rows_w, 3 * width))
        second_parts = gather_weights(
            jnp.concatenate([merge_weight.T, expand_weight], axis=1)
        )
        reduce_parts = gather_weights(reduce_weight.T)

        def spread(array):
            if not staged:
                whole = lax.all_to_all(array, "tensor", split_axis=1, concat_axis=0, tiled=True)
                return whole.reshape(NB, blk, tok)
            own = lax.dynamic_slice(array, (0, t * tok), (width, tok))
            recv = over_x(lax.dynamic_slice(array, (0, (1 - t) * tok), (width, tok)))
            return jnp.concatenate([own, recv], axis=0).reshape(NB, blk, tok)

        def collect(own, other):
            if not staged:
                return lax.all_to_all(
                    own.reshape(D, tok), "tensor", split_axis=0, concat_axis=1, tiled=True
                )
            recv = over_x(other).astype(F32).reshape(width, tok)
            own = own.reshape(width, tok)
            first = jnp.where(t == 0, own, recv)
            last = jnp.where(t == 0, recv, own)
            return jnp.concatenate([first, last], axis=1)

        cond = condition.astype(F32)
        lifted = jax.nn.silu(cond).astype(BF16)
        lifted_all = lax.all_gather(lifted, "fsdp", axis=0, tiled=True)
        lifted_cols = lax.dynamic_slice(
            lifted_all, (0, f * rows_w), (lifted_all.shape[0], rows_w)
        )
        mod_weight = modulation_weight.reshape(rows_w, 6 * width)
        mod_part = times(lifted_cols, mod_weight, 1, 0)
        mod_group = lax.psum_scatter(mod_part, "fsdp", scatter_dimension=0, tiled=True)
        mod_group = mod_group.reshape(group, 6, width) + modulation_bias.astype(F32)
        if staged:
            own = lax.dynamic_slice(mod_group, (t * images, 0, 0), (images, 6, width))
            recv = over_x(
                lax.dynamic_slice(mod_group, ((1 - t) * images, 0, 0), (images, 6, width))
            )
            mod = jnp.concatenate([own, recv], axis=2)
        else:
            mod = lax.all_to_all(mod_group, "tensor", split_axis=0, concat_axis=2, tiled=True)
        mod = jnp.take(mod.reshape(images, 6, NB, blk), pick, axis=2).reshape(images, 6, D)
        mod = jnp.pad(jnp.swapaxes(mod, 1, 2), ((0, 0), (0, 0), (0, 2)))

        bias_local = jnp.concatenate(
            [attend_bias.reshape(-1), expand_bias, merge_bias, reduce_bias]
        )
        if staged:
            bias_all = jnp.stack([bias_local, over_x(bias_local)], axis=0)
        else:
            bias_all = lax.all_gather(bias_local, "tensor", axis=0, tiled=False)
        bias_all = bias_all.astype(F32)
        at = 2 * width
        zeros = jnp.zeros((T, width), F32)
        attend_b = jnp.concatenate([bias_all[:, :width], zeros, bias_all[:, width:at]], axis=1)
        expand_b = bias_all[:, at : at + hidden]
        at = at + hidden

        def channels(block):
            return jnp.take(block.reshape(NB, blk), pick, axis=0).reshape(D, 1)

        merge_b = channels(bias_all[:, at : at + width])
        reduce_b = channels(bias_all[:, at + width : at + 2 * width])

        grids = lax.dynamic_slice(grid_shapes, (t * images, 0), (images, 2))
        present = grids[:, 0] * grids[:, 1]
        line = jnp.arange(SLOTS, dtype=jnp.int32)
        spots = jnp.stack([line[None, :] // grids[:, 1:2], line[None, :] % grids[:, 1:2]], axis=1)
        spots = jnp.pad(spots, ((0, 0), (0, 6), (0, 0)))
        channel = (order[:, None] * blk + jnp.arange(blk, dtype=jnp.int32)[None, :]).reshape(D)
        quarter = channel // (D // 4)
        within = channel % (D // 4)
        frequency = jnp.exp(within.astype(F32) * (-math.log(10000.0) / (D // 4)))
        angle = jnp.arange(SPOTS, dtype=jnp.int32).astype(F32)[None, :] * frequency[:, None]
        wave = jnp.where((quarter % 2 == 0)[:, None], jnp.sin(angle), jnp.cos(angle))
        high = lax.reduce_precision(wave, 8, 7)
        middle_bits = lax.reduce_precision(wave - high, 8, 7)
        low_bits = lax.reduce_precision(wave - high - middle_bits, 8, 7)
        bits = jnp.concatenate([high, middle_bits, low_bits], axis=1)
        by_row = (quarter < 2)[:, None]
        table = jnp.concatenate(
            [jnp.where(by_row, bits, 0.0), jnp.where(by_row, 0.0, bits)], axis=1
        )
        table = table.astype(BF16).reshape(NB, blk, 6 * SPOTS)

        cube = (NB, blk, tok)
        big = image_rows(NB, blk)
        kept_spec = image_rows(KB, blk)
        stat_spec = pl.BlockSpec((8, SLOTS), lambda i: (0, i))
        act_bytes = D * tok * 4

        tokens_all = spread(tokens)
        cot_all = spread(cotangent)
        residual, features_a, stats_a = pl.pallas_call(
            pre_kernel,
            name="pre",
            grid=(images,),
            in_specs=[
                smem(),
                big,
                pl.BlockSpec((NB, blk, 6 * SPOTS), lambda i: (0, 0, 0)),
                pl.BlockSpec((1, 8, SLOTS), lambda i: (i, 0, 0)),
                column_spec(8),
            ],
            out_specs=[big, big, stat_spec],
            out_shape=[
                jax.ShapeDtypeStruct(cube, F32),
                jax.ShapeDtypeStruct(cube, BF16),
                jax.ShapeDtypeStruct((8, tok), F32),
            ],
            compiler_params=ARB,
            cost_estimate=cost(2 * D * tok * 384, 2 * act_bytes),
        )(pick, tokens_all, table, spots, mod)
        features_a = features_a.reshape(D, tok)

        attend_w = [joined(p, 0, 3 * width) for p in attend_parts]
        head_cube = (heads, HD, tok)
        qkv_spec = pl.BlockSpec((3, heads, HD, SLOTS), lambda i: (0, 0, 0, i))
        head_spec = pl.BlockSpec((heads, HD, SLOTS), lambda i: (0, 0, i))
        log_spec = pl.BlockSpec((heads, SLOTS), lambda i: (0, i))
        qkv, mixture, logs = [], [], []
        for i in range(T):
            projected = times(attend_w[i], features_a, 0, 0) + attend_b[i][:, None]
            qkv.append(projected.astype(BF16).reshape(3, heads, HD, tok))
            mix, log = pl.pallas_call(
                attend_kernel,
                name="attend",
                grid=(images,),
                in_specs=[smem(), qkv_spec],
                out_specs=[head_spec, log_spec],
                out_shape=[
                    jax.ShapeDtypeStruct(head_cube, BF16),
                    jax.ShapeDtypeStruct((heads, tok), F32),
                ],
                compiler_params=ARB,
                cost_estimate=cost(
                    8 * heads * tok * SLOTS * SLOTS, 8 * width * tok, heads * tok * SLOTS
                ),
            )(present, qkv[i])
            mixture.append(mix.reshape(width, tok))
            logs.append(log)
        merge_w = [joined(p, 0, width) for p in second_parts]
        attended = merge_b + sum(times(merge_w[i], mixture[i], 1, 0) for i in range(T))
        attended = attended.reshape(cube)
        middle, features_b, stats_b = pl.pallas_call(
            mid_kernel,
            name="mid",
            grid=(images,),
            in_specs=[big, big, column_spec(8)],
            out_specs=[big, big, stat_spec],
            out_shape=[
                jax.ShapeDtypeStruct(cube, F32),
                jax.ShapeDtypeStruct(cube, BF16),
                jax.ShapeDtypeStruct((8, tok), F32),
            ],
            compiler_params=ARB,
            cost_estimate=cost(10 * D * tok, 4 * act_bytes),
        )(residual, attended, mod)
        features_b = features_b.reshape(D, tok)

        expand_w = [joined(p, width, width + hidden) for p in second_parts]
        expanded = [times(expand_w[i], features_b, 0, 0) + expand_b[i][:, None] for i in range(T)]
        activated = [gelu_tanh(v).astype(BF16) for v in expanded]
        reduce_w = [joined(p, 0, hidden) for p in reduce_parts]
        reduced = reduce_b + sum(times(reduce_w[i], activated[i], 1, 0) for i in range(T))
        kept_cube = (KB, blk, tok)
        other_specs = [kept_spec] if staged else []
        own_out, *other_out, red_grad, cols_out = pl.pallas_call(
            out_kernel if staged else functools.partial(without_other, out_kernel, 6),
            name="out",
            grid=(images,),
            in_specs=[smem(), big, big, big, column_spec(8)],
            out_specs=[kept_spec, *other_specs, big, column_spec(2)],
            out_shape=[
                jax.ShapeDtypeStruct(kept_cube, F32),
                *[jax.ShapeDtypeStruct(kept_cube, F32) for _ in other_specs],
                jax.ShapeDtypeStruct(cube, BF16),
                jax.ShapeDtypeStruct((images, D, 2), F32),
            ],
            scratch_shapes=[pltpu.VMEM((NB, blk, SLOTS), F32)],
            compiler_params=ARB,
            cost_estimate=cost(10 * D * tok, 4 * act_bytes),
        )(pick, middle, reduced.reshape(cube), cot_all, mod)
        output = collect(own_out, other_out[0] if staged else None)
        red_grad = red_grad.reshape(D, tok)

        expand_grad = [
            jax.vjp(gelu_tanh, expanded[i])[1](times(reduce_w[i], red_grad, 0, 0))[0].astype(BF16)
            for i in range(T)
        ]
        reduce_wg = scatter_grads(red_grad, activated)
        features_b_grad = sum(times(expand_w[i], expand_grad[i], 1, 0) for i in range(T))
        expand_wg = scatter_grads(features_b, expand_grad)
        mid_grad, att_grad, cols_mid = pl.pallas_call(
            back_mid_kernel,
            name="back_mid",
            grid=(images,),
            in_specs=[smem(), big, big, stat_spec, column_spec(8), big, big],
            out_specs=[big, big, column_spec(4)],
            out_shape=[
                jax.ShapeDtypeStruct(cube, F32),
                jax.ShapeDtypeStruct(cube, BF16),
                jax.ShapeDtypeStruct((images, D, 4), F32),
            ],
            compiler_params=ARB,
            cost_estimate=cost(20 * D * tok, 5 * act_bytes),
        )(pick, features_b_grad.reshape(cube), middle, stats_b, mod, cot_all, attended)
        att_grad = att_grad.reshape(D, tok)

        qkv_grad = []
        for i in range(T):
            mix_grad = times(merge_w[i], att_grad, 0, 0).astype(BF16).reshape(head_cube)
            grads = pl.pallas_call(
                attend_back_kernel,
                name="attend_back",
                grid=(images,),
                in_specs=[smem(), qkv_spec, head_spec, log_spec],
                out_specs=qkv_spec,
                out_shape=jax.ShapeDtypeStruct((3, heads, HD, tok), BF16),
                compiler_params=ARB,
                cost_estimate=cost(
                    20 * heads * tok * SLOTS * SLOTS, 16 * width * tok, heads * tok * SLOTS
                ),
            )(present, qkv[i], mix_grad, logs[i])
            qkv_grad.append(grads.reshape(3 * width, tok))
        merge_wg = scatter_grads(att_grad, mixture)
        attend_wg = scatter_grads(features_a, qkv_grad)
        features_a_grad = sum(times(attend_w[i], qkv_grad[i], 1, 0) for i in range(T))
        own_in, *other_in, cols_pre = pl.pallas_call(
            back_pre_kernel if staged else functools.partial(without_other, back_pre_kernel, 7),
            name="back_pre",
            grid=(images,),
            in_specs=[smem(), big, big, stat_spec, column_spec(8), big],
            out_specs=[kept_spec, *other_specs, column_spec(2)],
            out_shape=[
                jax.ShapeDtypeStruct(kept_cube, F32),
                *[jax.ShapeDtypeStruct(kept_cube, BF16) for _ in other_specs],
                jax.ShapeDtypeStruct((images, D, 2), F32),
            ],
            scratch_shapes=[pltpu.VMEM((NB, blk, SLOTS), F32)],
            compiler_params=ARB,
            cost_estimate=cost(20 * D * tok, 5 * act_bytes),
        )(pick, features_a_grad.reshape(cube), residual, stats_a, mod, mid_grad)
        tokens_grad = collect(own_in, other_in[0] if staged else None)

        def own_first(values):
            lead = values.shape[:-1]
            blocks = jnp.take(values.reshape(*lead, NB, blk), back, axis=len(lead))
            return blocks.reshape(*lead, T, width)

        def slot_sums(values):
            return jnp.sum(values.astype(F32), axis=1)

        qkv_sums = [slot_sums(v) for v in qkv_grad]
        hidden_sums = [slot_sums(v) for v in expand_grad]
        merge_sums = own_first(jnp.sum(cols_mid[:, :, 3], axis=0))
        reduce_sums = own_first(jnp.sum(cols_out[:, :, 1], axis=0))
        bias_rows = [
            jnp.concatenate(
                [
                    qkv_sums[i][:width],
                    qkv_sums[i][2 * width :],
                    merge_sums[i],
                    hidden_sums[i],
                    reduce_sums[i],
                ]
            )
            for i in range(T)
        ]
        if staged:
            bias_sum = bias_rows[0] + over_x(bias_rows[1])
        else:
            bias_sum = lax.psum_scatter(
                jnp.stack(bias_rows), "tensor", scatter_dimension=0, tiled=True
            )[0]
        bias_sum = lax.psum(bias_sum, "fsdp")

        mod_grad = jnp.stack(
            [
                cols_pre[:, :, 0],
                cols_pre[:, :, 1],
                cols_mid[:, :, 2],
                cols_mid[:, :, 0],
                cols_mid[:, :, 1],
                cols_out[:, :, 0],
            ],
            axis=1,
        ).astype(BF16)
        mod_grad = own_first(mod_grad)
        if staged:
            mine, recv = mod_grad[:, :, 0], over_x(mod_grad[:, :, 1])
            mod_grad = jnp.concatenate(
                [jnp.where(t == 0, mine, recv), jnp.where(t == 0, recv, mine)], axis=0
            )
        else:
            mod_grad = lax.all_to_all(
                mod_grad, "tensor", split_axis=2, concat_axis=0, tiled=True
            )
        flat_grad = mod_grad.reshape(group, 6 * width)
        flat_all = lax.all_gather(flat_grad, "fsdp", axis=0, tiled=True)
        mod_wg = times(lifted_cols, flat_all, 0, 0).reshape(rows_w, 6, width)
        mod_bg = jnp.sum(flat_all.astype(F32), axis=0).reshape(6, width)
        lift_part = times(flat_all, mod_weight, 1, 1)
        lift_rows = lax.all_to_all(lift_part, "fsdp", split_axis=0, concat_axis=1, tiled=True)
        if staged:
            lift_mine = lax.dynamic_slice(lift_rows, (0, t * width), (group, width))
            lift_sent = lax.dynamic_slice(lift_rows, (0, (1 - t) * width), (group, width))
            lift_grad = lift_mine + over_x(lift_sent)
        else:
            lift_grad = lax.psum_scatter(lift_rows, "tensor", scatter_dimension=1, tiled=True)
        cond_here = lax.dynamic_slice(cond, (0, t * width), (group, width))
        cond_grad = jax.vjp(jax.nn.silu, cond_here)[1](lift_grad)[0]

        bounds = [0, 2 * width, 3 * width, 3 * width + hidden, 4 * width + hidden]
        attend_bg, merge_bg, expand_bg, reduce_bg = [
            bias_sum[a:b] for a, b in zip(bounds[:-1], bounds[1:])
        ]
        return (
            output,
            tokens_grad,
            cond_grad,
            mod_wg,
            mod_bg,
            attend_wg.reshape(rows_w, 3, width),
            attend_bg.reshape(2, width),
            merge_wg.T,
            merge_bg,
            expand_wg,
            expand_bg,
            reduce_wg.T,
            reduce_bg,
        )

    return per_device


def without_other(body, place, *refs):
    return body(*refs[:place], None, *refs[place:])


def solution(mesh):
    return jax.shard_map(
        build(mesh),
        mesh=mesh,
        in_specs=(
            P("tensor", "fsdp"),
            P("fsdp", None),
            P("fsdp", None),
            P("tensor", "fsdp"),
            P("fsdp", None, "tensor"),
            P(None, "tensor"),
            P("fsdp", None, "tensor"),
            P(None, "tensor"),
            P("tensor", "fsdp"),
            P("tensor"),
            P("fsdp", "tensor"),
            P("tensor"),
            P("tensor", "fsdp"),
            P("tensor"),
        ),
        out_specs=(
            P("tensor", "fsdp"),
            P("tensor", "fsdp"),
            P("fsdp", "tensor"),
            P("fsdp", None, "tensor"),
            P(None, "tensor"),
            P("fsdp", None, "tensor"),
            P(None, "tensor"),
            P("tensor", "fsdp"),
            P("tensor"),
            P("fsdp", "tensor"),
            P("tensor"),
            P("tensor", "fsdp"),
            P("tensor"),
        ),
        check_vma=False,
    )
```

time: 1860 us -> 994 us (0.53)
  other arithmetic: 497 us -> 62.2 us
  local copies, waits for them, and re-layouts: 336 us -> 111 us
  waiting for transfers between devices: 510 us -> 310 us
  matrix products: 379 us -> 208 us
  Pallas kernels: 0 us -> 108 us
  starting transfers between devices: 6.1 us -> 56.6 us
    reduce_scatter x19 -> x0, waiting for transfers between devices: 322 us -> none  [the longest x8 211 us: branch_output(): lax.psum_scatter(jnp.dot(unit_values, weight_local, preferred_element_typ...]
    ppermute x0 -> x81, waiting for transfers between devices: none -> 255 us  [the longest x23 104 us: over_x(): return lax.ppermute(v, 'tensor', swap_x)]
    reduce_sum x24 -> x6, other arithmetic: 211 us -> 7.91 us  [the longest x2 5.93 us: slot_sums(): return jnp.sum(values.astype(F32), axis=1)]
    all_gather x21 -> x0, waiting for transfers between devices: 181 us -> none  [the longest x8 55.1 us: gather_features(): return lax.all_gather(features, 'tensor', axis=1, tiled=True)]
    add x15 -> x8, other arithmetic: 183 us -> 8.76 us  [the longest x4 6.26 us: scatter_grads(): own[:half].astype(F32) + over_x(send_x).astype(F32)]
    dot_general x84 -> x35, matrix products: 379 us -> 208 us  [times(): lax.dot_general(left, right, (((dim_left,), (dim_right,)), ((), ())), pre...]
    pallas_call x0 -> x9, Pallas kernels: none -> 108 us  [the longest x2 27.9 us: per_device(): pl.pallas_call(attend_back_kernel, name='attend_back', grid=(images,), in...]
    convert_element_type x22 -> x20, other arithmetic: 62.9 us -> 3.3 us  [the longest x1 0.74 us: per_device(): lifted = jax.nn.silu(cond).astype(BF16)]
  transfers between devices with their start and end apart: 43 -> 83, of which waited for: 26 -> 31; matrix products, arithmetic and copies ran while one was open for 61% -> 21% of each run, Pallas kernels for 0% -> 4%
where the time goes in v1:
time: 994 us; the launch traced here: 984 us
  waiting for transfers between devices  310 us (31%)
  matrix products  208 us (21%)
  local copies, waits for them, and re-layouts  111 us (11%)
  blocking collectives  111 us (11%)
  Pallas kernels  108 us (11%)
  other arithmetic  62.2 us (6%)
  starting transfers between devices  56.6 us (6%)
  between operations  17.3 us (2%)
    dot_general x35, matrix products, times(): lax.dot_general(left, right, (((dim_left,), (dim_right,)), ((), ())), pre...  208 us
    ppermute x23, waiting for transfers between devices, over_x(): return lax.ppermute(v, 'tensor', swap_x)  104 us
    ppermute x21, waiting for transfers between devices, over_z(): return lax.ppermute(v, 'fsdp', ring_z)  87.7 us
    ppermute x14, waiting for transfers between devices, over_y(): return lax.ppermute(v, 'fsdp', swap_y)  60.9 us
    psum x1, blocking collectives, per_device(): bias_sum = lax.psum(bias_sum, 'fsdp')  59.6 us
    unnamed x2, waiting for transfers between devices  50.3 us
    unnamed x273, local copies, waits for them, and re-layouts  36.6 us
    all_gather x1, blocking collectives, per_device(): lifted_all = lax.all_gather(lifted, 'fsdp', axis=0, tiled=True)  31.5 us
  transfers between devices with their start and end apart: 83, of which 31 were waited for; matrix products, arithmetic and copies ran while one was open for 21% of the time, Pallas kernels for 4%

profile of v1, /device:TPU:0, one launch (start us, length us, event | category | flops | bytes accessed | tf_op | source)
XLA Modules:
  0.0 984.4 jit_solution(2141941545519098005)
XLA Ops:
  21.3 31.5 %all_gather.6 = bf16[128,1152]{1,0:T(8,128)(2,1)S(1)} all-gather(bf16[8,1152]{1,0:T(8,128)(2,1)S(1)} %multiply_convert_fusion.2), channel_id=1, replica_groups=mesh['fsdp'=16,'tensor'=2] {'fsdp'}, dimensions={0}, use_global_device_ids=true | all-gather | bytes 313344 | tf_op jit(solution)/shard_map/all_gather | solution.py:352
  89.6 10.9 %collective-permute-done.10 = bf16[72,1728]{1,0:T(8,128)(2,1)S(1)} collective-permute-done((bf16[72,1728]{1,0:T(8,128)(2,1)S(1)}, bf16[72,1728]{1,0:T(8,128)(2,1)S(1)}, u32[]{:S(2)}, u32[]{:S(2)}) %collective-permute-start.10) | collective-permute-done | bytes 248864 | tf_op jit(solution)/shard_map/ppermute | solution.py:222
  109.5 50.3 %all-reduce.5.cloned.1.call-done = f32[128,3456]{1,0:T(8,128)} async-done(((f32[128,3456]{1,0:T(8,128)}), f32[128,3456]{1,0:T(8,128)}) %all-reduce.5.cloned.1.call-update) | async-done | bytes 1769488
  209.8 18.2 %collective-permute-done.22 = bf16[144,1728]{1,0:T(8,128)(2,1)S(1)} collective-permute-done((bf16[144,1728]{1,0:T(8,128)(2,1)S(1)}, bf16[144,1728]{1,0:T(8,128)(2,1)S(1)}, u32[]{:S(2)}, u32[]{:S(2)}) %collective-permute-start.22) | collective-permute-done | bytes 497696 | tf_op jit(solution)/shard_map/ppermute | solution.py:213
  229.5 11.7 %collective-permute-done.23 = bf16[144,1728]{1,0:T(8,128)(2,1)S(1)} collective-permute-done((bf16[144,1728]{1,0:T(8,128)(2,1)S(1)}, bf16[144,1728]{1,0:T(8,128)(2,1)S(1)}, u32[]{:S(2)}, u32[]{:S(2)}) %collective-permute-start.23) | collective-permute-done | bytes 497696 | tf_op jit(solution)/shard_map/ppermute | solution.py:216
  265.9 12.8 %attend.2 = (bf16[8,72,1024]{2,1,0:T(8,128)(2,1)}, f32[8,1024]{1,0:T(8,128)}) custom-call(s32[4]{0:T(128)} %bitcast_multiply_fusion.present, bf16[3,8,72,1024]{3,2,1,0:T(8,128)(2,1)} %bitcast.191), custom_call_target="tpu_custom_call" | custom-call | flops 4294967296 | bytes 4718592 | tf_op jit(solution)/shard_map/attend/pallas_call | solution.py:451
  278.6 12.9 %attend.3 = (bf16[8,72,1024]{2,1,0:T(8,128)(2,1)}, f32[8,1024]{1,0:T(8,128)}) custom-call(s32[4]{0:T(128)} %bitcast_multiply_fusion.present, bf16[3,8,72,1024]{3,2,1,0:T(8,128)(2,1)} %bitcast.193), custom_call_target="tpu_custom_call" | custom-call | flops 4294967296 | bytes 4718592 | tf_op jit(solution)/shard_map/attend/pallas_call | solution.py:451
  355.1 14.3 %multiply_convert_fusion = (bf16[2304,1024]{0,1:T(8,128)(2,1)S(1)}, f32[2304,1024]{0,1:T(8,128)}) fusion(f32[2304]{0:T(1024)S(1)} %get-tuple-element.138, bf16[1152,2304]{1,0:T(8,128)(2,1)} %slice_dynamic-update-slice_fusion.2, bf16[1152,1024]{1,0:T(8,128)(2,1)S(1)} %bitcast.158), kind=kOutput, calls=%fused_computation.26 | convolution fusion | flops 5459410944 | bytes 21832704 | tf_op jit(solution)/shard_map/dot_general | solution.py:23
  379.1 10.8 %multiply_convert_fusion.1 = (bf16[2304,1024]{0,1:T(8,128)(2,1)S(1)}, f32[2304,1024]{0,1:T(8,128)}) fusion(f32[2304]{0:T(1024)S(1)} %copy-done.74, bf16[1152,1024]{1,0:T(8,128)(2,1)S(1)} %bitcast.159, bf16[288,2304]{1,0:T(8,128)(2,1)S(1)} %slice.557, bf16[288,2304]{1,0:T(8,128)(2,1)S(1)} %copy-done.25, bf16[288,2304]{1,0:T(8,128)(2,1)S(1)} %copy-done.27, ...), kind=kOutput, calls=%fused_computation.27 | convolution fusion | flops 5480644608 | bytes 21832704 | tf_op jit(solution)/shard_map/dot_general | solution.py:23
  389.9 10.8 %add_add_fusion = f32[1152,1024]{1,0:T(8,128)} fusion(f32[1152,1024]{1,0:T(8,128)} %fusion.99, bf16[1152,2304]{1,0:T(8,128)(2,1)S(1)} %bitcast.190, bf16[2304,1024]{0,1:T(8,128)(2,1)S(1)} %get-tuple-element.219, f32[1152]{0:T(1024)S(1)} %copy-done.77), kind=kOutput, calls=%fused_computation.39 | convolution fusion | flops 5438177280 | bytes 19468800 | tf_op jit(solution)/shard_map/dot_general | solution.py:23
  400.7 14.2 %out.1 = (f32[8,72,1024]{2,1,0:T(8,128)}, f32[8,72,1024]{2,1,0:T(8,128)}, bf16[16,72,1024]{2,1,0:T(8,128)(2,1)}, f32[4,1152,2]{2,1,0:T(8,128)}) custom-call(s32[16]{0:T(128)} %copy-done.72, f32[16,72,1024]{2,1,0:T(8,128)} %get-tuple-element.38.mid, f32[16,72,1024]{2,1,0:T(8,128)} %bitcast.147, bf16[16,72,1024]{2,1,0:T(8,128)(2,1)} %bitcast.135, ...), custom_call_target="tpu_custom_call" | custom-call | flops 11796480 | bytes 18874368 | tf_op jit(solution)/shard_map/out/pallas_call | solution.py:494
  415.0 19.2 %convert_reduce_fusion.1 = (f32[2304]{0:T(1024)}, bf16[2304,1024]{0,1:T(8,128)(2,1)}) fusion(f32[2304,1024]{0,1:T(8,128)} %get-tuple-element.220, f32[2304]{0:T(1024)S(1)} %copy-done.74, bf16[1152,2304]{1,0:T(8,128)(2,1)} %constant_dynamic-update-slice_fusion.17, bf16[1152,1024]{1,0:T(8,128)(2,1)} %bitcast.156), kind=kOutput, calls=%fused_computation.25 | convolution fusion | flops 5490079744 | bytes 21841920 | tf_op jit(solution)/shard_map/dot_general | solution.py:23
  434.2 16.9 %convert_reduce_fusion = (f32[2304]{0:T(1024)}, bf16[2304,1024]{0,1:T(8,128)(2,1)S(1)}) fusion(f32[2304,1024]{0,1:T(8,128)} %get-tuple-element.218, f32[2304]{0:T(1024)S(1)} %get-tuple-element.138, bf16[1152,2304]{1,0:T(8,128)(2,1)} %constant_dynamic-update-slice_fusion.24, bf16[1152,1024]{1,0:T(8,128)(2,1)S(1)} %bitcast.157), kind=kOutput, calls=%fused_computation.24 | convolution fusion | flops 5490079744 | bytes 21841920 | tf_op jit(solution)/shard_map/dot_general | solution.py:23
  458.8 12.8 %convolution_add_fusion.1 = f32[1152,1024]{1,0:T(8,128)} fusion(f32[1152,1024]{1,0:T(8,128)} %fusion.100, bf16[2304,1024]{0,1:T(8,128)(2,1)} %get-tuple-element.144, bf16[288,2304]{1,0:T(8,128)(2,1)S(1)} %copy-done.30, bf16[288,2304]{1,0:T(8,128)(2,1)S(1)} %copy-done.26, bf16[288,2304]{1,0:T(8,128)(2,1)S(1)} %copy-done.28, bf16[288,2304]{1,0:T(8,128)(2,1)S(1)} %copy-done.24), kind=kOutput, calls=%fused_computation.46 | convolution fusion | flops 5458231296 | bytes 19464192 | tf_op jit(solution)/shard_map/dot_general | solution.py:23
  471.6 14.6 %back_mid.1 = (f32[16,72,1024]{2,1,0:T(8,128)}, bf16[16,72,1024]{2,1,0:T(8,128)(2,1)}, f32[4,1152,4]{2,1,0:T(8,128)}) custom-call(s32[16]{0:T(128)} %copy-done.72, f32[16,72,1024]{2,1,0:T(8,128)} %bitcast.146, f32[16,72,1024]{2,1,0:T(8,128)} %get-tuple-element.38.mid, f32[8,1024]{1,0:T(8,128)} %get-tuple-element.43.stats, f32[4,1152,8]{2,1,0:T(8,128)} %pad.9.mod, ...), custom_call_target="tpu_custom_call" | custom-call | flops 23592960 | bytes 23592960 | tf_op jit(solution)/shard_map/back_mid/pallas_call | solution.py:520
  529.0 13.9 %attend_back.3 = bf16[3,8,72,1024]{3,2,1,0:T(8,128)(2,1)} custom-call(s32[4]{0:T(128)} %bitcast_multiply_fusion.present, bf16[3,8,72,1024]{3,2,1,0:T(8,128)(2,1)} %bitcast.194, bf16[8,72,1024]{2,1,0:T(8,128)(2,1)} %bitcast.202, f32[8,1024]{1,0:T(8,128)} %get-tuple-element.46.logs), custom_call_target="tpu_custom_call" | custom-call | flops 10737418240 | bytes 9437184 | tf_op jit(solution)/shard_map/attend_back/pallas_call | solution.py:539
  546.8 14.0 %attend_back.2 = bf16[3,8,72,1024]{3,2,1,0:T(8,128)(2,1)} custom-call(s32[4]{0:T(128)} %bitcast_multiply_fusion.present, bf16[3,8,72,1024]{3,2,1,0:T(8,128)(2,1)} %bitcast.192, bf16[8,72,1024]{2,1,0:T(8,128)(2,1)} %bitcast.201, f32[8,1024]{1,0:T(8,128)} %get-tuple-element.45.logs), custom_call_target="tpu_custom_call" | custom-call | flops 10737418240 | bytes 9437184 | tf_op jit(solution)/shard_map/attend_back/pallas_call | solution.py:539
  607.0 59.6 %psum.7 = f32[4608]{0:T(1024)S(1)} all-reduce(f32[4608]{0:T(1024)S(1)} %add.656), channel_id=1, replica_groups=mesh['fsdp'=16,'tensor'=2] {'fsdp'}, use_global_device_ids=true, to_apply=%region_9.11 | all-reduce | flops 4608 | bytes 36864 | tf_op jit(solution)/shard_map/psum | solution.py:602
  668.9 20.2 %all_gather.7 = bf16[128,3456]{1,0:T(8,128)(2,1)S(1)} all-gather(bf16[8,3456]{1,0:T(8,128)(2,1)S(1)} %reshape.932), channel_id=1, replica_groups=mesh['fsdp'=16,'tensor'=2] {'fsdp'}, dimensions={0}, use_global_device_ids=true | all-gather | bytes 940032 | tf_op jit(solution)/shard_map/all_gather | solution.py:626
  720.3 50.1 %collective-permute-done.43 = f32[8,576]{1,0:T(8,128)S(1)} collective-permute-done((f32[8,576]{1,0:T(8,128)S(1)}, f32[8,576]{1,0:T(8,128)S(1)}, u32[]{:S(2)}, u32[]{:S(2)}) %collective-permute-start.43) | collective-permute-done | bytes 18464 | tf_op jit(solution)/shard_map/ppermute | solution.py:213
  815.6 11.5 %collective-permute-done.48 = bf16[144,1728]{1,0:T(8,128)(2,1)S(1)} collective-permute-done((bf16[144,1728]{1,0:T(8,128)(2,1)S(1)}, bf16[144,1728]{1,0:T(8,128)(2,1)S(1)}, u32[]{:S(2)}, u32[]{:S(2)}) %collective-permute-start.48) | collective-permute-done | bytes 497696 | tf_op jit(solution)/shard_map/ppermute | solution.py:213
  870.3 11.0 %collective-permute-done.74 = bf16[144,2304]{1,0:T(8,128)(2,1)S(1)} collective-permute-done((bf16[144,2304]{1,0:T(8,128)(2,1)S(1)}, bf16[144,2304]{1,0:T(8,128)(2,1)S(1)}, u32[]{:S(2)}, u32[]{:S(2)}) %collective-permute-start.74) | collective-permute-done | bytes 663584 | tf_op jit(solution)/shard_map/ppermute | solution.py:216
  916.2 19.8 %collective-permute-done.75 = bf16[288,2304]{1,0:T(8,128)(2,1)} collective-permute-done((bf16[288,2304]{1,0:T(8,128)(2,1)}, bf16[288,2304]{1,0:T(8,128)(2,1)}, u32[]{:S(2)}, u32[]{:S(2)}) %collective-permute-start.75) | collective-permute-done | bytes 1327136 | tf_op jit(solution)/shard_map/ppermute | solution.py:213
  940.2 12.3 %collective-permute-done.78 = bf16[72,2304]{1,0:T(8,128)(2,1)S(1)} collective-permute-done((bf16[72,2304]{1,0:T(8,128)(2,1)S(1)}, bf16[72,2304]{1,0:T(8,128)(2,1)S(1)}, u32[]{:S(2)}, u32[]{:S(2)}) %collective-permute-start.78) | collective-permute-done | bytes 331808 | tf_op jit(solution)/shard_map/ppermute | solution.py:222
  (672 shorter events, 492.6 us)
Async XLA Ops:
  7.2 152.6 %all-reduce.5.cloned.1.call-start = ((), (), s32[]{:S(2)}) async-start(), calls=%async_computation.1 | async-start | bytes 3538944
  10.2 71.2 %collective-permute-start.2 = (bf16[4608]{0:T(1024)(128)(2,1)S(1)}, bf16[4608]{0:T(1024)(128)(2,1)}, u32[]{:S(2)}, u32[]{:S(2)}) collective-permute-start(bf16[4608]{0:T(1024)(128)(2,1)S(1)} %concatenate.108), channel_id=1, source_target_pairs={{0,1},{1,0},{2,3},{3,2},{4,5},{5,4},{6,7},{7,6},{8,9},{9,8},{10,11... | collective-permute-start | bytes 27656 | tf_op jit(solution)/shard_map/ppermute | solution.py:213
  13.2 75.6 %collective-permute-start.27 = (bf16[72,2304]{1,0:T(8,128)(2,1)}, bf16[72,2304]{1,0:T(8,128)(2,1)S(1)}, u32[]{:S(2)}, u32[]{:S(2)}) collective-permute-start(bf16[72,2304]{1,0:T(8,128)(2,1)} %bitcast.162), channel_id=1, source_target_pairs={{0,8},{2,10},{4,12},{6,14},{8,16},{10,18},{12,20},{14,22},{16,24},... | collective-permute-start | bytes 995336 | tf_op jit(solution)/shard_map/ppermute | solution.py:222
  16.1 71.8 %collective-permute-start.9 = (bf16[72,1728]{1,0:T(8,128)(2,1)S(1)}, bf16[72,1728]{1,0:T(8,128)(2,1)S(1)}, u32[]{:S(2)}, u32[]{:S(2)}) collective-permute-start(bf16[72,1728]{1,0:T(8,128)(2,1)S(1)} %reshape.913), channel_id=1, source_target_pairs={{0,8},{2,10},{4,12},{6,14},{8,16},{10,18},{12,20},{14,22},{16,24},... | collective-permute-start | bytes 746504 | tf_op jit(solution)/shard_map/ppermute | solution.py:222
  18.9 70.7 %collective-permute-start.3 = (bf16[72,2880]{1,0:T(8,128)(2,1)S(1)}, bf16[72,2880]{1,0:T(8,128)(2,1)}, u32[]{:S(2)}, u32[]{:S(2)}) collective-permute-start(bf16[72,2880]{1,0:T(8,128)(2,1)S(1)} %pad_maximum_fusion.18), channel_id=1, source_target_pairs={{0,8},{2,10},{4,12},{6,14},{8,16},{10,18},{12,20},{14,22},{16,24},... | collective-permute-start | bytes 1244168 | tf_op jit(solution)/shard_map/ppermute | solution.py:222
  58.1 119.7 %collective-permute-start = (bf16[576,1024]{1,0:T(8,128)(2,1)}, bf16[576,1024]{1,0:T(8,128)(2,1)}, u32[]{:S(2)}, u32[]{:S(2)}) collective-permute-start(bf16[576,1024]{1,0:T(8,128)(2,1)} %get-tuple-element.168), channel_id=1, source_target_pairs={{0,1},{1,0},{2,3},{3,2},{4,5},{5,4},{6,7},{7,6},{8,9},{9,8},{10,11... | collective-permute-start | bytes 3538952 | tf_op jit(solution)/shard_map/ppermute | solution.py:213
  81.4 99.8 %collective-permute-start.39 = (bf16[576,1024]{1,0:T(8,128)(2,1)}, bf16[576,1024]{1,0:T(8,128)(2,1)}, u32[]{:S(2)}, u32[]{:S(2)}) collective-permute-start(bf16[576,1024]{1,0:T(8,128)(2,1)} %get-tuple-element.166), channel_id=1, source_target_pairs={{0,1},{1,0},{2,3},{3,2},{4,5},{5,4},{6,7},{7,6},{8,9},{9,8},{10,11... | collective-permute-start | bytes 3538952 | tf_op jit(solution)/shard_map/ppermute | solution.py:213
  89.6 86.6 %collective-permute-start.4 = (bf16[72,2880]{1,0:T(8,128)(2,1)}, bf16[72,2880]{1,0:T(8,128)(2,1)}, u32[]{:S(2)}, u32[]{:S(2)}) collective-permute-start(bf16[72,2880]{1,0:T(8,128)(2,1)} %collective-permute-done.3), channel_id=1, source_target_pairs={{0,8},{2,10},{4,12},{6,14},{8,16},{10,18},{12,20},{14,22},{16,24},... | collective-permute-start | bytes 1244168 | tf_op jit(solution)/shard_map/ppermute | solution.py:222
  100.5 60.3 %collective-permute-start.11 = (bf16[72,1728]{1,0:T(8,128)(2,1)S(1)}, bf16[72,1728]{1,0:T(8,128)(2,1)S(1)}, u32[]{:S(2)}, u32[]{:S(2)}) collective-permute-start(bf16[72,1728]{1,0:T(8,128)(2,1)S(1)} %collective-permute-done.10), channel_id=1, source_target_pairs={{0,8},{2,10},{4,12},{6,14},{8,16},{10,18},{12,20},{14,22},{16,24},... | collective-permute-start | bytes 746504 | tf_op jit(solution)/shard_map/ppermute | solution.py:222
  107.7 64.5 %collective-permute-start.29 = (bf16[72,2304]{1,0:T(8,128)(2,1)}, bf16[72,2304]{1,0:T(8,128)(2,1)}, u32[]{:S(2)}, u32[]{:S(2)}) collective-permute-start(bf16[72,2304]{1,0:T(8,128)(2,1)} %collective-permute-done.28), channel_id=1, source_target_pairs={{0,8},{2,10},{4,12},{6,14},{8,16},{10,18},{12,20},{14,22},{16,24},... | collective-permute-start | bytes 995336 | tf_op jit(solution)/shard_map/ppermute | solution.py:222
  181.2 59.9 %collective-permute-start.33 = (bf16[288,2304]{1,0:T(8,128)(2,1)}, bf16[288,2304]{1,0:T(8,128)(2,1)}, u32[]{:S(2)}, u32[]{:S(2)}) collective-permute-start(bf16[288,2304]{1,0:T(8,128)(2,1)} %pad_maximum_fusion.7), channel_id=1, source_target_pairs={{0,1},{1,0},{2,3},{3,2},{4,5},{5,4},{6,7},{7,6},{8,9},{9,8},{10,11... | collective-permute-start | bytes 3981320 | tf_op jit(solution)/shard_map/ppermute | solution.py:213
  228.0 63.5 %collective-permute-start.15 = (bf16[288,2880]{1,0:T(8,128)(2,1)S(1)}, bf16[288,2880]{1,0:T(8,128)(2,1)S(1)}, u32[]{:S(2)}, u32[]{:S(2)}) collective-permute-start(bf16[288,2880]{1,0:T(8,128)(2,1)S(1)} %pad_maximum_fusion.5), channel_id=1, source_target_pairs={{0,1},{1,0},{2,3},{3,2},{4,5},{5,4},{6,7},{7,6},{8,9},{9,8},{10,11... | collective-permute-start | bytes 4976648 | tf_op jit(solution)/shard_map/ppermute | solution.py:213
  258.3 52.6 %collective-permute-start.35 = (bf16[144,2304]{1,0:T(8,128)(2,1)}, bf16[144,2304]{1,0:T(8,128)(2,1)}, u32[]{:S(2)}, u32[]{:S(2)}) collective-permute-start(bf16[144,2304]{1,0:T(8,128)(2,1)} %slice.559), channel_id=1, source_target_pairs={{0,4},{2,6},{4,0},{6,2},{8,12},{10,14},{12,8},{14,10},{16,20},{18,... | collective-permute-start | bytes 1990664 | tf_op jit(solution)/shard_map/ppermute | solution.py:216
  603.5 65.2 %collective-permute-start.42 = (bf16[4,6,576]{2,0,1:T(4,128)(2,1)S(1)}, bf16[4,6,576]{2,0,1:T(4,128)(2,1)S(1)}, u32[]{:S(2)}, u32[]{:S(2)}) collective-permute-start(bf16[4,6,576]{2,0,1:T(4,128)(2,1)S(1)} %bitcast.188), channel_id=1, source_target_pairs={{0,1},{1,0},{2,3},{3,2},{4,5},{5,4},{6,7},{7,6},{8,9},{9,8},{10,11... | collective-permute-start | bytes 82952 | tf_op jit(solution)/shard_map/ppermute | solution.py:213
  604.9 171.8 %collective-permute-start.41 = (bf16[8,72,1024]{2,1,0:T(8,128)(2,1)}, bf16[8,72,1024]{2,1,0:T(8,128)(2,1)}, u32[]{:S(2)}, u32[]{:S(2)}) collective-permute-start(bf16[8,72,1024]{2,1,0:T(8,128)(2,1)} %get-tuple-element.50), channel_id=1, source_target_pairs={{0,1},{1,0},{2,3},{3,2},{4,5},{5,4},{6,7},{7,6},{8,9},{9,8},{10,11... | collective-permute-start | bytes 3538952 | tf_op jit(solution)/shard_map/ppermute | solution.py:213
  605.6 185.3 %collective-permute-start.44 = (bf16[576,1728]{1,0:T(8,128)(2,1)}, bf16[576,1728]{1,0:T(8,128)(2,1)}, u32[]{:S(2)}, u32[]{:S(2)}) collective-permute-start(bf16[576,1728]{1,0:T(8,128)(2,1)} %convolution_convert_fusion.5), channel_id=1, source_target_pairs={{0,2},{2,0},{4,6},{6,4},{8,10},{10,8},{12,14},{14,12},{16,18},{18,... | collective-permute-start | bytes 5971976 | tf_op jit(solution)/shard_map/ppermute | solution.py:219
  605.6 189.9 %collective-permute-start.45 = (bf16[576,1728]{1,0:T(8,128)(2,1)}, bf16[576,1728]{1,0:T(8,128)(2,1)}, u32[]{:S(2)}, u32[]{:S(2)}) collective-permute-start(bf16[576,1728]{1,0:T(8,128)(2,1)} %convolution_convert_fusion.4), channel_id=1, source_target_pairs={{0,2},{2,0},{4,6},{6,4},{8,10},{10,8},{12,14},{14,12},{16,18},{18,... | collective-permute-start | bytes 5971976 | tf_op jit(solution)/shard_map/ppermute | solution.py:219
  606.2 88.7 %collective-permute-start.54 = (bf16[576,576]{1,0:T(8,128)(2,1)}, bf16[576,576]{1,0:T(8,128)(2,1)}, u32[]{:S(2)}, u32[]{:S(2)}) collective-permute-start(bf16[576,576]{1,0:T(8,128)(2,1)} %convolution_convert_fusion.9), channel_id=1, source_target_pairs={{0,2},{2,0},{4,6},{6,4},{8,10},{10,8},{12,14},{14,12},{16,18},{18,... | collective-permute-start | bytes 1990664 | tf_op jit(solution)/shard_map/ppermute | solution.py:219
  717.0 82.7 %collective-permute-start.40 = (f32[8,72,1024]{2,1,0:T(8,128)}, f32[8,72,1024]{2,1,0:T(8,128)S(1)}, u32[]{:S(2)}, u32[]{:S(2)}) collective-permute-start(f32[8,72,1024]{2,1,0:T(8,128)} %get-tuple-element.41), channel_id=1, source_target_pairs={{0,1},{1,0},{2,3},{3,2},{4,5},{5,4},{6,7},{7,6},{8,9},{9,8},{10,11... | collective-permute-start | bytes 7077896 | tf_op jit(solution)/shard_map/ppermute | solution.py:213
  776.7 52.2 %collective-permute-start.64 = (bf16[576,2304]{1,0:T(8,128)(2,1)}, bf16[576,2304]{1,0:T(8,128)(2,1)S(1)}, u32[]{:S(2)}, u32[]{:S(2)}) collective-permute-start(bf16[576,2304]{1,0:T(8,128)(2,1)} %convolution_convert_fusion.2), channel_id=1, source_target_pairs={{0,2},{2,0},{4,6},{6,4},{8,10},{10,8},{12,14},{14,12},{16,18},{18,... | collective-permute-start | bytes 7962632 | tf_op jit(solution)/shard_map/ppermute | solution.py:219
  795.5 54.0 %collective-permute-start.73 = (bf16[576,2304]{1,0:T(8,128)(2,1)S(1)}, bf16[576,2304]{1,0:T(8,128)(2,1)}, u32[]{:S(2)}, u32[]{:S(2)}) collective-permute-start(bf16[576,2304]{1,0:T(8,128)(2,1)S(1)} %copy-done.87), channel_id=1, source_target_pairs={{0,2},{2,0},{4,6},{6,4},{8,10},{10,8},{12,14},{14,12},{16,18},{18,... | collective-permute-start | bytes 7962632 | tf_op jit(solution)/shard_map/ppermute | solution.py:219
  827.2 55.0 %collective-permute-start.47 = (bf16[288,1728]{1,0:T(8,128)(2,1)S(1)}, bf16[288,1728]{1,0:T(8,128)(2,1)S(1)}, u32[]{:S(2)}, u32[]{:S(2)}) collective-permute-start(bf16[288,1728]{1,0:T(8,128)(2,1)S(1)} %pad_maximum_fusion.13), channel_id=1, source_target_pairs={{0,1},{1,0},{2,3},{3,2},{4,5},{5,4},{6,7},{7,6},{8,9},{9,8},{10,11... | collective-permute-start | bytes 2985992 | tf_op jit(solution)/shard_map/ppermute | solution.py:213
  828.9 53.2 %collective-permute-start.49 = (bf16[288,1728]{1,0:T(8,128)(2,1)S(1)}, bf16[288,1728]{1,0:T(8,128)(2,1)S(1)}, u32[]{:S(2)}, u32[]{:S(2)}) collective-permute-start(bf16[288,1728]{1,0:T(8,128)(2,1)S(1)} %pad_maximum_fusion.14), channel_id=1, source_target_pairs={{0,4},{2,6},{4,0},{6,2},{8,12},{10,14},{12,8},{14,10},{16,20},{18,... | collective-permute-start | bytes 2985992 | tf_op jit(solution)/shard_map/ppermute | solution.py:216
  883.7 52.3 %collective-permute-start.75 = (bf16[288,2304]{1,0:T(8,128)(2,1)}, bf16[288,2304]{1,0:T(8,128)(2,1)}, u32[]{:S(2)}, u32[]{:S(2)}) collective-permute-start(bf16[288,2304]{1,0:T(8,128)(2,1)} %pad_maximum_fusion.10), channel_id=1, source_target_pairs={{0,1},{1,0},{2,3},{3,2},{4,5},{5,4},{6,7},{7,6},{8,9},{9,8},{10,11... | collective-permute-start | bytes 3981320 | tf_op jit(solution)/shard_map/ppermute | solution.py:213
  (174 other events, 2480.7 us)
Sparse Core Ops, SparseCore 0:
  55.2 104.5 all-reduce.4

commit v2 on v1

--- a/solution.py
+++ b/solution.py
@@ -23,6 +23,10 @@
     return lax.dot_general(
         left, right, (((dim_left,), (dim_right,)), ((), ())), preferred_element_type=F32
     )
+
+
+def fence(*trees):
+    return lax.optimization_barrier(trees)
 
 
 def gelu_tanh(values):
@@ -202,7 +206,7 @@
 
 def build(mesh):
     FS, T = mesh.shape["fsdp"], mesh.shape["tensor"]
-    staged = T == 2 and FS % 8 == 0 and (D // FS) % 8 == 0
+    staged = T == 2 and FS == 16
     Z = FS // 4
     swap_x = [(0, 1), (1, 0)]
     swap_y = [(i, i ^ 2) for i in range(FS)]
@@ -221,65 +225,110 @@
     def over_z(v):
         return lax.ppermute(v, "fsdp", ring_z)
 
-    def gather_weights(piece):
+    def along_z(piece):
         if not staged:
-            whole = lax.all_gather(piece, "fsdp", axis=0, tiled=True)
-            whole = lax.all_gather(whole, "tensor", axis=0, tiled=False)
-            return [[whole[i]] for i in range(T)]
+            return piece
         held = [piece]
         for _ in range(Z - 1):
             held.append(over_z(held[-1]))
-        base = jnp.concatenate(held, axis=0)
+        return jnp.concatenate(held, axis=0)
+
+    def across(base):
+        if not staged:
+            whole = lax.all_gather(base, "fsdp", axis=0, tiled=True)
+            whole = lax.all_gather(whole, "tensor", axis=0, tiled=False)
+            return [[whole[i]] for i in range(T)], whole
         half = base.shape[0] // 2
         side_x, side_y = over_x(base), over_y(base)
         far_a = over_x(side_y[:half])
         far_b = over_y(side_x[half:])
         own = [base, side_y]
         other = [side_x, far_a, far_b]
+        last = (far_a, far_b)
         own = own + [over_c(v) for v in own]
         other = other + [over_c(v) for v in other]
-        return [own, other]
+        return [own, other], last
 
     def joined(parts, start, stop):
         return jnp.concatenate([v[:, start:stop] for v in parts], axis=0)
 
-    def scatter_grads(left, rights):
+    def all_sum(values):
         if not staged:
-            local = jnp.stack([times(left, r, 1, 1).astype(BF16) for r in rights], axis=0)
-            part = lax.psum_scatter(local, "tensor", scatter_dimension=0, tiled=True)[0]
-            return lax.psum_scatter(part, "fsdp", scatter_dimension=0, tiled=True).astype(F32)
-        rows = D // 2
-        sent = [over_c(times(left[rows:], r, 1, 1).astype(BF16)) for r in rights]
-        own, other = [
-            (times(left[:rows], r, 1, 1) + s.astype(F32)).astype(BF16)
-            for r, s in zip(rights, sent)
-        ]
-        quarter, half = rows // 4, rows // 2
-        from_x = over_x(other[half : half + quarter]).astype(F32)
-        from_y = over_y(other[half + quarter :]).astype(F32)
-        send_y = jnp.concatenate(
-            [
+            return lax.psum(values, "fsdp")
+        bit = 1
+        while bit < FS:
+            values = values + lax.ppermute(values, "fsdp", [(i, i ^ bit) for i in range(FS)])
+            bit *= 2
+        return values
+
+    class Scatter:
+        def __init__(self, left, rights):
+            self.left, self.rights, self.state = left, rights, ()
+
+        def low(self):
+            start = D // 2 if staged else 0
+            self.state = [times(self.left[start:], r, 1, 1).astype(BF16) for r in self.rights]
+            return self
+
+        def core(self):
+            if not staged:
+                return self
+            sent = [over_c(v) for v in self.state]
+            self.state = [
+                (times(self.left[: D // 2], r, 1, 1) + v.astype(F32)).astype(BF16)
+                for r, v in zip(self.rights, sent)
+            ]
+            return self
+
+        def first(self):
+            if not staged:
+                return self
+            own, other = self.state
+            quarter, half = D // 8, D // 4
+            from_x = over_x(other[half : half + quarter]).astype(F32)
+            from_y = over_y(other[half + quarter :]).astype(F32)
+            send_y = [
                 (own[half : half + quarter].astype(F32) + from_x).astype(BF16),
                 own[half + quarter :],
-            ],
-            axis=0,
-        )
-        send_x = jnp.concatenate(
-            [
+            ]
+            send_x = [
                 other[:quarter],
                 (other[quarter:half].astype(F32) + from_y).astype(BF16),
-            ],
-            axis=0,
-        )
-        base = own[:half].astype(F32) + over_x(send_x).astype(F32) + over_y(send_y).astype(F32)
-        blk = half // Z
-        moving = base[blk : 2 * blk].astype(BF16)
-        for k in range(2, Z + 1):
-            slot = k % Z
-            moving = over_z(moving).astype(F32) + base[slot * blk : (slot + 1) * blk]
-            if slot:
-                moving = moving.astype(BF16)
-        return moving
+            ]
+            self.state = [
+                own[:half],
+                jnp.concatenate(send_x, axis=0),
+                jnp.concatenate(send_y, axis=0),
+            ]
+            return self
+
+        def second(self):
+            if not staged:
+                return self
+            own, send_x, send_y = self.state
+            base = own.astype(F32) + over_x(send_x).astype(F32) + over_y(send_y).astype(F32)
+            self.state = [base, base[D // 4 // Z : D // 2 // Z].astype(BF16)]
+            self.step = 2
+            return self
+
+        def ring(self):
+            if not staged:
+                return self
+            base, moving = self.state
+            blk = base.shape[0] // Z
+            at = self.step % Z
+            moving = over_z(moving).astype(F32) + base[at * blk : (at + 1) * blk]
+            self.step += 1
+            self.state = [base, moving.astype(BF16) if at else moving]
+            return self
+
+        def done(self):
+            if staged:
+                return self.state[1]
+            part = lax.psum_scatter(
+                jnp.stack(self.state), "tensor", scatter_dimension=0, tiled=True
+            )[0]
+            return lax.psum_scatter(part, "fsdp", scatter_dimension=0, tiled=True).astype(F32)
 
     def per_device(
         tokens,
@@ -322,11 +371,16 @@
             jnp.where(pick[None, :] == slot[:, None], slot[None, :], 0), axis=1
         )
 
-        attend_parts = gather_weights(attend_weight.reshape(rows_w, 3 * width))
-        second_parts = gather_weights(
-            jnp.concatenate([merge_weight.T, expand_weight], axis=1)
-        )
-        reduce_parts = gather_weights(reduce_weight.T)
+        attend_base = along_z(attend_weight.reshape(rows_w, 3 * width))
+        second_piece = jnp.concatenate([merge_weight.T, expand_weight], axis=1)
+        attend_base, second_piece = fence(attend_base, second_piece)
+        second_base = along_z(second_piece)
+        attend_parts, attend_last = across(attend_base)
+        second_base, reduce_piece, attend_last = fence(second_base, reduce_weight.T, attend_last)
+        second_parts, second_last = across(second_base)
+        reduce_base = along_z(reduce_piece)
+        reduce_base, cotangent, second_last = fence(reduce_base, cotangent, second_last)
+        reduce_parts, _ = across(reduce_base)
 
         def spread(array):
             if not staged:
@@ -349,13 +403,12 @@
 
         cond = condition.astype(F32)
         lifted = jax.nn.silu(cond).astype(BF16)
-        lifted_all = lax.all_gather(lifted, "fsdp", axis=0, tiled=True)
-        lifted_cols = lax.dynamic_slice(
-            lifted_all, (0, f * rows_w), (lifted_all.shape[0], rows_w)
-        )
+        lifted_cols = lax.all_to_all(lifted, "fsdp", split_axis=1, concat_axis=0, tiled=True)
         mod_weight = modulation_weight.reshape(rows_w, 6 * width)
-        mod_part = times(lifted_cols, mod_weight, 1, 0)
-        mod_group = lax.psum_scatter(mod_part, "fsdp", scatter_dimension=0, tiled=True)
+        mod_part = times(lifted_cols, mod_weight, 1, 0).reshape(FS, group, 6 * width)
+        mod_group = jnp.sum(
+            lax.all_to_all(mod_part, "fsdp", split_axis=0, concat_axis=0, tiled=True), axis=0
+        )
         mod_group = mod_group.reshape(group, 6, width) + modulation_bias.astype(F32)
         if staged:
             own = lax.dynamic_slice(mod_group, (t * images, 0, 0), (images, 6, width))
@@ -499,7 +552,7 @@
             out_specs=[kept_spec, *other_specs, big, column_spec(2)],
             out_shape=[
                 jax.ShapeDtypeStruct(kept_cube, F32),
-                *[jax.ShapeDtypeStruct(kept_cube, F32) for _ in other_specs],
+                *[jax.ShapeDtypeStruct(kept_cube, BF16) for _ in other_specs],
                 jax.ShapeDtypeStruct(cube, BF16),
                 jax.ShapeDtypeStruct((images, D, 2), F32),
             ],
@@ -510,13 +563,27 @@
         output = collect(own_out, other_out[0] if staged else None)
         red_grad = red_grad.reshape(D, tok)
 
-        expand_grad = [
-            jax.vjp(gelu_tanh, expanded[i])[1](times(reduce_w[i], red_grad, 0, 0))[0].astype(BF16)
-            for i in range(T)
-        ]
-        reduce_wg = scatter_grads(red_grad, activated)
-        features_b_grad = sum(times(expand_w[i], expand_grad[i], 1, 0) for i in range(T))
-        expand_wg = scatter_grads(features_b, expand_grad)
+        def hidden_grad(i, upstream):
+            grad = times(reduce_w[i], upstream, 0, 0)
+            return jax.vjp(gelu_tanh, expanded[i])[1](grad)[0].astype(BF16)
+
+        reduce_s = Scatter(red_grad, activated).low()
+        upstream, reduce_s.state = fence(red_grad, reduce_s.state)
+        expand_grad = [hidden_grad(0, upstream)]
+        reduce_s.core()
+        upstream, expand_grad, reduce_s.state = fence(upstream, expand_grad, reduce_s.state)
+        expand_grad = expand_grad + [hidden_grad(i, upstream) for i in range(1, T)]
+        reduce_s.first()
+        expand_s = Scatter(features_b, expand_grad).low()
+        expand_back, expand_s.state, reduce_s.state = fence(
+            expand_grad, expand_s.state, reduce_s.state
+        )
+        features_b_grad = sum(times(expand_w[i], expand_back[i], 1, 0) for i in range(T))
+        expand_s.core()
+        reduce_s.second()
+        features_b_grad, expand_s.state, reduce_s.state = fence(
+            features_b_grad, expand_s.state, reduce_s.state
+        )
         mid_grad, att_grad, cols_mid = pl.pallas_call(
             back_mid_kernel,
             name="back_mid",
@@ -533,9 +600,18 @@
         )(pick, features_b_grad.reshape(cube), middle, stats_b, mod, cot_all, attended)
         att_grad = att_grad.reshape(D, tok)
 
+        reduce_s.ring()
+        expand_s.first()
+        att_grad, expand_s.state, reduce_s.state = fence(att_grad, expand_s.state, reduce_s.state)
+
+        merge_s = Scatter(att_grad, mixture).low()
+        mix_grad = [
+            times(merge_w[i], att_grad, 0, 0).astype(BF16).reshape(head_cube) for i in range(T)
+        ]
+        reduce_s.ring()
+        mix_grad, merge_s.state, reduce_s.state = fence(mix_grad, merge_s.state, reduce_s.state)
         qkv_grad = []
         for i in range(T):
-            mix_grad = times(merge_w[i], att_grad, 0, 0).astype(BF16).reshape(head_cube)
             grads = pl.pallas_call(
                 attend_back_kernel,
                 name="attend_back",
@@ -547,11 +623,33 @@
                 cost_estimate=cost(
                     20 * heads * tok * SLOTS * SLOTS, 16 * width * tok, heads * tok * SLOTS
                 ),
-            )(present, qkv[i], mix_grad, logs[i])
+            )(present, qkv[i], mix_grad[i], logs[i])
             qkv_grad.append(grads.reshape(3 * width, tok))
-        merge_wg = scatter_grads(att_grad, mixture)
-        attend_wg = scatter_grads(features_a, qkv_grad)
-        features_a_grad = sum(times(attend_w[i], qkv_grad[i], 1, 0) for i in range(T))
+            if i == 0:
+                reduce_s.ring()
+                merge_s.core()
+                qkv_grad, mix_grad, reduce_s.state, merge_s.state = fence(
+                    qkv_grad, mix_grad, reduce_s.state, merge_s.state
+                )
+        expand_s.second()
+        merge_s.first()
+        attend_s = Scatter(features_a, qkv_grad).low()
+        qkv_back, attend_s.state, expand_s.state, merge_s.state = fence(
+            qkv_grad, attend_s.state, expand_s.state, merge_s.state
+        )
+        part = times(attend_w[0], qkv_back[0], 1, 0)
+        attend_s.core()
+        expand_s.ring()
+        part, qkv_back, attend_s.state, expand_s.state = fence(
+            part, qkv_back, attend_s.state, expand_s.state
+        )
+        features_a_grad = part + sum(times(attend_w[i], qkv_back[i], 1, 0) for i in range(1, T))
+        attend_s.first()
+        merge_s.second()
+        expand_s.ring()
+        features_a_grad, attend_s.state, merge_s.state, expand_s.state = fence(
+            features_a_grad, attend_s.state, merge_s.state, expand_s.state
+        )
         own_in, *other_in, cols_pre = pl.pallas_call(
             back_pre_kernel if staged else functools.partial(without_other, back_pre_kernel, 7),
             name="back_pre",
@@ -569,6 +667,14 @@
         )(pick, features_a_grad.reshape(cube), residual, stats_a, mod, mid_grad)
         tokens_grad = collect(own_in, other_in[0] if staged else None)
 
+        expand_s.ring()
+        attend_s.second()
+        for _ in range(Z - 1):
+            merge_s.ring()
+            attend_s.ring()
+        reduce_wg, expand_wg = reduce_s.done(), expand_s.done()
+        merge_wg, attend_wg = merge_s.done(), attend_s.done()
+
         def own_first(values):
             lead = values.shape[:-1]
             blocks = jnp.take(values.reshape(*lead, NB, blk), back, axis=len(lead))
@@ -577,56 +683,66 @@
         def slot_sums(values):
             return jnp.sum(values.astype(F32), axis=1)
 
-        qkv_sums = [slot_sums(v) for v in qkv_grad]
-        hidden_sums = [slot_sums(v) for v in expand_grad]
+        def total(rows):
+            if staged:
+                return all_sum(rows[0] + over_x(rows[1]))
+            return all_sum(
+                lax.psum_scatter(jnp.stack(rows), "tensor", scatter_dimension=0, tiled=True)[0]
+            )
+
         merge_sums = own_first(jnp.sum(cols_mid[:, :, 3], axis=0))
         reduce_sums = own_first(jnp.sum(cols_out[:, :, 1], axis=0))
-        bias_rows = [
-            jnp.concatenate(
-                [
-                    qkv_sums[i][:width],
-                    qkv_sums[i][2 * width :],
-                    merge_sums[i],
-                    hidden_sums[i],
-                    reduce_sums[i],
-                ]
+        hidden_sums = [slot_sums(v) for v in expand_grad]
+        early_sum = total(
+            [jnp.concatenate([merge_sums[i], hidden_sums[i], reduce_sums[i]]) for i in range(T)]
+        )
+        qkv_sums = [slot_sums(v) for v in qkv_grad]
+        attend_bg = total(
+            [jnp.concatenate([v[:width], v[2 * width :]]) for v in qkv_sums]
+        )
+        merge_bg = early_sum[:width]
+        expand_bg = early_sum[width : width + hidden]
+        reduce_bg = early_sum[width + hidden :]
+
+        def share(columns):
+            grad = own_first(jnp.stack(columns, axis=1).astype(BF16))
+            if staged:
+                mine, recv = grad[:, :, 0], over_x(grad[:, :, 1])
+                grad = jnp.concatenate(
+                    [jnp.where(t == 0, mine, recv), jnp.where(t == 0, recv, mine)], axis=0
+                )
+            else:
+                grad = lax.all_to_all(grad, "tensor", split_axis=2, concat_axis=0, tiled=True)
+            flat = grad.reshape(1, group, len(columns) * width)
+            everyone = lax.all_to_all(
+                jnp.broadcast_to(flat, (FS, *flat.shape[1:])),
+                "fsdp",
+                split_axis=0,
+                concat_axis=0,
+                tiled=True,
             )
-            for i in range(T)
-        ]
-        if staged:
-            bias_sum = bias_rows[0] + over_x(bias_rows[1])
-        else:
-            bias_sum = lax.psum_scatter(
-                jnp.stack(bias_rows), "tensor", scatter_dimension=0, tiled=True
-            )[0]
-        bias_sum = lax.psum(bias_sum, "fsdp")
-
-        mod_grad = jnp.stack(
+            return everyone.reshape(FS * group, len(columns) * width)
+
+        early = share(
+            [cols_mid[:, :, 2], cols_mid[:, :, 0], cols_mid[:, :, 1], cols_out[:, :, 0]]
+        )
+        late = share([cols_pre[:, :, 0], cols_pre[:, :, 1]])
+        cut = 2 * width
+        mod_wg = jnp.concatenate(
             [
-                cols_pre[:, :, 0],
-                cols_pre[:, :, 1],
-                cols_mid[:, :, 2],
-                cols_mid[:, :, 0],
-                cols_mid[:, :, 1],
-                cols_out[:, :, 0],
+                times(lifted_cols, late, 0, 0).reshape(rows_w, 2, width),
+                times(lifted_cols, early, 0, 0).reshape(rows_w, 4, width),
             ],
             axis=1,
-        ).astype(BF16)
-        mod_grad = own_first(mod_grad)
-        if staged:
-            mine, recv = mod_grad[:, :, 0], over_x(mod_grad[:, :, 1])
-            mod_grad = jnp.concatenate(
-                [jnp.where(t == 0, mine, recv), jnp.where(t == 0, recv, mine)], axis=0
-            )
-        else:
-            mod_grad = lax.all_to_all(
-                mod_grad, "tensor", split_axis=2, concat_axis=0, tiled=True
-            )
-        flat_grad = mod_grad.reshape(group, 6 * width)
-        flat_all = lax.all_gather(flat_grad, "fsdp", axis=0, tiled=True)
-        mod_wg = times(lifted_cols, flat_all, 0, 0).reshape(rows_w, 6, width)
-        mod_bg = jnp.sum(flat_all.astype(F32), axis=0).reshape(6, width)
-        lift_part = times(flat_all, mod_weight, 1, 1)
+        )
+        mod_bg = jnp.concatenate(
+            [
+                jnp.sum(late.astype(F32), axis=0).reshape(2, width),
+                jnp.sum(early.astype(F32), axis=0).reshape(4, width),
+            ],
+            axis=0,
+        )
+        lift_part = times(late, mod_weight[:, :cut], 1, 1) + times(early, mod_weight[:, cut:], 1, 1)
         lift_rows = lax.all_to_all(lift_part, "fsdp", split_axis=0, concat_axis=1, tiled=True)
         if staged:
             lift_mine = lax.dynamic_slice(lift_rows, (0, t * width), (group, width))
@@ -636,11 +752,6 @@
             lift_grad = lax.psum_scatter(lift_rows, "tensor", scatter_dimension=1, tiled=True)
         cond_here = lax.dynamic_slice(cond, (0, t * width), (group, width))
         cond_grad = jax.vjp(jax.nn.silu, cond_here)[1](lift_grad)[0]
-
-        bounds = [0, 2 * width, 3 * width, 3 * width + hidden, 4 * width + hidden]
-        attend_bg, merge_bg, expand_bg, reduce_bg = [
-            bias_sum[a:b] for a, b in zip(bounds[:-1], bounds[1:])
-        ]
         return (
             output,
             tokens_grad,

time: 994 us -> 796 us (0.80)
  waiting for transfers between devices: 310 us -> 192 us
  blocking collectives: 111 us -> 0 us
  starting transfers between devices: 56.6 us -> 105 us
  local copies, waits for them, and re-layouts: 111 us -> 94.8 us
  between operations: 17.3 us -> 3.21 us
  other arithmetic: 62.2 us -> 74 us
    psum x1 -> x0, blocking collectives: 59.6 us -> none  [per_device(): bias_sum = lax.psum(bias_sum, 'fsdp')]
    ppermute x14, waiting for transfers between devices: 60.9 us -> 7.34 us  [over_y(): return lax.ppermute(v, 'fsdp', swap_y)]
    all_gather x2 -> x0, blocking collectives: 51.8 us -> none  [the longest x1 31.5 us: per_device(): lifted_all = lax.all_gather(lifted, 'fsdp', axis=0, tiled=True)]
    unnamed x2 -> x0, waiting for transfers between devices: 50.3 us -> none
    ppermute x23 -> x25, waiting for transfers between devices: 104 us -> 64.5 us  [over_x(): return lax.ppermute(v, 'tensor', swap_x)]
    ppermute x21, starting transfers between devices: 6.6 us -> 28.7 us  [over_z(): return lax.ppermute(v, 'fsdp', ring_z)]
    all_to_all x0 -> x4, starting transfers between devices: none -> 18 us  [the longest x2 9.38 us: share(): lax.all_to_all(jnp.broadcast_to(flat, (FS, *flat.shape[1:])), 'fsdp', spl...]
    ppermute x21, waiting for transfers between devices: 87.7 us -> 102 us  [over_z(): return lax.ppermute(v, 'fsdp', ring_z)]
  transfers between devices with their start and end apart: 83 -> 96, of which waited for: 31 -> 40; matrix products, arithmetic and copies ran while one was open for 21% -> 42% of each run, Pallas kernels for 4% -> 10%
where the time goes in v2:
time: 796 us; the launch traced here: 785 us
  matrix products  208 us (26%)
  waiting for transfers between devices  192 us (24%)
  Pallas kernels  108 us (14%)
  starting transfers between devices  105 us (13%)
  local copies, waits for them, and re-layouts  94.8 us (12%)
  other arithmetic  74 us (9%)
    dot_general x37, matrix products, times(): lax.dot_general(left, right, (((dim_left,), (dim_right,)), ((), ())), pre...  208 us
    ppermute x21, waiting for transfers between devices, over_z(): return lax.ppermute(v, 'fsdp', ring_z)  102 us
    ppermute x25, waiting for transfers between devices, over_x(): return lax.ppermute(v, 'tensor', swap_x)  64.5 us
    ppermute x21, starting transfers between devices, over_z(): return lax.ppermute(v, 'fsdp', ring_z)  28.7 us
    pallas_call x2, Pallas kernels, per_device(): pl.pallas_call(attend_back_kernel, name='attend_back', grid=(images,), in...  28.7 us
    ppermute x25, starting transfers between devices, over_x(): return lax.ppermute(v, 'tensor', swap_x)  27.1 us
    pallas_call x2, Pallas kernels, per_device(): pl.pallas_call(attend_kernel, name='attend', grid=(images,), in_specs=[sm...  25.8 us
    unnamed x249, local copies, waits for them, and re-layouts  25.1 us
  transfers between devices with their start and end apart: 96, of which 40 were waited for; matrix products, arithmetic and copies ran while one was open for 42% of the time, Pallas kernels for 10%

profile of v2, /device:TPU:0, one launch (start us, length us, event | category | flops | bytes accessed | tf_op | source)
XLA Modules:
  0.0 785.1 jit_solution(7092773043453966306)
XLA Ops:
  26.3 7.8 collective-permute-done.4
  68.0 32.0 %collective-permute-done.7 = bf16[72,2880]{1,0:T(8,128)(2,1)S(1)} collective-permute-done((bf16[72,2880]{1,0:T(8,128)(2,1)}, bf16[72,2880]{1,0:T(8,128)(2,1)S(1)}, u32[]{:S(2)}, u32[]{:S(2)}) %collective-permute-start.7) | collective-permute-done | bytes 414752 | tf_op jit(solution)/shard_map/ppermute | solution.py:226
  100.0 8.0 %collective-permute-start.8 = (bf16[72,2880]{1,0:T(8,128)(2,1)S(1)}, bf16[72,2880]{1,0:T(8,128)(2,1)S(1)}, u32[]{:S(2)}, u32[]{:S(2)}) collective-permute-start(bf16[72,2880]{1,0:T(8,128)(2,1)S(1)} %collective-permute-done.7), channel_id=1, source_target_pairs={{0,8},{2,10},{4,12},{6,14},{8,16},{10,18},{12,20},{14,22},{16,24},... | collective-permute-start | bytes 1244168 | tf_op jit(solution)/shard_map/ppermute | solution.py:226
  144.1 9.5 %collective-permute-done.28 = bf16[72,2304]{1,0:T(8,128)(2,1)} collective-permute-done((bf16[72,2304]{1,0:T(8,128)(2,1)S(1)}, bf16[72,2304]{1,0:T(8,128)(2,1)}, u32[]{:S(2)}, u32[]{:S(2)}) %collective-permute-start.28) | collective-permute-done | bytes 331808 | tf_op jit(solution)/shard_map/ppermute | solution.py:226
  156.1 8.9 %collective-permute-done.29 = bf16[72,2304]{1,0:T(8,128)(2,1)S(1)} collective-permute-done((bf16[72,2304]{1,0:T(8,128)(2,1)}, bf16[72,2304]{1,0:T(8,128)(2,1)S(1)}, u32[]{:S(2)}, u32[]{:S(2)}) %collective-permute-start.29) | collective-permute-done | bytes 331808 | tf_op jit(solution)/shard_map/ppermute | solution.py:226
  167.3 7.8 collective-permute-done.1
  178.8 7.7 pre.1
  186.5 9.5 %add_convert_fusion = bf16[1728,1024]{1,0:T(8,128)(2,1)} fusion(bf16[1152,1728]{1,0:T(8,128)(2,1)} %copy-done.57, bf16[1152,1024]{1,0:T(8,128)(2,1)} %bitcast.185, f32[1728]{0:T(1024)S(1)} %get-tuple-element.257), kind=kOutput, calls=%fused_computation.31 | convolution fusion | flops 4080402432 | bytes 9886464 | tf_op jit(solution)/shard_map/dot_general | solution.py:23
  196.0 12.9 %attend.3 = (bf16[8,72,1024]{2,1,0:T(8,128)(2,1)}, f32[8,1024]{1,0:T(8,128)}) custom-call(s32[4]{0:T(128)} %bitcast_multiply_fusion.present, bf16[3,8,72,1024]{3,2,1,0:T(8,128)(2,1)} %bitcast.225), custom_call_target="tpu_custom_call" | custom-call | flops 4294967296 | bytes 4718592 | tf_op jit(solution)/shard_map/attend/pallas_call | solution.py:504
  218.2 12.9 %attend.2 = (bf16[8,72,1024]{2,1,0:T(8,128)(2,1)}, f32[8,1024]{1,0:T(8,128)}) custom-call(s32[4]{0:T(128)} %bitcast_multiply_fusion.present, bf16[3,8,72,1024]{3,2,1,0:T(8,128)(2,1)} %bitcast.227), custom_call_target="tpu_custom_call" | custom-call | flops 4294967296 | bytes 4718592 | tf_op jit(solution)/shard_map/attend/pallas_call | solution.py:504
  280.1 14.0 %multiply_convert_fusion.1 = (bf16[2304,1024]{1,0:T(8,128)(2,1)S(1)}, f32[2304,1024]{1,0:T(8,128)}) fusion(f32[2304]{0:T(1024)S(1)} %get-tuple-element.254, bf16[1152,1024]{1,0:T(8,128)(2,1)S(1)} %bitcast.183, bf16[288,2304]{1,0:T(8,128)(2,1)S(1)} %slice.545, bf16[288,2304]{1,0:T(8,128)(2,1)} %slice.544, bf16[288,2304]{1,0:T(8,128)(2,1)} %slice.543, ...), kind=kOutput, calls=%fused_computation.28 | convolution fusion | flops 5480644608 | bytes 21832704 | tf_op jit(solution)/shard_map/dot_general | solution.py:23
  296.2 11.5 %multiply_convert_fusion = (bf16[2304,1024]{1,0:T(8,128)(2,1)}, f32[2304,1024]{1,0:T(8,128)}) fusion(f32[2304]{0:T(1024)S(1)} %get-tuple-element.255, bf16[1152,2304]{1,0:T(8,128)(2,1)S(1)} %slice_dynamic-update-slice_fusion.2, bf16[1152,1024]{1,0:T(8,128)(2,1)S(1)} %bitcast.184), kind=kOutput, calls=%fused_computation.27 | convolution fusion | flops 5459410944 | bytes 21832704 | tf_op jit(solution)/shard_map/dot_general | solution.py:23
  329.0 8.1 %collective-permute-done.34 = bf16[144,2304]{1,0:T(8,128)(2,1)S(1)} collective-permute-done((bf16[144,2304]{1,0:T(8,128)(2,1)S(1)}, bf16[144,2304]{1,0:T(8,128)(2,1)S(1)}, u32[]{:S(2)}, u32[]{:S(2)}) %collective-permute-start.34) | collective-permute-done | bytes 663584 | tf_op jit(solution)/shard_map/ppermute | solution.py:217
  354.2 13.6 %out.1 = (f32[8,72,1024]{2,1,0:T(8,128)}, bf16[8,72,1024]{2,1,0:T(8,128)(2,1)}, bf16[16,72,1024]{2,1,0:T(8,128)(2,1)}, f32[4,1152,2]{2,1,0:T(8,128)}) custom-call(s32[16]{0:T(128)} %copy-done.70, f32[16,72,1024]{2,1,0:T(8,128)} %get-tuple-element.106.mid, f32[16,72,1024]{2,1,0:T(8,128)} %bitcast.173, bf16[16,72,1024]{2,1,0:T(8,128)(2,1)} %bitcast.157, ...), custom_call_target="tpu_custom_call" | custom-call | flops 11796480 | bytes 18874368 | tf_op jit(solution)/shard_map/out/pallas_call | solution.py:547
  382.9 14.2 %fusion.6 = bf16[2304,1024]{1,0:T(8,128)(2,1)} fusion(f32[2304,1024]{1,0:T(8,128)S(1)} %bitcast.244, f32[2304]{0:T(1024)S(1)} %get-tuple-element.254, bf16[1152,2304]{1,0:T(8,128)(2,1)S(1)} %bitcast.206, bf16[1152,1024]{1,0:T(8,128)(2,1)S(1)} %bitcast.181), kind=kOutput, calls=%fused_computation.17 | convolution fusion | flops 5485363200 | bytes 21832704 | tf_op jit(solution)/shard_map/dot_general | solution.py:23
  402.2 7.7 collective-permute-done.40
  434.4 16.5 %convert_reduce_fusion = (f32[2304]{0:T(1024)S(1)}, bf16[2304,1024]{1,0:T(8,128)(2,1)}) fusion(f32[2304,1024]{1,0:T(8,128)} %get-tuple-element.327, f32[2304]{0:T(1024)S(1)} %copy-done.72, bf16[1152,2304]{1,0:T(8,128)(2,1)S(1)} %bitcast.208, bf16[1152,1024]{1,0:T(8,128)(2,1)S(1)} %bitcast.182), kind=kOutput, calls=%fused_computation.25 | convolution fusion | flops 5490079744 | bytes 21841920 | tf_op jit(solution)/shard_map/dot_general | solution.py:23
  460.7 9.7 %fusion.105 = f32[1152,1024]{1,0:T(8,128)} fusion(bf16[1152,2304]{1,0:T(8,128)(2,1)} %copy-done.55, bf16[2304,1024]{1,0:T(8,128)(2,1)S(1)} %copy-done.89), kind=kOutput, calls=%fused_computation.349 | convolution fusion | flops 5435817984 | bytes 14745600 | tf_op jit(solution)/shard_map/dot_general | solution.py:23
  470.4 11.9 %convolution_add_fusion = f32[1152,1024]{1,0:T(8,128)} fusion(f32[1152,1024]{1,0:T(8,128)} %fusion.105, bf16[2304,1024]{1,0:T(8,128)(2,1)S(1)} %bitcast.171, bf16[288,2304]{1,0:T(8,128)(2,1)S(1)} %copy-done.30, bf16[288,2304]{1,0:T(8,128)(2,1)S(1)} %copy-done.28, bf16[288,2304]{1,0:T(8,128)(2,1)S(1)} %copy-done.27, bf16[288,2304]{1,0:T(8,128)(2,1)S(1)} %copy-done.26), kind=kOutput, calls=%fused_computation.46 | convolution fusion | flops 5458231296 | bytes 19464192 | tf_op jit(solution)/shard_map/dot_general | solution.py:23
  503.5 14.5 %back_mid.1 = (f32[16,72,1024]{2,1,0:T(8,128)}, bf16[16,72,1024]{2,1,0:T(8,128)(2,1)}, f32[4,1152,4]{2,1,0:T(8,128)}) custom-call(s32[16]{0:T(128)} %copy-done.70, f32[16,72,1024]{2,1,0:T(8,128)} %bitcast.172, f32[16,72,1024]{2,1,0:T(8,128)} %get-tuple-element.106.mid, f32[8,1024]{1,0:T(8,128)} %get-tuple-element.129.stats, f32[4,1152,8]{2,1,0:T(8,128)} %pad.9.mod, ...), custom_call_target="tpu_custom_call" | custom-call | flops 23592960 | bytes 23592960 | tf_op jit(solution)/shard_map/back_mid/pallas_call | solution.py:587
  575.5 14.2 %attend_back.2 = bf16[3,8,72,1024]{3,2,1,0:T(8,128)(2,1)} custom-call(s32[4]{0:T(128)} %bitcast_multiply_fusion.present, bf16[3,8,72,1024]{3,2,1,0:T(8,128)(2,1)} %bitcast.228, bf16[8,72,1024]{2,1,0:T(8,128)(2,1)} %bitcast.236, f32[8,1024]{1,0:T(8,128)} %get-tuple-element.139.logs), custom_call_target="tpu_custom_call" | custom-call | flops 10737418240 | bytes 9437184 | tf_op jit(solution)/shard_map/attend_back/pallas_call | solution.py:615
  604.0 14.5 %attend_back.3 = bf16[3,8,72,1024]{3,2,1,0:T(8,128)(2,1)} custom-call(s32[4]{0:T(128)} %bitcast_multiply_fusion.present, bf16[3,8,72,1024]{3,2,1,0:T(8,128)(2,1)} %bitcast.226, bf16[8,72,1024]{2,1,0:T(8,128)(2,1)} %bitcast.235, f32[8,1024]{1,0:T(8,128)} %get-tuple-element.147.logs), custom_call_target="tpu_custom_call" | custom-call | flops 10737418240 | bytes 9437184 | tf_op jit(solution)/shard_map/attend_back/pallas_call | solution.py:615
  693.7 10.2 %back_pre.1 = (f32[8,72,1024]{2,1,0:T(8,128)}, bf16[8,72,1024]{2,1,0:T(8,128)(2,1)}, f32[4,1152,2]{2,1,0:T(8,128)}) custom-call(s32[16]{0:T(128)} %copy-done.70, f32[16,72,1024]{2,1,0:T(8,128)} %bitcast.168, f32[16,72,1024]{2,1,0:T(8,128)} %get-tuple-element.99.res, f32[8,1024]{1,0:T(8,128)} %get-tuple-element.169.stats, f32[4,1152,8]{2,1,0:T(8,128)} %pad.9.mod, ...), custom_call_target="tpu_custom_call" | custom-call | flops 23592960 | bytes 23592960 | tf_op jit(solution)/shard_map/back_pre/pallas_call | solution.py:653
  759.3 7.8 collective-permute-done.74
  (710 shorter events, 496.3 us)
Async XLA Ops:
  6.7 44.7 %all-to-all-start = ((bf16[8,16,72]{2,0,1:T(8,128)(2,1)}), bf16[8,16,72]{2,0,1:T(8,128)(2,1)S(1)}, u32[]{:S(2)}, u32[]{:S(2)}) async-start(bf16[8,16,72]{2,0,1:T(8,128)(2,1)} %copy.105), calls=%async_computation | async-start | bytes 65536 | tf_op jit(solution)/shard_map/all_to_all | solution.py:406
  14.5 50.5 %collective-permute-start = (bf16[576,1024]{1,0:T(8,128)(2,1)}, bf16[576,1024]{1,0:T(8,128)(2,1)}, u32[]{:S(2)}, u32[]{:S(2)}) collective-permute-start(bf16[576,1024]{1,0:T(8,128)(2,1)} %get-tuple-element.281), channel_id=1, source_target_pairs={{0,1},{1,0},{2,3},{3,2},{4,5},{5,4},{6,7},{7,6},{8,9},{9,8},{10,11... | collective-permute-start | bytes 3538952 | tf_op jit(solution)/shard_map/ppermute | solution.py:217
  46.8 61.3 %collective-permute-start.9 = (bf16[288,1728]{1,0:T(8,128)(2,1)}, bf16[288,1728]{1,0:T(8,128)(2,1)}, u32[]{:S(2)}, u32[]{:S(2)}) collective-permute-start(bf16[288,1728]{1,0:T(8,128)(2,1)} %pad_maximum_fusion.14), channel_id=1, source_target_pairs={{0,4},{2,6},{4,0},{6,2},{8,12},{10,14},{12,8},{14,10},{16,20},{18,... | collective-permute-start | bytes 2985992 | tf_op jit(solution)/shard_map/ppermute | solution.py:220
  48.4 61.3 %collective-permute-start.11 = (bf16[288,1728]{1,0:T(8,128)(2,1)}, bf16[288,1728]{1,0:T(8,128)(2,1)}, u32[]{:S(2)}, u32[]{:S(2)}) collective-permute-start(bf16[288,1728]{1,0:T(8,128)(2,1)} %pad_maximum_fusion.14), channel_id=1, source_target_pairs={{0,1},{1,0},{2,3},{3,2},{4,5},{5,4},{6,7},{7,6},{8,9},{9,8},{10,11... | collective-permute-start | bytes 2985992 | tf_op jit(solution)/shard_map/ppermute | solution.py:217
  53.0 101.3 %all-to-all-start.1 = ((f32[16,8,3456]{2,1,0:T(8,128)}), f32[16,8,3456]{2,1,0:T(8,128)S(1)}, u32[]{:S(2)}, u32[]{:S(2)}) async-start(f32[16,8,3456]{2,1,0:T(8,128)} %fusion.41), calls=%async_computation.1 | async-start | bytes 3538944 | tf_op jit(solution)/shard_map/all_to_all | solution.py:410
  57.3 56.8 %collective-permute-start.16 = (bf16[288,1728]{1,0:T(8,128)(2,1)}, bf16[288,1728]{1,0:T(8,128)(2,1)S(1)}, u32[]{:S(2)}, u32[]{:S(2)}) collective-permute-start(bf16[288,1728]{1,0:T(8,128)(2,1)} %pad_maximum_fusion.14), channel_id=1, source_target_pairs={{0,2},{2,0},{4,6},{6,4},{8,10},{10,8},{12,14},{14,12},{16,18},{18,... | collective-permute-start | bytes 2985992 | tf_op jit(solution)/shard_map/ppermute | solution.py:223
  63.1 36.9 %collective-permute-start.7 = (bf16[72,2880]{1,0:T(8,128)(2,1)}, bf16[72,2880]{1,0:T(8,128)(2,1)S(1)}, u32[]{:S(2)}, u32[]{:S(2)}) collective-permute-start(bf16[72,2880]{1,0:T(8,128)(2,1)} %collective-permute-done.6), channel_id=1, source_target_pairs={{0,8},{2,10},{4,12},{6,14},{8,16},{10,18},{12,20},{14,22},{16,24},... | collective-permute-start | bytes 1244168 | tf_op jit(solution)/shard_map/ppermute | solution.py:226
  122.6 108.5 %collective-permute-start.13 = (bf16[288,2880]{1,0:T(8,128)(2,1)}, bf16[288,2880]{1,0:T(8,128)(2,1)}, u32[]{:S(2)}, u32[]{:S(2)}) collective-permute-start(bf16[288,2880]{1,0:T(8,128)(2,1)} %pad_maximum_fusion.5), channel_id=1, source_target_pairs={{0,4},{2,6},{4,0},{6,2},{8,12},{10,14},{12,8},{14,10},{16,20},{18,... | collective-permute-start | bytes 4976648 | tf_op jit(solution)/shard_map/ppermute | solution.py:220
  134.4 99.6 %collective-permute-start.18 = (bf16[288,2880]{1,0:T(8,128)(2,1)}, bf16[288,2880]{1,0:T(8,128)(2,1)}, u32[]{:S(2)}, u32[]{:S(2)}) collective-permute-start(bf16[288,2880]{1,0:T(8,128)(2,1)} %pad_maximum_fusion.5), channel_id=1, source_target_pairs={{0,1},{1,0},{2,3},{3,2},{4,5},{5,4},{6,7},{7,6},{8,9},{9,8},{10,11... | collective-permute-start | bytes 4976648 | tf_op jit(solution)/shard_map/ppermute | solution.py:217
  141.6 99.5 %collective-permute-start.14 = (bf16[288,2880]{1,0:T(8,128)(2,1)}, bf16[288,2880]{1,0:T(8,128)(2,1)}, u32[]{:S(2)}, u32[]{:S(2)}) collective-permute-start(bf16[288,2880]{1,0:T(8,128)(2,1)} %pad_maximum_fusion.5), channel_id=1, source_target_pairs={{0,2},{2,0},{4,6},{6,4},{8,10},{10,8},{12,14},{14,12},{16,18},{18,... | collective-permute-start | bytes 4976648 | tf_op jit(solution)/shard_map/ppermute | solution.py:223
  254.7 64.8 %collective-permute-start.30 = (bf16[288,2304]{1,0:T(8,128)(2,1)S(1)}, bf16[288,2304]{1,0:T(8,128)(2,1)}, u32[]{:S(2)}, u32[]{:S(2)}) collective-permute-start(bf16[288,2304]{1,0:T(8,128)(2,1)S(1)} %copy-done.7), channel_id=1, source_target_pairs={{0,4},{2,6},{4,0},{6,2},{8,12},{10,14},{12,8},{14,10},{16,20},{18,... | collective-permute-start | bytes 3981320 | tf_op jit(solution)/shard_map/ppermute | solution.py:220
  259.2 68.4 %collective-permute-start.31 = (bf16[288,2304]{1,0:T(8,128)(2,1)S(1)}, bf16[288,2304]{1,0:T(8,128)(2,1)}, u32[]{:S(2)}, u32[]{:S(2)}) collective-permute-start(bf16[288,2304]{1,0:T(8,128)(2,1)S(1)} %copy-done.7), channel_id=1, source_target_pairs={{0,2},{2,0},{4,6},{6,4},{8,10},{10,8},{12,14},{14,12},{16,18},{18,... | collective-permute-start | bytes 3981320 | tf_op jit(solution)/shard_map/ppermute | solution.py:223
  259.3 62.2 %collective-permute-start.33 = (bf16[288,2304]{1,0:T(8,128)(2,1)S(1)}, bf16[288,2304]{1,0:T(8,128)(2,1)}, u32[]{:S(2)}, u32[]{:S(2)}) collective-permute-start(bf16[288,2304]{1,0:T(8,128)(2,1)S(1)} %copy-done.7), channel_id=1, source_target_pairs={{0,1},{1,0},{2,3},{3,2},{4,5},{5,4},{6,7},{7,6},{8,9},{9,8},{10,11... | collective-permute-start | bytes 3981320 | tf_op jit(solution)/shard_map/ppermute | solution.py:217
  260.1 56.1 %collective-permute-start.39 = (bf16[576,1024]{1,0:T(8,128)(2,1)}, bf16[576,1024]{1,0:T(8,128)(2,1)}, u32[]{:S(2)}, u32[]{:S(2)}) collective-permute-start(bf16[576,1024]{1,0:T(8,128)(2,1)} %get-tuple-element.279), channel_id=1, source_target_pairs={{0,1},{1,0},{2,3},{3,2},{4,5},{5,4},{6,7},{7,6},{8,9},{9,8},{10,11... | collective-permute-start | bytes 3538952 | tf_op jit(solution)/shard_map/ppermute | solution.py:217
  381.1 34.2 %collective-permute-start.42 = (bf16[576,2304]{1,0:T(8,128)(2,1)}, bf16[576,2304]{1,0:T(8,128)(2,1)}, u32[]{:S(2)}, u32[]{:S(2)}) collective-permute-start(bf16[576,2304]{1,0:T(8,128)(2,1)} %convolution_convert_fusion.2), channel_id=1, source_target_pairs={{0,2},{2,0},{4,6},{6,4},{8,10},{10,8},{12,14},{14,12},{16,18},{18,... | collective-permute-start | bytes 7962632 | tf_op jit(solution)/shard_map/ppermute | solution.py:223
  381.2 40.3 %collective-permute-start.41 = (bf16[576,2304]{1,0:T(8,128)(2,1)}, bf16[576,2304]{1,0:T(8,128)(2,1)}, u32[]{:S(2)}, u32[]{:S(2)}) collective-permute-start(bf16[576,2304]{1,0:T(8,128)(2,1)} %convolution_convert_fusion.3), channel_id=1, source_target_pairs={{0,2},{2,0},{4,6},{6,4},{8,10},{10,8},{12,14},{14,12},{16,18},{18,... | collective-permute-start | bytes 7962632 | tf_op jit(solution)/shard_map/ppermute | solution.py:223
  459.7 38.2 %collective-permute-start.45 = (bf16[576,2304]{1,0:T(8,128)(2,1)S(1)}, bf16[576,2304]{1,0:T(8,128)(2,1)}, u32[]{:S(2)}, u32[]{:S(2)}) collective-permute-start(bf16[576,2304]{1,0:T(8,128)(2,1)S(1)} %copy-done.79), channel_id=1, source_target_pairs={{0,2},{2,0},{4,6},{6,4},{8,10},{10,8},{12,14},{14,12},{16,18},{18,... | collective-permute-start | bytes 7962632 | tf_op jit(solution)/shard_map/ppermute | solution.py:223
  544.0 45.7 %all-to-all-start.3 = ((bf16[16,8,2304]{2,1,0:T(8,128)(2,1)}), bf16[16,8,2304]{2,1,0:T(8,128)(2,1)S(1)}, u32[]{:S(2)}, u32[]{:S(2)}) async-start(bf16[16,8,2304]{2,1,0:T(8,128)(2,1)} %broadcast_in_dim.135), calls=%async_computation.3 | async-start | bytes 1179648 | tf_op jit(solution)/shard_map/all_to_all | solution.py:717
  566.1 87.2 %collective-permute-start.56 = (bf16[288,2304]{1,0:T(8,128)(2,1)}, bf16[288,2304]{1,0:T(8,128)(2,1)}, u32[]{:S(2)}, u32[]{:S(2)}) collective-permute-start(bf16[288,2304]{1,0:T(8,128)(2,1)} %pad_maximum_fusion.10), channel_id=1, source_target_pairs={{0,1},{1,0},{2,3},{3,2},{4,5},{5,4},{6,7},{7,6},{8,9},{9,8},{10,11... | collective-permute-start | bytes 3981320 | tf_op jit(solution)/shard_map/ppermute | solution.py:217
  567.3 86.1 %collective-permute-start.57 = (bf16[288,2304]{1,0:T(8,128)(2,1)}, bf16[288,2304]{1,0:T(8,128)(2,1)}, u32[]{:S(2)}, u32[]{:S(2)}) collective-permute-start(bf16[288,2304]{1,0:T(8,128)(2,1)} %pad_maximum_fusion.11), channel_id=1, source_target_pairs={{0,4},{2,6},{4,0},{6,2},{8,12},{10,14},{12,8},{14,10},{16,20},{18,... | collective-permute-start | bytes 3981320 | tf_op jit(solution)/shard_map/ppermute | solution.py:220
  687.7 45.5 %collective-permute-start.90 = (bf16[72,2304]{1,0:T(8,128)(2,1)}, bf16[72,2304]{1,0:T(8,128)(2,1)}, u32[]{:S(2)}, u32[]{:S(2)}) collective-permute-start(bf16[72,2304]{1,0:T(8,128)(2,1)} %add_convert_fusion.16), channel_id=1, source_target_pairs={{0,8},{2,10},{4,12},{6,14},{8,16},{10,18},{12,20},{14,22},{16,24},... | collective-permute-start | bytes 995336 | tf_op jit(solution)/shard_map/ppermute | solution.py:226
  691.9 64.0 %collective-permute-start.72 = (bf16[288,1728]{1,0:T(8,128)(2,1)}, bf16[288,1728]{1,0:T(8,128)(2,1)}, u32[]{:S(2)}, u32[]{:S(2)}) collective-permute-start(bf16[288,1728]{1,0:T(8,128)(2,1)} %pad_maximum_fusion.15), channel_id=1, source_target_pairs={{0,1},{1,0},{2,3},{3,2},{4,5},{5,4},{6,7},{7,6},{8,9},{9,8},{10,11... | collective-permute-start | bytes 2985992 | tf_op jit(solution)/shard_map/ppermute | solution.py:217
  692.7 63.2 %collective-permute-start.73 = (bf16[288,1728]{1,0:T(8,128)(2,1)}, bf16[288,1728]{1,0:T(8,128)(2,1)}, u32[]{:S(2)}, u32[]{:S(2)}) collective-permute-start(bf16[288,1728]{1,0:T(8,128)(2,1)} %pad_maximum_fusion.16), channel_id=1, source_target_pairs={{0,4},{2,6},{4,0},{6,2},{8,12},{10,14},{12,8},{14,10},{16,20},{18,... | collective-permute-start | bytes 2985992 | tf_op jit(solution)/shard_map/ppermute | solution.py:220
  709.1 58.0 %collective-permute-start.68 = (bf16[8,72,1024]{2,1,0:T(8,128)(2,1)}, bf16[8,72,1024]{2,1,0:T(8,128)(2,1)}, u32[]{:S(2)}, u32[]{:S(2)}) collective-permute-start(bf16[8,72,1024]{2,1,0:T(8,128)(2,1)} %get-tuple-element.172), channel_id=1, source_target_pairs={{0,1},{1,0},{2,3},{3,2},{4,5},{5,4},{6,7},{7,6},{8,9},{9,8},{10,11... | collective-permute-start | bytes 3538952 | tf_op jit(solution)/shard_map/ppermute | solution.py:217
  (186 other events, 2404.2 us)

commit v3 on v1

--- a/solution.py
+++ b/solution.py
@@ -23,6 +23,10 @@
     return lax.dot_general(
         left, right, (((dim_left,), (dim_right,)), ((), ())), preferred_element_type=F32
     )
+
+
+def fence(*trees):
+    return lax.optimization_barrier(trees)
 
 
 def gelu_tanh(values):
@@ -202,12 +206,11 @@
 
 def build(mesh):
     FS, T = mesh.shape["fsdp"], mesh.shape["tensor"]
-    staged = T == 2 and FS % 8 == 0 and (D // FS) % 8 == 0
+    staged = T == 2 and FS == 16
     Z = FS // 4
     swap_x = [(0, 1), (1, 0)]
     swap_y = [(i, i ^ 2) for i in range(FS)]
     swap_c = [(i, i ^ 1) for i in range(FS)]
-    ring_z = [(i, (i + 4) % FS) for i in range(FS)]
 
     def over_x(v):
         return lax.ppermute(v, "tensor", swap_x)
@@ -218,68 +221,107 @@
     def over_c(v):
         return lax.ppermute(v, "fsdp", swap_c)
 
-    def over_z(v):
-        return lax.ppermute(v, "fsdp", ring_z)
-
-    def gather_weights(piece):
+    def over_z(v, step):
+        return lax.ppermute(v, "fsdp", [(i, (i + 4 * step) % FS) for i in range(FS)])
+
+    def along_z(piece):
         if not staged:
-            whole = lax.all_gather(piece, "fsdp", axis=0, tiled=True)
-            whole = lax.all_gather(whole, "tensor", axis=0, tiled=False)
-            return [[whole[i]] for i in range(T)]
-        held = [piece]
-        for _ in range(Z - 1):
-            held.append(over_z(held[-1]))
-        base = jnp.concatenate(held, axis=0)
-        half = base.shape[0] // 2
-        side_x, side_y = over_x(base), over_y(base)
-        far_a = over_x(side_y[:half])
-        far_b = over_y(side_x[half:])
-        own = [base, side_y]
-        other = [side_x, far_a, far_b]
-        own = own + [over_c(v) for v in own]
-        other = other + [over_c(v) for v in other]
-        return [own, other]
-
-    def joined(parts, start, stop):
-        return jnp.concatenate([v[:, start:stop] for v in parts], axis=0)
-
-    def scatter_grads(left, rights):
-        if not staged:
-            local = jnp.stack([times(left, r, 1, 1).astype(BF16) for r in rights], axis=0)
-            part = lax.psum_scatter(local, "tensor", scatter_dimension=0, tiled=True)[0]
+            return piece
+        return jnp.concatenate([piece] + [over_z(piece, k) for k in range(1, Z)], axis=0)
+
+    class Gather:
+        def __init__(self, base):
+            self.base, self.near, self.far = base, (), ()
+
+        def first(self):
+            if staged:
+                self.near = (over_x(self.base), over_y(self.base))
+
+        def second(self):
+            if staged:
+                half = self.base.shape[0] // 2
+                side_x, side_y = self.near
+                self.far = (over_x(side_y[:half]), over_y(side_x[half:]))
+
+        def parts(self):
+            if not staged:
+                whole = lax.all_gather(self.base, "fsdp", axis=0, tiled=True)
+                whole = lax.all_gather(whole, "tensor", axis=0, tiled=False)
+                return [[whole[i]] for i in range(T)]
+            own = [self.base, self.near[1]]
+            other = [self.near[0], *self.far]
+            return [own + [over_c(v) for v in own], other + [over_c(v) for v in other]]
+
+    def from_all(values):
+        return lax.all_to_all(
+            jnp.broadcast_to(values[None], (FS, *values.shape)),
+            "fsdp",
+            split_axis=0,
+            concat_axis=0,
+            tiled=True,
+        )
+
+    class Scatter:
+        def __init__(self, left, rights):
+            self.left, self.rights, self.recv = left, rights, ()
+            start = D // 2 if staged else 0
+            self.local = [times(left[start:], r, 1, 1).astype(BF16) for r in rights]
+            if staged:
+                self.recv = [over_c(v) for v in self.local]
+
+        def core(self, left):
+            if not staged:
+                return
+            own, other = [
+                (times(left[: D // 2], r, 1, 1) + v.astype(F32)).astype(BF16)
+                for r, v in zip(self.rights, self.recv)
+            ]
+            quarter, half = D // 8, D // 4
+            self.local = [own, other]
+            self.recv = (
+                over_x(other[half : half + quarter]),
+                over_y(other[half + quarter :]),
+            )
+
+        def first(self):
+            if not staged:
+                return
+            own, other = self.local
+            quarter, half = D // 8, D // 4
+            from_x, from_y = self.recv
+            send_y = [
+                (own[half : half + quarter].astype(F32) + from_x.astype(F32)).astype(BF16),
+                own[half + quarter :],
+            ]
+            send_x = [
+                other[:quarter],
+                (other[quarter:half].astype(F32) + from_y.astype(F32)).astype(BF16),
+            ]
+            send_x, send_y = jnp.concatenate(send_x, axis=0), jnp.concatenate(send_y, axis=0)
+            self.recv = (over_x(send_x), over_y(send_y))
+            self.local = [own[:half], send_x, send_y]
+
+        def second(self):
+            if not staged:
+                return
+            base = self.local[0].astype(F32) + sum(v.astype(F32) for v in self.recv)
+            blocks = jnp.split(base, Z, axis=0)
+            rounded = [v.astype(BF16) for v in blocks[1:]]
+            self.recv = [over_z(rounded[k - 1], Z - k) for k in range(1, Z)]
+            self.local = [blocks[0], rounded]
+
+        def third(self):
+            if not staged:
+                return
+            self.local = [self.local[0] + sum(v.astype(F32) for v in self.recv)]
+
+        def done(self):
+            if staged:
+                return self.local[0]
+            part = lax.psum_scatter(
+                jnp.stack(self.local), "tensor", scatter_dimension=0, tiled=True
+            )[0]
             return lax.psum_scatter(part, "fsdp", scatter_dimension=0, tiled=True).astype(F32)
-        rows = D // 2
-        sent = [over_c(times(left[rows:], r, 1, 1).astype(BF16)) for r in rights]
-        own, other = [
-            (times(left[:rows], r, 1, 1) + s.astype(F32)).astype(BF16)
-            for r, s in zip(rights, sent)
-        ]
-        quarter, half = rows // 4, rows // 2
-        from_x = over_x(other[half : half + quarter]).astype(F32)
-        from_y = over_y(other[half + quarter :]).astype(F32)
-        send_y = jnp.concatenate(
-            [
-                (own[half : half + quarter].astype(F32) + from_x).astype(BF16),
-                own[half + quarter :],
-            ],
-            axis=0,
-        )
-        send_x = jnp.concatenate(
-            [
-                other[:quarter],
-                (other[quarter:half].astype(F32) + from_y).astype(BF16),
-            ],
-            axis=0,
-        )
-        base = own[:half].astype(F32) + over_x(send_x).astype(F32) + over_y(send_y).astype(F32)
-        blk = half // Z
-        moving = base[blk : 2 * blk].astype(BF16)
-        for k in range(2, Z + 1):
-            slot = k % Z
-            moving = over_z(moving).astype(F32) + base[slot * blk : (slot + 1) * blk]
-            if slot:
-                moving = moving.astype(BF16)
-        return moving
 
     def per_device(
         tokens,
@@ -322,12 +364,6 @@
             jnp.where(pick[None, :] == slot[:, None], slot[None, :], 0), axis=1
         )
 
-        attend_parts = gather_weights(attend_weight.reshape(rows_w, 3 * width))
-        second_parts = gather_weights(
-            jnp.concatenate([merge_weight.T, expand_weight], axis=1)
-        )
-        reduce_parts = gather_weights(reduce_weight.T)
-
         def spread(array):
             if not staged:
                 whole = lax.all_to_all(array, "tensor", split_axis=1, concat_axis=0, tiled=True)
@@ -349,13 +385,34 @@
 
         cond = condition.astype(F32)
         lifted = jax.nn.silu(cond).astype(BF16)
-        lifted_all = lax.all_gather(lifted, "fsdp", axis=0, tiled=True)
-        lifted_cols = lax.dynamic_slice(
-            lifted_all, (0, f * rows_w), (lifted_all.shape[0], rows_w)
-        )
+        lifted, attend_piece = fence(lifted, attend_weight.reshape(rows_w, 3 * width))
+        lifted_cols = lax.all_to_all(lifted, "fsdp", split_axis=1, concat_axis=0, tiled=True)
         mod_weight = modulation_weight.reshape(rows_w, 6 * width)
+        room = -3 * width % 128
+        attend_g = Gather(
+            along_z(
+                jnp.concatenate(
+                    [jnp.pad(attend_piece, ((0, 0), (0, room))), merge_weight.T], axis=1
+                )
+            )
+        )
         mod_part = times(lifted_cols, mod_weight, 1, 0)
-        mod_group = lax.psum_scatter(mod_part, "fsdp", scatter_dimension=0, tiled=True)
+        if staged:
+            held = mod_part.reshape(Z, 2, 2, group, 6 * width)
+            sent = over_c(jnp.where(c == 0, held[:, :, 1], held[:, :, 0]))
+            held = jnp.where(c == 0, held[:, :, 0], held[:, :, 1]) + sent
+            sent = over_y(jnp.where(y == 0, held[:, 1], held[:, 0]))
+            held = jnp.where(y == 0, held[:, 0], held[:, 1]) + sent
+            mod_group = lax.dynamic_index_in_dim(held, z, 0, keepdims=False)
+            for k in range(1, Z):
+                mod_group = mod_group + over_z(
+                    lax.dynamic_index_in_dim(held, (z + k) % Z, 0, keepdims=False), k
+                )
+        else:
+            mod_group = lax.psum_scatter(mod_part, "fsdp", scatter_dimension=0, tiled=True)
+        attend_g.first()
+        mod_group, expand_piece = fence(mod_group, expand_weight)
+        expand_g = Gather(along_z(expand_piece))
         mod_group = mod_group.reshape(group, 6, width) + modulation_bias.astype(F32)
         if staged:
             own = lax.dynamic_slice(mod_group, (t * images, 0, 0), (images, 6, width))
@@ -417,6 +474,8 @@
 
         tokens_all = spread(tokens)
         cot_all = spread(cotangent)
+        mod, attend_g.near = fence(mod, attend_g.near)
+        attend_g.second()
         residual, features_a, stats_a = pl.pallas_call(
             pre_kernel,
             name="pre",
@@ -437,9 +496,16 @@
             compiler_params=ARB,
             cost_estimate=cost(2 * D * tok * 384, 2 * act_bytes),
         )(pick, tokens_all, table, spots, mod)
-        features_a = features_a.reshape(D, tok)
-
-        attend_w = [joined(p, 0, 3 * width) for p in attend_parts]
+        features_a, reduce_piece, expand_g.base = fence(
+            features_a.reshape(D, tok), reduce_weight.T, expand_g.base
+        )
+        reduce_g = Gather(along_z(reduce_piece))
+        expand_g.first()
+
+        attend_parts = attend_g.parts()
+        attend_all = [jnp.concatenate(p, axis=0) for p in attend_parts]
+        attend_w = [v[:, : 3 * width] for v in attend_all]
+        merge_w = [v[:, 3 * width + room :] for v in attend_all]
         head_cube = (heads, HD, tok)
         qkv_spec = pl.BlockSpec((3, heads, HD, SLOTS), lambda i: (0, 0, 0, i))
         head_spec = pl.BlockSpec((heads, HD, SLOTS), lambda i: (0, 0, i))
@@ -465,9 +531,14 @@
             )(present, qkv[i])
             mixture.append(mix.reshape(width, tok))
             logs.append(log)
-        merge_w = [joined(p, 0, width) for p in second_parts]
+            if i == 0:
+                features_a, mixture, expand_g.near, reduce_g.base = fence(
+                    features_a, mixture, expand_g.near, reduce_g.base
+                )
+                expand_g.second()
         attended = merge_b + sum(times(merge_w[i], mixture[i], 1, 0) for i in range(T))
-        attended = attended.reshape(cube)
+        attended, expand_g.far = fence(attended.reshape(cube), expand_g.far)
+        reduce_g.first()
         middle, features_b, stats_b = pl.pallas_call(
             mid_kernel,
             name="mid",
@@ -484,10 +555,17 @@
         )(residual, attended, mod)
         features_b = features_b.reshape(D, tok)
 
-        expand_w = [joined(p, width, width + hidden) for p in second_parts]
-        expanded = [times(expand_w[i], features_b, 0, 0) + expand_b[i][:, None] for i in range(T)]
-        activated = [gelu_tanh(v).astype(BF16) for v in expanded]
-        reduce_w = [joined(p, 0, hidden) for p in reduce_parts]
+        expand_w = [jnp.concatenate(p, axis=0) for p in expand_g.parts()]
+        expanded, activated = [], []
+        for i in range(T):
+            expanded.append(times(expand_w[i], features_b, 0, 0) + expand_b[i][:, None])
+            activated.append(gelu_tanh(expanded[i]).astype(BF16))
+            if i == 0:
+                features_b, activated, reduce_g.near = fence(
+                    features_b, activated, reduce_g.near
+                )
+                reduce_g.second()
+        reduce_w = [jnp.concatenate(p, axis=0) for p in reduce_g.parts()]
         reduced = reduce_b + sum(times(reduce_w[i], activated[i], 1, 0) for i in range(T))
         kept_cube = (KB, blk, tok)
         other_specs = [kept_spec] if staged else []
@@ -499,7 +577,7 @@
             out_specs=[kept_spec, *other_specs, big, column_spec(2)],
             out_shape=[
                 jax.ShapeDtypeStruct(kept_cube, F32),
-                *[jax.ShapeDtypeStruct(kept_cube, F32) for _ in other_specs],
+                *[jax.ShapeDtypeStruct(kept_cube, BF16) for _ in other_specs],
                 jax.ShapeDtypeStruct(cube, BF16),
                 jax.ShapeDtypeStruct((images, D, 2), F32),
             ],
@@ -507,16 +585,29 @@
             compiler_params=ARB,
             cost_estimate=cost(10 * D * tok, 4 * act_bytes),
         )(pick, middle, reduced.reshape(cube), cot_all, mod)
-        output = collect(own_out, other_out[0] if staged else None)
         red_grad = red_grad.reshape(D, tok)
 
-        expand_grad = [
-            jax.vjp(gelu_tanh, expanded[i])[1](times(reduce_w[i], red_grad, 0, 0))[0].astype(BF16)
-            for i in range(T)
-        ]
-        reduce_wg = scatter_grads(red_grad, activated)
-        features_b_grad = sum(times(expand_w[i], expand_grad[i], 1, 0) for i in range(T))
-        expand_wg = scatter_grads(features_b, expand_grad)
+        def hidden_grad(i, upstream):
+            grad = times(reduce_w[i], upstream, 0, 0)
+            return jax.vjp(gelu_tanh, expanded[i])[1](grad)[0].astype(BF16)
+
+        reduce_s = Scatter(red_grad, activated)
+        upstream, reduce_s.local = fence(red_grad, reduce_s.local)
+        expand_grad = [hidden_grad(0, upstream)]
+        upstream, expand_grad = fence(upstream, expand_grad)
+        reduce_s.core(upstream)
+        upstream, reduce_s.local = fence(upstream, reduce_s.local)
+        expand_grad = expand_grad + [hidden_grad(i, upstream) for i in range(1, T)]
+        expand_grad, reduce_s.local = fence(expand_grad, reduce_s.local)
+        reduce_s.first()
+        expand_s = Scatter(features_b, expand_grad)
+        expand_back, expand_s.local, reduce_s.local = fence(
+            expand_grad, expand_s.local, reduce_s.local
+        )
+        features_b_grad = sum(times(expand_w[i], expand_back[i], 1, 0) for i in range(T))
+        features_b_grad, features_b = fence(features_b_grad, features_b)
+        expand_s.core(features_b)
+        features_b_grad, expand_s.local = fence(features_b_grad, expand_s.local)
         mid_grad, att_grad, cols_mid = pl.pallas_call(
             back_mid_kernel,
             name="back_mid",
@@ -533,9 +624,22 @@
         )(pick, features_b_grad.reshape(cube), middle, stats_b, mod, cot_all, attended)
         att_grad = att_grad.reshape(D, tok)
 
+        att_grad, expand_s.local, reduce_s.local, own_out = fence(
+            att_grad, expand_s.local, reduce_s.local, own_out
+        )
+        output = collect(own_out, other_out[0] if staged else None)
+        expand_s.first()
+        reduce_s.second()
+
+        merge_s = Scatter(att_grad, mixture)
+        mix_grad = [
+            times(merge_w[i], att_grad, 0, 0).astype(BF16).reshape(head_cube) for i in range(T)
+        ]
+        mix_grad, merge_s.local, expand_s.local, reduce_s.local = fence(
+            mix_grad, merge_s.local, expand_s.local, reduce_s.local
+        )
         qkv_grad = []
         for i in range(T):
-            mix_grad = times(merge_w[i], att_grad, 0, 0).astype(BF16).reshape(head_cube)
             grads = pl.pallas_call(
                 attend_back_kernel,
                 name="attend_back",
@@ -547,11 +651,37 @@
                 cost_estimate=cost(
                     20 * heads * tok * SLOTS * SLOTS, 16 * width * tok, heads * tok * SLOTS
                 ),
-            )(present, qkv[i], mix_grad, logs[i])
+            )(present, qkv[i], mix_grad[i], logs[i])
             qkv_grad.append(grads.reshape(3 * width, tok))
-        merge_wg = scatter_grads(att_grad, mixture)
-        attend_wg = scatter_grads(features_a, qkv_grad)
-        features_a_grad = sum(times(attend_w[i], qkv_grad[i], 1, 0) for i in range(T))
+            if i == 0:
+                qkv_grad, mix_grad, att_grad, reduce_s.local = fence(
+                    qkv_grad, mix_grad, att_grad, reduce_s.local
+                )
+                merge_s.core(att_grad)
+                reduce_s.third()
+                mix_grad, merge_s.local, reduce_s.local = fence(
+                    mix_grad, merge_s.local, reduce_s.local
+                )
+        qkv_grad, merge_s.local, expand_s.local = fence(qkv_grad, merge_s.local, expand_s.local)
+        attend_s = Scatter(features_a, qkv_grad)
+        merge_s.first()
+        expand_s.second()
+        qkv_back, attend_s.local, merge_s.local, expand_s.local = fence(
+            qkv_grad, attend_s.local, merge_s.local, expand_s.local
+        )
+        part = times(attend_w[0], qkv_back[0], 1, 0)
+        part, qkv_back, features_a = fence(part, qkv_back, features_a)
+        attend_s.core(features_a)
+        part, qkv_back, attend_s.local = fence(part, qkv_back, attend_s.local)
+        features_a_grad = part + sum(times(attend_w[i], qkv_back[i], 1, 0) for i in range(1, T))
+        features_a_grad, attend_s.local, merge_s.local = fence(
+            features_a_grad, attend_s.local, merge_s.local
+        )
+        attend_s.first()
+        merge_s.second()
+        features_a_grad, attend_s.local, merge_s.local = fence(
+            features_a_grad, attend_s.local, merge_s.local
+        )
         own_in, *other_in, cols_pre = pl.pallas_call(
             back_pre_kernel if staged else functools.partial(without_other, back_pre_kernel, 7),
             name="back_pre",
@@ -567,7 +697,13 @@
             compiler_params=ARB,
             cost_estimate=cost(20 * D * tok, 5 * act_bytes),
         )(pick, features_a_grad.reshape(cube), residual, stats_a, mod, mid_grad)
-        tokens_grad = collect(own_in, other_in[0] if staged else None)
+        cols_pre, attend_s.local = fence(cols_pre, attend_s.local)
+        attend_s.second()
+        merge_s.third()
+        expand_s.third()
+        attend_s.third()
+        reduce_wg, expand_wg = reduce_s.done(), expand_s.done()
+        merge_wg, attend_wg = merge_s.done(), attend_s.done()
 
         def own_first(values):
             lead = values.shape[:-1]
@@ -577,10 +713,10 @@
         def slot_sums(values):
             return jnp.sum(values.astype(F32), axis=1)
 
-        qkv_sums = [slot_sums(v) for v in qkv_grad]
-        hidden_sums = [slot_sums(v) for v in expand_grad]
         merge_sums = own_first(jnp.sum(cols_mid[:, :, 3], axis=0))
         reduce_sums = own_first(jnp.sum(cols_out[:, :, 1], axis=0))
+        hidden_sums = [slot_sums(v) for v in expand_grad]
+        qkv_sums = [slot_sums(v) for v in qkv_grad]
         bias_rows = [
             jnp.concatenate(
                 [
@@ -594,12 +730,16 @@
             for i in range(T)
         ]
         if staged:
-            bias_sum = bias_rows[0] + over_x(bias_rows[1])
+            bias_sum = jnp.sum(from_all(bias_rows[0] + over_x(bias_rows[1])), axis=0)
         else:
             bias_sum = lax.psum_scatter(
                 jnp.stack(bias_rows), "tensor", scatter_dimension=0, tiled=True
             )[0]
-        bias_sum = lax.psum(bias_sum, "fsdp")
+            bias_sum = lax.psum(bias_sum, "fsdp")
+        bounds = [0, 2 * width, 3 * width, 3 * width + hidden, 4 * width + hidden]
+        attend_bg, merge_bg, expand_bg, reduce_bg = [
+            bias_sum[a:b] for a, b in zip(bounds[:-1], bounds[1:])
+        ]
 
         mod_grad = jnp.stack(
             [
@@ -622,8 +762,9 @@
             mod_grad = lax.all_to_all(
                 mod_grad, "tensor", split_axis=2, concat_axis=0, tiled=True
             )
-        flat_grad = mod_grad.reshape(group, 6 * width)
-        flat_all = lax.all_gather(flat_grad, "fsdp", axis=0, tiled=True)
+        mod_grad, other_in = fence(mod_grad, other_in)
+        tokens_grad = collect(own_in, other_in[0] if staged else None)
+        flat_all = from_all(mod_grad.reshape(group, 6 * width)).reshape(FS * group, 6 * width)
         mod_wg = times(lifted_cols, flat_all, 0, 0).reshape(rows_w, 6, width)
         mod_bg = jnp.sum(flat_all.astype(F32), axis=0).reshape(6, width)
         lift_part = times(flat_all, mod_weight, 1, 1)
@@ -636,11 +777,6 @@
             lift_grad = lax.psum_scatter(lift_rows, "tensor", scatter_dimension=1, tiled=True)
         cond_here = lax.dynamic_slice(cond, (0, t * width), (group, width))
         cond_grad = jax.vjp(jax.nn.silu, cond_here)[1](lift_grad)[0]
-
-        bounds = [0, 2 * width, 3 * width, 3 * width + hidden, 4 * width + hidden]
-        attend_bg, merge_bg, expand_bg, reduce_bg = [
-            bias_sum[a:b] for a, b in zip(bounds[:-1], bounds[1:])
-        ]
         return (
             output,
             tokens_grad,

time: 994 us -> 756 us (0.76)
  waiting for transfers between devices: 310 us -> 164 us
  blocking collectives: 111 us -> 0 us
  starting transfers between devices: 56.6 us -> 109 us
  local copies, waits for them, and re-layouts: 111 us -> 92 us
  between operations: 17.3 us -> 2.78 us
    psum x1 -> x0, blocking collectives: 59.6 us -> none  [per_device(): bias_sum = lax.psum(bias_sum, 'fsdp')]
    all_gather x2 -> x0, blocking collectives: 51.8 us -> none  [the longest x1 31.5 us: per_device(): lifted_all = lax.all_gather(lifted, 'fsdp', axis=0, tiled=True)]
    unnamed x2 -> x0, waiting for transfers between devices: 50.3 us -> none
    ppermute x23, waiting for transfers between devices: 104 us -> 60.2 us  [over_x(): return lax.ppermute(v, 'tensor', swap_x)]
    ppermute x21 -> x24, starting transfers between devices: 6.6 us -> 47.2 us  [over_z(): lax.ppermute(v, 'fsdp', [(i, (i + 4 * step) % FS) for i in range(FS)])]
    ppermute x14 -> x15, waiting for transfers between devices: 60.9 us -> 29.3 us  [over_y(): return lax.ppermute(v, 'fsdp', swap_y)]
    ppermute x21 -> x24, waiting for transfers between devices: 87.7 us -> 59.6 us  [over_z(): lax.ppermute(v, 'fsdp', [(i, (i + 4 * step) % FS) for i in range(FS)])]
    slice x32 -> x31, local copies, waits for them, and re-layouts: 28.5 us -> 12.1 us  [the longest x6 8.44 us: second(): self.far = (over_x(side_y[:half]), over_y(side_x[half:]))]
  transfers between devices with their start and end apart: 83 -> 90, of which waited for: 31 -> 25; matrix products, arithmetic and copies ran while one was open for 21% -> 44% of each run, Pallas kernels for 4% -> 13%
where the time goes in v3:
time: 756 us; the launch traced here: 752 us
  matrix products  206 us (27%)
  waiting for transfers between devices  164 us (22%)
  starting transfers between devices  109 us (14%)
  Pallas kernels  108 us (14%)
  local copies, waits for them, and re-layouts  92 us (12%)
  other arithmetic  70.1 us (9%)
    dot_general x35, matrix products, times(): lax.dot_general(left, right, (((dim_left,), (dim_right,)), ((), ())), pre...  206 us
    ppermute x23, waiting for transfers between devices, over_x(): return lax.ppermute(v, 'tensor', swap_x)  60.2 us
    ppermute x24, waiting for transfers between devices, over_z(): lax.ppermute(v, 'fsdp', [(i, (i + 4 * step) % FS) for i in range(FS)])  59.6 us
    ppermute x24, starting transfers between devices, over_z(): lax.ppermute(v, 'fsdp', [(i, (i + 4 * step) % FS) for i in range(FS)])  47.2 us
    unnamed x186, local copies, waits for them, and re-layouts  37.1 us
    ppermute x15, waiting for transfers between devices, over_y(): return lax.ppermute(v, 'fsdp', swap_y)  29.3 us
    pallas_call x2, Pallas kernels, per_device(): pl.pallas_call(attend_back_kernel, name='attend_back', grid=(images,), in...  28.6 us
    pallas_call x2, Pallas kernels, per_device(): pl.pallas_call(attend_kernel, name='attend', grid=(images,), in_specs=[sm...  25.5 us
  transfers between devices with their start and end apart: 90, of which 25 were waited for; matrix products, arithmetic and copies ran while one was open for 44% of the time, Pallas kernels for 13%

profile of v3, /device:TPU:0, one launch (start us, length us, event | category | flops | bytes accessed | tf_op | source)
XLA Modules:
  0.0 751.9 jit_solution(8141516244415517388)
XLA Ops:
  55.8 8.4 %collective-permute-done.2 = f32[4,8,3456]{2,1,0:T(8,128)S(1)} collective-permute-done((f32[4,8,3456]{2,1,0:T(8,128)S(1)}, f32[4,8,3456]{2,1,0:T(8,128)S(1)}, u32[]{:S(2)}, u32[]{:S(2)}) %collective-permute-start.2) | collective-permute-done | bytes 442400 | tf_op jit(solution)/shard_map/ppermute | solution.py:219
  83.9 22.8 %collective-permute-done.6 = f32[4,6,576]{2,1,0:T(8,128)S(1)} collective-permute-done((f32[4,6,576]{2,1,0:T(8,128)S(1)}, f32[4,6,576]{2,1,0:T(8,128)S(1)}, u32[]{:S(2)}, u32[]{:S(2)}) %collective-permute-start.6) | collective-permute-done | bytes 55328 | tf_op jit(solution)/shard_map/ppermute | solution.py:216
  113.0 12.0 %collective-permute-start.12 = (bf16[72,2304]{1,0:T(8,128)(2,1)}, bf16[72,2304]{1,0:T(8,128)(2,1)S(1)}, u32[]{:S(2)}, u32[]{:S(2)}) collective-permute-start(bf16[72,2304]{1,0:T(8,128)(2,1)} %param.26), channel_id=1, source_target_pairs={{0,8},{2,10},{4,12},{6,14},{8,16},{10,18},{12,20},{14,22},{16,24},... | collective-permute-start | bytes 995336 | tf_op jit(solution)/shard_map/ppermute | solution.py:225
  128.2 7.6 %pre.1 = (f32[16,72,1024]{2,1,0:T(8,128)}, bf16[16,72,1024]{2,1,0:T(8,128)(2,1)}, f32[8,1024]{1,0:T(8,128)}) custom-call(s32[16]{0:T(128)} %copy-done.39, bf16[16,72,1024]{2,1,0:T(8,128)(2,1)} %bitcast.174, bf16[16,72,384]{2,1,0:T(8,128)(2,1)} %pad_maximum_fusion.14.table, s32[4,8,256]{2,1,0:T(8,128)} %pad.12.spots, f32[4,1152,8]{2,1,0:T(8,128)} %pad.13.mod), custom_call_target="tpu_custom_call" | custom-call | flops 905969664 | bytes 9437184 | tf_op jit(solution)/shard_map/pre/pallas_call | solution.py:479
  155.4 19.7 %collective-permute-done.21 = bf16[72,2304]{1,0:T(8,128)(2,1)S(1)} collective-permute-done((bf16[72,2304]{1,0:T(8,128)(2,1)S(1)}, bf16[72,2304]{1,0:T(8,128)(2,1)S(1)}, u32[]{:S(2)}, u32[]{:S(2)}) %collective-permute-start.21) | collective-permute-done | bytes 331808 | tf_op jit(solution)/shard_map/ppermute | solution.py:225
  177.5 16.3 %collective-permute-done.26 = bf16[144,2368]{1,0:T(8,128)(2,1)S(1)} collective-permute-done((bf16[144,2368]{1,0:T(8,128)(2,1)S(1)}, bf16[144,2368]{1,0:T(8,128)(2,1)S(1)}, u32[]{:S(2)}, u32[]{:S(2)}) %collective-permute-start.26) | collective-permute-done | bytes 682016 | tf_op jit(solution)/shard_map/ppermute | solution.py:219
  208.1 12.7 %attend.2 = (bf16[8,72,1024]{2,1,0:T(8,128)(2,1)}, f32[8,1024]{1,0:T(8,128)}) custom-call(s32[4]{0:T(128)} %bitcast_multiply_fusion.present, bf16[3,8,72,1024]{3,2,1,0:T(8,128)(2,1)} %bitcast.244), custom_call_target="tpu_custom_call" | custom-call | flops 4294967296 | bytes 4718592 | tf_op jit(solution)/shard_map/attend/pallas_call | solution.py:517
  232.8 8.4 %add_convert_fusion = bf16[1728,1024]{1,0:T(8,128)(2,1)} fusion(bf16[1152,1024]{1,0:T(8,128)(2,1)S(1)} %bitcast.227, bf16[1152,2368]{1,0:T(8,128)(2,1)} %copy-done.25, f32[1728]{0:T(1024)S(1)} %get-tuple-element.307), kind=kOutput, calls=%fused_computation.30 | convolution fusion | flops 4080402432 | bytes 10033920 | tf_op jit(solution)/shard_map/dot_general | solution.py:23
  246.2 12.8 %attend.3 = (bf16[8,72,1024]{2,1,0:T(8,128)(2,1)}, f32[8,1024]{1,0:T(8,128)}) custom-call(s32[4]{0:T(128)} %bitcast_multiply_fusion.present, bf16[3,8,72,1024]{3,2,1,0:T(8,128)(2,1)} %bitcast.242), custom_call_target="tpu_custom_call" | custom-call | flops 4294967296 | bytes 4718592 | tf_op jit(solution)/shard_map/attend/pallas_call | solution.py:517
  281.4 7.9 %mid.1 = (f32[16,72,1024]{2,1,0:T(8,128)}, bf16[16,72,1024]{2,1,0:T(8,128)(2,1)}, f32[8,1024]{1,0:T(8,128)}) custom-call(f32[16,72,1024]{2,1,0:T(8,128)} %get-tuple-element.130.res, f32[16,72,1024]{2,1,0:T(8,128)} %bitcast.171, f32[4,1152,8]{2,1,0:T(8,128)} %pad.13.mod), custom_call_target="tpu_custom_call" | custom-call | flops 11796480 | bytes 18874368 | tf_op jit(solution)/shard_map/mid/pallas_call | solution.py:542
  294.8 13.1 %multiply_convert_fusion.1 = (bf16[2304,1024]{1,0:T(8,128)(2,1)S(1)}, f32[2304,1024]{1,0:T(8,128)}) fusion(f32[2304]{0:T(1024)S(1)} %get-tuple-element.306, bf16[1152,2304]{1,0:T(8,128)(2,1)} %constant_dynamic-update-slice_fusion.7, bf16[1152,1024]{1,0:T(8,128)(2,1)S(1)} %bitcast.230), kind=kOutput, calls=%fused_computation.27 | convolution fusion | flops 5459410944 | bytes 21832704 | tf_op jit(solution)/shard_map/dot_general | solution.py:23
  316.0 11.8 %multiply_convert_fusion = (bf16[2304,1024]{1,0:T(8,128)(2,1)}, f32[2304,1024]{1,0:T(8,128)}) fusion(f32[2304]{0:T(1024)S(1)} %get-tuple-element.305, bf16[1152,2304]{1,0:T(8,128)(2,1)S(1)} %constant_dynamic-update-slice_fusion.27, bf16[1152,1024]{1,0:T(8,128)(2,1)S(1)} %bitcast.231), kind=kOutput, calls=%fused_computation.26 | convolution fusion | flops 5459410944 | bytes 21832704 | tf_op jit(solution)/shard_map/dot_general | solution.py:23
  344.8 13.5 %out.1 = (f32[8,72,1024]{2,1,0:T(8,128)}, bf16[8,72,1024]{2,1,0:T(8,128)(2,1)}, bf16[16,72,1024]{2,1,0:T(8,128)(2,1)}, f32[4,1152,2]{2,1,0:T(8,128)}) custom-call(s32[16]{0:T(128)} %copy-done.39, f32[16,72,1024]{2,1,0:T(8,128)} %get-tuple-element.137.mid, f32[16,72,1024]{2,1,0:T(8,128)} %bitcast.184, bf16[16,72,1024]{2,1,0:T(8,128)(2,1)} %bitcast.169, ...), custom_call_target="tpu_custom_call" | custom-call | flops 11796480 | bytes 18874368 | tf_op jit(solution)/shard_map/out/pallas_call | solution.py:572
  376.9 17.3 %fusion.6 = bf16[2304,1024]{1,0:T(8,128)(2,1)} fusion(f32[2304,1024]{1,0:T(8,128)} %get-tuple-element.387, f32[2304]{0:T(1024)S(1)} %get-tuple-element.306, bf16[1152,2304]{1,0:T(8,128)(2,1)} %copy-done.26, bf16[1152,1024]{1,0:T(8,128)(2,1)S(1)} %bitcast.198), kind=kOutput, calls=%fused_computation.16 | convolution fusion | flops 5485363200 | bytes 21832704 | tf_op jit(solution)/shard_map/dot_general | solution.py:23
  408.1 14.6 %fusion.13 = bf16[2304,1024]{1,0:T(8,128)(2,1)S(1)} fusion(f32[2304,1024]{1,0:T(8,128)} %get-tuple-element.389, f32[2304]{0:T(1024)S(1)} %get-tuple-element.305, bf16[1152,2304]{1,0:T(8,128)(2,1)S(1)} %bitcast.214, bf16[1152,1024]{1,0:T(8,128)(2,1)S(1)} %bitcast.201), kind=kOutput, calls=%fused_computation.23 | convolution fusion | flops 5485363200 | bytes 21832704 | tf_op jit(solution)/shard_map/dot_general | solution.py:23
  450.6 9.2 %convolution_add_fusion.1 = f32[1152,1024]{1,0:T(8,128)} fusion(f32[1152,1024]{1,0:T(8,128)S(1)} %fusion.130, bf16[1152,2304]{1,0:T(8,128)(2,1)} %constant_dynamic-update-slice_fusion.7, bf16[2304,1024]{1,0:T(8,128)(2,1)S(1)} %bitcast.182), kind=kOutput, calls=%fused_computation.45 | convolution fusion | flops 5436997632 | bytes 19464192 | tf_op jit(solution)/shard_map/dot_general | solution.py:23
  471.1 14.6 %back_mid.1 = (f32[16,72,1024]{2,1,0:T(8,128)}, bf16[16,72,1024]{2,1,0:T(8,128)(2,1)}, f32[4,1152,4]{2,1,0:T(8,128)}) custom-call(s32[16]{0:T(128)} %copy-done.39, f32[16,72,1024]{2,1,0:T(8,128)} %bitcast.183, f32[16,72,1024]{2,1,0:T(8,128)} %get-tuple-element.137.mid, f32[8,1024]{1,0:T(8,128)} %get-tuple-element.162.stats, f32[4,1152,8]{2,1,0:T(8,128)} %pad.13.mod, ...), custom_call_target="tpu_custom_call" | custom-call | flops 23592960 | bytes 23592960 | tf_op jit(solution)/shard_map/back_mid/pallas_call | solution.py:611
  529.0 14.3 %attend_back.2 = bf16[3,8,72,1024]{3,2,1,0:T(8,128)(2,1)} custom-call(s32[4]{0:T(128)} %bitcast_multiply_fusion.present, bf16[3,8,72,1024]{3,2,1,0:T(8,128)(2,1)} %bitcast.245, bf16[8,72,1024]{2,1,0:T(8,128)(2,1)} %bitcast.253, f32[8,1024]{1,0:T(8,128)} %get-tuple-element.175.logs), custom_call_target="tpu_custom_call" | custom-call | flops 10737418240 | bytes 9437184 | tf_op jit(solution)/shard_map/attend_back/pallas_call | solution.py:643
  555.8 14.3 %attend_back.3 = bf16[3,8,72,1024]{3,2,1,0:T(8,128)(2,1)} custom-call(s32[4]{0:T(128)} %bitcast_multiply_fusion.present, bf16[3,8,72,1024]{3,2,1,0:T(8,128)(2,1)} %bitcast.243, bf16[8,72,1024]{2,1,0:T(8,128)(2,1)} %bitcast.252, f32[8,1024]{1,0:T(8,128)} %get-tuple-element.183.logs), custom_call_target="tpu_custom_call" | custom-call | flops 10737418240 | bytes 9437184 | tf_op jit(solution)/shard_map/attend_back/pallas_call | solution.py:643
  639.6 10.2 %collective-permute-done.68 = bf16[144,1728]{1,0:T(8,128)(2,1)S(1)} collective-permute-done((bf16[144,1728]{1,0:T(8,128)(2,1)S(1)}, bf16[144,1728]{1,0:T(8,128)(2,1)S(1)}, u32[]{:S(2)}, u32[]{:S(2)}) %collective-permute-start.68) | collective-permute-done | bytes 497696 | tf_op jit(solution)/shard_map/ppermute | solution.py:216
  654.4 10.2 %back_pre.1 = (f32[8,72,1024]{2,1,0:T(8,128)}, bf16[8,72,1024]{2,1,0:T(8,128)(2,1)}, f32[4,1152,2]{2,1,0:T(8,128)}) custom-call(s32[16]{0:T(128)} %copy-done.39, f32[16,72,1024]{2,1,0:T(8,128)} %bitcast.180, f32[16,72,1024]{2,1,0:T(8,128)} %get-tuple-element.130.res, f32[8,1024]{1,0:T(8,128)} %get-tuple-element.207.stats, f32[4,1152,8]{2,1,0:T(8,128)} %pad.13.mod, ...), custom_call_target="tpu_custom_call" | custom-call | flops 23592960 | bytes 23592960 | tf_op jit(solution)/shard_map/back_pre/pallas_call | solution.py:685
  695.8 8.7 %collective-permute-done.72 = bf16[8,72,1024]{2,1,0:T(8,128)(2,1)S(1)} collective-permute-done((bf16[8,72,1024]{2,1,0:T(8,128)(2,1)}, bf16[8,72,1024]{2,1,0:T(8,128)(2,1)S(1)}, u32[]{:S(2)}, u32[]{:S(2)}) %collective-permute-start.72) | collective-permute-done | bytes 1179680 | tf_op jit(solution)/shard_map/ppermute | solution.py:216
  711.6 8.1 %collective-permute-done.78 = bf16[72,1728]{1,0:T(8,128)(2,1)S(1)} collective-permute-done((bf16[72,1728]{1,0:T(8,128)(2,1)S(1)}, bf16[72,1728]{1,0:T(8,128)(2,1)S(1)}, u32[]{:S(2)}, u32[]{:S(2)}) %collective-permute-start.78) | collective-permute-done | bytes 248864 | tf_op jit(solution)/shard_map/ppermute | solution.py:225
  719.8 14.2 %collective-permute-done.77 = bf16[72,1728]{1,0:T(8,128)(2,1)S(1)} collective-permute-done((bf16[72,1728]{1,0:T(8,128)(2,1)S(1)}, bf16[72,1728]{1,0:T(8,128)(2,1)S(1)}, u32[]{:S(2)}, u32[]{:S(2)}) %collective-permute-start.77) | collective-permute-done | bytes 248864 | tf_op jit(solution)/shard_map/ppermute | solution.py:225
  (607 shorter events, 446.3 us)
Async XLA Ops:
  21.2 47.0 %collective-permute-start = (bf16[576,1024]{1,0:T(8,128)(2,1)}, bf16[576,1024]{1,0:T(8,128)(2,1)}, u32[]{:S(2)}, u32[]{:S(2)}) collective-permute-start(bf16[576,1024]{1,0:T(8,128)(2,1)} %get-tuple-element.330), channel_id=1, source_target_pairs={{0,1},{1,0},{2,3},{3,2},{4,5},{5,4},{6,7},{7,6},{8,9},{9,8},{10,11... | collective-permute-start | bytes 3538952 | tf_op jit(solution)/shard_map/ppermute | solution.py:216
  48.3 91.5 %collective-permute-start.15 = (bf16[288,2368]{1,0:T(8,128)(2,1)}, bf16[288,2368]{1,0:T(8,128)(2,1)}, u32[]{:S(2)}, u32[]{:S(2)}) collective-permute-start(bf16[288,2368]{1,0:T(8,128)(2,1)} %pad_maximum_fusion.4), channel_id=1, source_target_pairs={{0,2},{2,0},{4,6},{6,4},{8,10},{10,8},{12,14},{14,12},{16,18},{18,... | collective-permute-start | bytes 4091912 | tf_op jit(solution)/shard_map/ppermute | solution.py:222
  73.1 51.9 %collective-permute-start.10 = (bf16[288,2368]{1,0:T(8,128)(2,1)}, bf16[288,2368]{1,0:T(8,128)(2,1)}, u32[]{:S(2)}, u32[]{:S(2)}) collective-permute-start(bf16[288,2368]{1,0:T(8,128)(2,1)} %pad_maximum_fusion.4), channel_id=1, source_target_pairs={{0,1},{1,0},{2,3},{3,2},{4,5},{5,4},{6,7},{7,6},{8,9},{9,8},{10,11... | collective-permute-start | bytes 4091912 | tf_op jit(solution)/shard_map/ppermute | solution.py:216
  82.0 60.9 %collective-permute-start.14 = (bf16[72,2304]{1,0:T(8,128)(2,1)}, bf16[72,2304]{1,0:T(8,128)(2,1)}, u32[]{:S(2)}, u32[]{:S(2)}) collective-permute-start(bf16[72,2304]{1,0:T(8,128)(2,1)} %param.26), channel_id=1, source_target_pairs={{0,24},{2,26},{4,28},{6,30},{8,0},{10,2},{12,4},{14,6},{16,8},{18,... | collective-permute-start | bytes 995336 | tf_op jit(solution)/shard_map/ppermute | solution.py:225
  126.1 67.7 %collective-permute-start.27 = (bf16[288,2368]{1,0:T(8,128)(2,1)}, bf16[288,2368]{1,0:T(8,128)(2,1)}, u32[]{:S(2)}, u32[]{:S(2)}) collective-permute-start(bf16[288,2368]{1,0:T(8,128)(2,1)} %collective-permute-done.10), channel_id=1, source_target_pairs={{0,2},{2,0},{4,6},{6,4},{8,10},{10,8},{12,14},{14,12},{16,18},{18,... | collective-permute-start | bytes 4091912 | tf_op jit(solution)/shard_map/ppermute | solution.py:222
  155.4 41.9 %collective-permute-start.16 = (bf16[288,2368]{1,0:T(8,128)(2,1)}, bf16[288,2368]{1,0:T(8,128)(2,1)S(1)}, u32[]{:S(2)}, u32[]{:S(2)}) collective-permute-start(bf16[288,2368]{1,0:T(8,128)(2,1)} %collective-permute-done.11), channel_id=1, source_target_pairs={{0,2},{2,0},{4,6},{6,4},{8,10},{10,8},{12,14},{14,12},{16,18},{18,... | collective-permute-start | bytes 4091912 | tf_op jit(solution)/shard_map/ppermute | solution.py:222
  176.6 86.1 %collective-permute-start.23 = (bf16[288,2304]{1,0:T(8,128)(2,1)S(1)}, bf16[288,2304]{1,0:T(8,128)(2,1)}, u32[]{:S(2)}, u32[]{:S(2)}) collective-permute-start(bf16[288,2304]{1,0:T(8,128)(2,1)S(1)} %pad_maximum_fusion.5), channel_id=1, source_target_pairs={{0,2},{2,0},{4,6},{6,4},{8,10},{10,8},{12,14},{14,12},{16,18},{18,... | collective-permute-start | bytes 3981320 | tf_op jit(solution)/shard_map/ppermute | solution.py:222
  176.7 44.2 %collective-permute-start.19 = (bf16[288,2304]{1,0:T(8,128)(2,1)S(1)}, bf16[288,2304]{1,0:T(8,128)(2,1)}, u32[]{:S(2)}, u32[]{:S(2)}) collective-permute-start(bf16[288,2304]{1,0:T(8,128)(2,1)S(1)} %pad_maximum_fusion.5), channel_id=1, source_target_pairs={{0,4},{2,6},{4,0},{6,2},{8,12},{10,14},{12,8},{14,10},{16,20},{18,... | collective-permute-start | bytes 3981320 | tf_op jit(solution)/shard_map/ppermute | solution.py:219
  227.7 64.7 %collective-permute-start.24 = (bf16[288,2304]{1,0:T(8,128)(2,1)}, bf16[288,2304]{1,0:T(8,128)(2,1)}, u32[]{:S(2)}, u32[]{:S(2)}) collective-permute-start(bf16[288,2304]{1,0:T(8,128)(2,1)} %collective-permute-done.19), channel_id=1, source_target_pairs={{0,2},{2,0},{4,6},{6,4},{8,10},{10,8},{12,14},{14,12},{16,18},{18,... | collective-permute-start | bytes 3981320 | tf_op jit(solution)/shard_map/ppermute | solution.py:222
  229.6 82.0 %collective-permute-start.41 = (bf16[288,2304]{1,0:T(8,128)(2,1)}, bf16[288,2304]{1,0:T(8,128)(2,1)}, u32[]{:S(2)}, u32[]{:S(2)}) collective-permute-start(bf16[288,2304]{1,0:T(8,128)(2,1)} %collective-permute-done.18), channel_id=1, source_target_pairs={{0,2},{2,0},{4,6},{6,4},{8,10},{10,8},{12,14},{14,12},{16,18},{18,... | collective-permute-start | bytes 3981320 | tf_op jit(solution)/shard_map/ppermute | solution.py:222
  230.1 99.2 %collective-permute-start.34 = (bf16[288,2304]{1,0:T(8,128)(2,1)S(1)}, bf16[288,2304]{1,0:T(8,128)(2,1)}, u32[]{:S(2)}, u32[]{:S(2)}) collective-permute-start(bf16[288,2304]{1,0:T(8,128)(2,1)S(1)} %pad_maximum_fusion.6), channel_id=1, source_target_pairs={{0,2},{2,0},{4,6},{6,4},{8,10},{10,8},{12,14},{14,12},{16,18},{18,... | collective-permute-start | bytes 3981320 | tf_op jit(solution)/shard_map/ppermute | solution.py:222
  231.3 41.2 %collective-permute-start.31 = (bf16[144,2304]{1,0:T(8,128)(2,1)}, bf16[144,2304]{1,0:T(8,128)(2,1)S(1)}, u32[]{:S(2)}, u32[]{:S(2)}) collective-permute-start(bf16[144,2304]{1,0:T(8,128)(2,1)} %slice.305), channel_id=1, source_target_pairs={{0,4},{2,6},{4,0},{6,2},{8,12},{10,14},{12,8},{14,10},{16,20},{18,... | collective-permute-start | bytes 1990664 | tf_op jit(solution)/shard_map/ppermute | solution.py:219
  375.1 136.4 %collective-permute-start.51 = (bf16[8,72,1024]{2,1,0:T(8,128)(2,1)}, bf16[8,72,1024]{2,1,0:T(8,128)(2,1)}, u32[]{:S(2)}, u32[]{:S(2)}) collective-permute-start(bf16[8,72,1024]{2,1,0:T(8,128)(2,1)} %get-tuple-element.169), channel_id=1, source_target_pairs={{0,1},{1,0},{2,3},{3,2},{4,5},{5,4},{6,7},{7,6},{8,9},{9,8},{10,11... | collective-permute-start | bytes 3538952 | tf_op jit(solution)/shard_map/ppermute | solution.py:216
  440.6 62.0 %collective-permute-start.54 = (bf16[288,2304]{1,0:T(8,128)(2,1)S(1)}, bf16[288,2304]{1,0:T(8,128)(2,1)}, u32[]{:S(2)}, u32[]{:S(2)}) collective-permute-start(bf16[288,2304]{1,0:T(8,128)(2,1)S(1)} %pad_maximum_fusion.7), channel_id=1, source_target_pairs={{0,1},{1,0},{2,3},{3,2},{4,5},{5,4},{6,7},{7,6},{8,9},{9,8},{10,11... | collective-permute-start | bytes 3981320 | tf_op jit(solution)/shard_map/ppermute | solution.py:216
  443.3 59.3 %collective-permute-start.55 = (bf16[288,2304]{1,0:T(8,128)(2,1)}, bf16[288,2304]{1,0:T(8,128)(2,1)}, u32[]{:S(2)}, u32[]{:S(2)}) collective-permute-start(bf16[288,2304]{1,0:T(8,128)(2,1)} %pad_maximum_fusion.8), channel_id=1, source_target_pairs={{0,4},{2,6},{4,0},{6,2},{8,12},{10,14},{12,8},{14,10},{16,20},{18,... | collective-permute-start | bytes 3981320 | tf_op jit(solution)/shard_map/ppermute | solution.py:219
  502.6 46.6 %collective-permute-start.56 = (bf16[576,576]{1,0:T(8,128)(2,1)}, bf16[576,576]{1,0:T(8,128)(2,1)}, u32[]{:S(2)}, u32[]{:S(2)}) collective-permute-start(bf16[576,576]{1,0:T(8,128)(2,1)} %convolution_convert_fusion.9), channel_id=1, source_target_pairs={{0,2},{2,0},{4,6},{6,4},{8,10},{10,8},{12,14},{14,12},{16,18},{18,... | collective-permute-start | bytes 1990664 | tf_op jit(solution)/shard_map/ppermute | solution.py:222
  502.6 40.8 %collective-permute-start.57 = (bf16[576,576]{1,0:T(8,128)(2,1)}, bf16[576,576]{1,0:T(8,128)(2,1)}, u32[]{:S(2)}, u32[]{:S(2)}) collective-permute-start(bf16[576,576]{1,0:T(8,128)(2,1)} %convolution_convert_fusion.8), channel_id=1, source_target_pairs={{0,2},{2,0},{4,6},{6,4},{8,10},{10,8},{12,14},{14,12},{16,18},{18,... | collective-permute-start | bytes 1990664 | tf_op jit(solution)/shard_map/ppermute | solution.py:222
  511.5 42.2 %collective-permute-start.60 = (bf16[72,2304]{1,0:T(8,128)(2,1)}, bf16[72,2304]{1,0:T(8,128)(2,1)}, u32[]{:S(2)}, u32[]{:S(2)}) collective-permute-start(bf16[72,2304]{1,0:T(8,128)(2,1)} %get-tuple-element.336), channel_id=1, source_target_pairs={{0,8},{2,10},{4,12},{6,14},{8,16},{10,18},{12,20},{14,22},{16,24},... | collective-permute-start | bytes 995336 | tf_op jit(solution)/shard_map/ppermute | solution.py:225
  543.4 64.6 %collective-permute-start.64 = (bf16[288,2304]{1,0:T(8,128)(2,1)}, bf16[288,2304]{1,0:T(8,128)(2,1)}, u32[]{:S(2)}, u32[]{:S(2)}) collective-permute-start(bf16[288,2304]{1,0:T(8,128)(2,1)} %pad_maximum_fusion.10), channel_id=1, source_target_pairs={{0,4},{2,6},{4,0},{6,2},{8,12},{10,14},{12,8},{14,10},{16,20},{18,... | collective-permute-start | bytes 3981320 | tf_op jit(solution)/shard_map/ppermute | solution.py:219
  549.2 58.8 %collective-permute-start.63 = (bf16[288,2304]{1,0:T(8,128)(2,1)}, bf16[288,2304]{1,0:T(8,128)(2,1)}, u32[]{:S(2)}, u32[]{:S(2)}) collective-permute-start(bf16[288,2304]{1,0:T(8,128)(2,1)} %pad_maximum_fusion.9), channel_id=1, source_target_pairs={{0,1},{1,0},{2,3},{3,2},{4,5},{5,4},{6,7},{7,6},{8,9},{9,8},{10,11... | collective-permute-start | bytes 3981320 | tf_op jit(solution)/shard_map/ppermute | solution.py:216
  611.3 57.9 %collective-permute-start.85 = (bf16[72,2304]{1,0:T(8,128)(2,1)}, bf16[72,2304]{1,0:T(8,128)(2,1)}, u32[]{:S(2)}, u32[]{:S(2)}) collective-permute-start(bf16[72,2304]{1,0:T(8,128)(2,1)} %get-tuple-element.333), channel_id=1, source_target_pairs={{0,8},{2,10},{4,12},{6,14},{8,16},{10,18},{12,20},{14,22},{16,24},... | collective-permute-start | bytes 995336 | tf_op jit(solution)/shard_map/ppermute | solution.py:225
  619.0 51.6 %collective-permute-start.84 = (bf16[72,2304]{1,0:T(8,128)(2,1)}, bf16[72,2304]{1,0:T(8,128)(2,1)}, u32[]{:S(2)}, u32[]{:S(2)}) collective-permute-start(bf16[72,2304]{1,0:T(8,128)(2,1)} %get-tuple-element.334), channel_id=1, source_target_pairs={{0,16},{2,18},{4,20},{6,22},{8,24},{10,26},{12,28},{14,30},{16,0},... | collective-permute-start | bytes 995336 | tf_op jit(solution)/shard_map/ppermute | solution.py:225
  624.7 45.9 %collective-permute-start.83 = (bf16[72,2304]{1,0:T(8,128)(2,1)}, bf16[72,2304]{1,0:T(8,128)(2,1)}, u32[]{:S(2)}, u32[]{:S(2)}) collective-permute-start(bf16[72,2304]{1,0:T(8,128)(2,1)} %get-tuple-element.335), channel_id=1, source_target_pairs={{0,24},{2,26},{4,28},{6,30},{8,0},{10,2},{12,4},{14,6},{16,8},{18,... | collective-permute-start | bytes 995336 | tf_op jit(solution)/shard_map/ppermute | solution.py:225
  683.9 51.3 %all-to-all-start.1 = ((bf16[16,8,3456]{2,1,0:T(8,128)(2,1)}), bf16[16,8,3456]{2,1,0:T(8,128)(2,1)S(1)}, u32[]{:S(2)}, u32[]{:S(2)}) async-start(bf16[16,8,3456]{2,1,0:T(8,128)(2,1)} %broadcast_in_dim.120), calls=%async_computation.1 | async-start | bytes 1769472 | tf_op jit(solution)/shard_map/all_to_all | solution.py:256
  (150 other events, 2300.6 us)
